TPU v7x, 256 devices: a whole 4x4x8 slice. The times are simulated.
256 devices in a mesh: row: 8 (over y, core), col: 32 (over z, x).
Axes of the slice: x: 4, y: 4, z: 8, core: 2. Of those that a mesh axis runs over, the one named last changes fastest.
Arguments:
- block_values: bfloat16 [8, 32, 24, 256, 256], P('row', 'col'), may hold values from -0.078125 to 0.078125
- block_rows: int32 [8, 32, 24], P('row', 'col'), may hold values from 0 to 7, as said below
- block_cols: int32 [8, 32, 24], P('row', 'col'), may hold values from 0 to 7
- block_count: int32 [8, 32], P('row', 'col'), may hold values from 8 to 24, as said below
- basis: bfloat16 [65536, 256], P(('col', 'row')), may hold values from -6 to 6
Outputs:
- sweep_out: float32 [65536, 256], P(('col', 'row'))
Inputs may be any that keep to these rules, and one draw needn't show every extreme that they name: Within one device all slots give distinct (block_rows, block_cols) pairs; slots at or beyond block_count hold no block. `block_count`: some device holds exactly 24 live slots.
All inputs are finite; a program needn't handle non-finite values.
Results may differ from a plain program's by a relative error of at most 0.0026.
Values may be sent and summed in bfloat16 or wider, within the bound.
No kernel may reach another device: no remote copies, remote signals or barrier semaphores. Data moves between devices by JAX's collectives and lax.ppermute only.
A program may use at most 64 MiB of HBM per device.

v0:
```python
import jax
import jax.numpy as jnp
from jax import lax
from jax.sharding import PartitionSpec as P

RB = 8
CB = 8


def from_everyone(value, axis):
    count = lax.axis_size(axis)
    return lax.all_to_all(
        jnp.broadcast_to(value[None], (count, *value.shape)), axis, 0, 0, tiled=True
    )


def in_order(pieces, dim):
    dims = list(pieces.shape[1:])
    dims[dim] *= pieces.shape[0]
    return jnp.moveaxis(pieces, 0, dim).reshape(dims)


def collect(value, axis, dim):
    pieces = from_everyone(value, axis)
    return in_order(pieces, dim)


def cut_along(value, dim, count):
    before, after = (value.shape[:dim], value.shape[dim + 1 :])
    return jnp.moveaxis(value.reshape(*before, count, -1, *after), dim, 0)


def sum_at_owner(value, axis, dim):
    count = lax.axis_size(axis)
    pieces = lax.all_to_all(cut_along(value, dim, count), axis, 0, 0, tiled=True)
    return jnp.sum(pieces, axis=0)


def body(block_values, block_rows, block_cols, block_count, basis):
    blocks = block_values[0, 0]
    row_ids = block_rows[0, 0]
    col_ids = block_cols[0, 0]
    live_count = block_count[0, 0]
    slot_count = blocks.shape[0]
    tile_width = blocks.shape[1]
    live_mask = (jnp.arange(slot_count, dtype=jnp.int32) < live_count).astype(jnp.float32)
    column_basis = collect(basis, "row", 0)
    masked = jnp.where(live_mask[:, None, None] > 0.5, blocks, jnp.zeros_like(blocks))
    placed = jnp.zeros((RB, tile_width, CB, tile_width), jnp.bfloat16)
    placed = placed.at[row_ids, :, col_ids, :].set(masked)
    matrix = placed.reshape(RB * tile_width, CB * tile_width)
    row_part = jnp.dot(matrix, column_basis, preferred_element_type=jnp.float32)
    row_share = sum_at_owner(row_part, "col", 0)
    row_basis = collect(row_share.astype(jnp.bfloat16), "col", 0)
    column_part = lax.dot_general(
        matrix, row_basis, (((0,), (0,)), ((), ())), preferred_element_type=jnp.float32
    )
    return sum_at_owner(column_part, "row", 0)


def solution(mesh):
    in_specs = (
        P("row", "col", None, None, None),
        P("row", "col", None),
        P("row", "col", None),
        P("row", "col"),
        P(("col", "row"), None),
    )
    out_specs = P(("col", "row"), None)
    return jax.shard_map(body, mesh=mesh, in_specs=in_specs, out_specs=out_specs, check_vma=False)
```

profile of v0, /device:TPU:1, one launch (start us, length us, event | category | flops | bytes accessed | tf_op | source)
XLA Modules:
  0.0 188.0 jit_solution(17180123281201387398)
XLA Ops:
  0.0 0.0 copy-start.1
  0.0 0.0 copy-start
  0.0 2.0 %broadcast_in_dim.32 = bf16[8,256,256]{2,1,0:T(8,128)(2,1)} broadcast(bf16[256,256]{1,0:T(8,128)(2,1)} %param.9), dimensions={1,2} | broadcast | bytes 1179648 | tf_op jit(solution)/shard_map/broadcast_in_dim | solution.py:13
  2.0 7.3 %all-to-all-start = ((bf16[8,256,256]{2,1,0:T(8,128)(2,1)}), bf16[8,256,256]{2,1,0:T(8,128)(2,1)}, u32[]{:S(2)}, u32[]{:S(2)}) async-start(bf16[8,256,256]{2,1,0:T(8,128)(2,1)} %broadcast_in_dim.32), calls=%async_computation | async-start | bytes 2097152 | tf_op jit(solution)/shard_map/all_to_all | solution.py:12
  10.0 0.0 copy-done.1
  10.1 0.0 copy-done
  10.1 2.2 %bitcast_select_fusion = bf16[24,256,256]{2,1,0:T(8,128)(2,1)S(1)} fusion(bf16[1,1,24,256,256]{4,3,2,1,0:T(8,128)(2,1)} %param.5, pred[24]{0:T(512)(128)(4,1)S(1)} %fusion.1), kind=kLoop, calls=%fused_computation.1 | loop fusion | flops 1572864 | bytes 6291480 | tf_op jit(solution)/shard_map/jit(_where)/select_n | solution.py:48
  12.3 4.2 %broadcast_in_dim.16 = bf16[8,256,8,256]{3,1,2,0:T(8,128)(2,1)} broadcast(bf16[]{:T(256)} %constant.5.clone.1), dimensions={} | broadcast | bytes 8388610 | tf_op jit(solution)/shard_map/broadcast_in_dim | solution.py:49
  16.5 7.7 %scatter_fusion = bf16[8,256,8,256]{3,1,2,0:T(8,128)(2,1)} fusion(bf16[8,256,8,256]{3,1,2,0:T(8,128)(2,1)} %broadcast_in_dim.16, s32[24]{0:T(128)S(1)} %fusion.2, bf16[24,256,256]{2,1,0:T(8,128)(2,1)S(1)} %bitcast_select_fusion), kind=kCustom, calls=%fused_computation | custom fusion | bytes 9437376 | tf_op jit(solution)/shard_map/scatter | solution.py:50
  24.2 11.8 %copy.6 = bf16[8,256,8,256]{3,2,1,0:T(8,128)(2,1)} copy(bf16[8,256,8,256]{3,1,2,0:T(8,128)(2,1)} %scatter_fusion) | data formatting | bytes 16777216 | tf_op jit(solution)/shard_map/scatter | solution.py:50
  36.0 13.5 %dot_general.14 = bf16[32,64,2048]{2,1,0:T(8,128)(2,1)} reshape(bf16[8,256,8,256]{3,2,1,0:T(8,128)(2,1)} %copy.6) | data formatting | bytes 16777216 | tf_op jit(solution)/shard_map/dot_general | solution.py:52
  49.5 0.0 all-to-all-done
  49.5 6.1 %fusion.3 = f32[32,64,256]{2,1,0:T(8,128)S(1)} fusion(bf16[32,64,2048]{2,1,0:T(8,128)(2,1)} %dot_general.14, bf16[2048,256,1]{1,0,2:T(8,128)(2,1)} %bitcast.8), kind=kOutput, calls=%fused_computation.11 | convolution fusion | flops 2147483648 | bytes 11534336 | tf_op jit(solution)/shard_map/dot_general | solution.py:52
  55.6 59.2 %all_to_all.20 = f32[32,64,256]{2,1,0:T(8,128)S(1)} all-to-all(f32[32,64,256]{2,1,0:T(8,128)S(1)} %fusion.3), channel_id=1, replica_groups=mesh['row'=8,'col'=32] {'col'}, dimensions={0} | all-to-all | bytes 4194304 | tf_op jit(solution)/shard_map/all_to_all | solution.py:35
  114.7 0.1 reduce_sum.18
  114.8 1.1 broadcast_in_dim.33
  115.9 5.9 %all-to-all-start.2 = ((bf16[32,64,256]{2,1,0:T(8,128)(2,1)}), bf16[32,64,256]{2,1,0:T(8,128)(2,1)S(1)}, u32[]{:S(2)}, u32[]{:S(2)}) async-start(bf16[32,64,256]{2,1,0:T(8,128)(2,1)} %broadcast_in_dim.33), calls=%async_computation.2 | async-start | bytes 2097152 | tf_op jit(solution)/shard_map/all_to_all | solution.py:12
  121.8 10.3 %copy.10 = bf16[256,8,8,256]{3,1,2,0:T(8,128)(2,1)} copy(bf16[256,8,8,256]{3,2,1,0:T(8,128)(2,1)} %bitcast.32) | data formatting | bytes 16777216
  132.1 12.3 %copy.9 = bf16[2048,2048]{1,0:T(8,128)(2,1)} copy(bf16[2048,2048]{0,1:T(8,128)(2,1)} %bitcast.33) | data formatting | bytes 16777216 | tf_op jit(solution)/shard_map/dot_general | solution.py:55
  144.4 2.9 %all-to-all-done.2 = bf16[32,64,256]{2,1,0:T(8,128)(2,1)S(1)} async-done(((bf16[32,64,256]{2,1,0:T(8,128)(2,1)}), bf16[32,64,256]{2,1,0:T(8,128)(2,1)S(1)}, u32[]{:S(2)}, u32[]{:S(2)}) %all-to-all-start.2) | async-done | bytes 1048608 | tf_op jit(solution)/shard_map/all_to_all | solution.py:12
  147.3 5.9 %fusion.4 = f32[8,256,256]{2,1,0:T(8,128)S(1)} fusion(bf16[8,256,2048]{2,1,0:T(8,128)(2,1)} %bitcast.34, bf16[2048,256,1]{1,0,2:T(8,128)(2,1)S(1)} %bitcast.35), kind=kOutput, calls=%fused_computation.12 | convolution fusion | flops 2147483648 | bytes 11534336 | tf_op jit(solution)/shard_map/dot_general | solution.py:55
  153.1 34.0 %all_to_all.21 = f32[8,256,256]{2,1,0:T(8,128)S(1)} all-to-all(f32[8,256,256]{2,1,0:T(8,128)S(1)} %fusion.4), channel_id=1, replica_groups=mesh['row'=8,'col'=32] {'row'}, dimensions={0} | all-to-all | bytes 4194304 | tf_op jit(solution)/shard_map/all_to_all | solution.py:35
  187.1 0.8 reduce_sum.19
  (2 shorter events, 0.0 us)
Async XLA Ops:
  0.0 10.0 %copy-start.1 = (s32[1,1,24]{2,1,0:T(1,128)S(1)}, s32[1,1,24]{2,1,0:T(1,128)}, u32[]{:S(2)}) copy-start(s32[1,1,24]{2,1,0:T(1,128)} %param.6) | copy-start | bytes 292
  0.0 10.1 %copy-start = (s32[1,1,24]{2,1,0:T(1,128)S(1)}, s32[1,1,24]{2,1,0:T(1,128)}, u32[]{:S(2)}) copy-start(s32[1,1,24]{2,1,0:T(1,128)} %param.7) | copy-start | bytes 292
  2.0 47.4 %all-to-all-start = ((bf16[8,256,256]{2,1,0:T(8,128)(2,1)}), bf16[8,256,256]{2,1,0:T(8,128)(2,1)}, u32[]{:S(2)}, u32[]{:S(2)}) async-start(bf16[8,256,256]{2,1,0:T(8,128)(2,1)} %broadcast_in_dim.32), calls=%async_computation | async-start | bytes 2097152 | tf_op jit(solution)/shard_map/all_to_all | solution.py:12
  115.9 31.3 %all-to-all-start.2 = ((bf16[32,64,256]{2,1,0:T(8,128)(2,1)}), bf16[32,64,256]{2,1,0:T(8,128)(2,1)S(1)}, u32[]{:S(2)}, u32[]{:S(2)}) async-start(bf16[32,64,256]{2,1,0:T(8,128)(2,1)} %broadcast_in_dim.33), calls=%async_computation.2 | async-start | bytes 2097152 | tf_op jit(solution)/shard_map/all_to_all | solution.py:12
where the time goes:
time: 189 us; the launch traced here: 188 us
  blocking collectives  93.1 us (49%)
  local copies, waits for them, and re-layouts  62.9 us (33%)
  starting transfers between devices  13.2 us (7%)
  matrix products  11.9 us (6%)
  other arithmetic  3.14 us (2%)
  waiting for transfers between devices  2.87 us (2%)
    all_to_all x2, blocking collectives, sum_at_owner(): lax.all_to_all(cut_along(value, dim, count), axis, 0, 0, tiled=True)  93.1 us
    scatter x2, local copies, waits for them, and re-layouts, body(): placed = placed.at[row_ids, :, col_ids, :].set(masked)  19.5 us
    dot_general x1, local copies, waits for them, and re-layouts, body(): row_part = jnp.dot(matrix, column_basis, preferred_element_type=jnp.float32)  13.5 us
    all_to_all x2, starting transfers between devices, from_everyone(): lax.all_to_all(jnp.broadcast_to(value[None], (count, *value.shape)), axis...  13.2 us
    dot_general x1, local copies, waits for them, and re-layouts, body(): lax.dot_general(matrix, row_basis, (((0,), (0,)), ((), ())), preferred_el...  12.3 us
    unnamed x5, local copies, waits for them, and re-layouts  10.3 us
    dot_general x1, matrix products, body(): row_part = jnp.dot(matrix, column_basis, preferred_element_type=jnp.float32)  6.09 us
    dot_general x1, matrix products, body(): lax.dot_general(matrix, row_basis, (((0,), (0,)), ((), ())), preferred_el...  5.86 us
  transfers between devices with their start and end apart: 2, of which 1 were waited for; matrix products, arithmetic and copies ran while one was open for 33% of the time, Pallas kernels for 0%

commit v1 on v0

v1 whole, which is shorter than its diff:
```python
import functools

import jax
import jax.numpy as jnp
from jax import lax
from jax.experimental import pallas as pl
from jax.experimental.pallas import tpu as pltpu
from jax.sharding import PartitionSpec as P

BF16 = jnp.bfloat16
F32 = jnp.float32
F16 = jnp.float16
CORES = 2
NX = 4
SCALE_X = 64.0
SCALE_Z = 16.0


def shift_y(count, d):
    ny = count // CORES
    return [(y * CORES + k, (y + d) % ny * CORES + k) for y in range(ny) for k in range(CORES)]


def swap_core(count):
    return [(i, i ^ 1) for i in range(count)]


def shift_x(count, d):
    return [(i, i // NX * NX + (i % NX + d) % NX) for i in range(count)]


def z_groups(count):
    return [[z * NX + x for z in range(count // NX)] for x in range(NX)]


def vmem(n):
    return [pl.BlockSpec(memory_space=pltpu.VMEM)] * n


def smem(n):
    return [pl.BlockSpec(memory_space=pltpu.SMEM)] * n


def forward_kernel(rows, cols, count, blocks, *refs):
    pieces, (own, *sends), (basis, acc) = refs[:8], refs[8:12], refs[12:]
    y, k = lax.axis_index("row") // CORES, lax.axis_index("row") % CORES
    x = lax.axis_index("col") % NX
    for d in range(4):
        at = (y + 4 - d) % 4
        basis[at * CORES + k] = pieces[d][...]
        basis[at * CORES + 1 - k] = pieces[4 + d][...]
    acc[...] = jnp.zeros_like(acc)

    def visit(s, carry):
        r, c = rows[0, 0, s], cols[0, 0, s]
        acc[r] += jnp.dot(blocks[0, 0, s], basis[c], preferred_element_type=F32)
        return carry

    lax.fori_loop(0, count[0, 0], visit, 0)
    for h in range(2):
        own[h] = acc[x * 2 + h]
    for d in range(1, 4):
        to = (x + d) % NX
        for h in range(2):
            sends[d - 1][h] = acc[to * 2 + h] * SCALE_X


def backward_kernel(rows, cols, count, blocks, *refs):
    pieces, (own, send), (basis, acc) = refs[:4], refs[4:6], refs[6:]
    k = lax.axis_index("row") % CORES
    x = lax.axis_index("col") % NX
    for d in range(4):
        at = (x + 4 - d) % 4
        for h in range(2):
            basis[at * 2 + h] = pieces[d][h]
    acc[...] = jnp.zeros_like(acc)

    def visit(s, carry):
        r, c = rows[0, 0, s], cols[0, 0, s]
        acc[c] += lax.dot_general(
            blocks[0, 0, s], basis[r], (((0,), (0,)), ((), ())), preferred_element_type=F32
        )
        return carry

    lax.fori_loop(0, count[0, 0], visit, 0)
    for y in range(4):
        own[y] = acc[y * CORES + k]
        send[y] = acc[y * CORES + 1 - k].astype(send.dtype)


def call(kernel, outs, scratch, n_vmem, *args):
    return pl.pallas_call(
        kernel,
        out_shape=outs,
        in_specs=smem(3) + vmem(n_vmem),
        out_specs=vmem(len(outs)),
        scratch_shapes=scratch,
        compiler_params=pltpu.CompilerParams(vmem_limit_bytes=24 << 20),
    )(*args)


def body(block_values, block_rows, block_cols, block_count, basis):
    n_row, n_col = lax.axis_size("row"), lax.axis_size("col")
    size, rank = basis.shape
    table = (block_rows, block_cols, block_count)

    mine = [basis] + [lax.ppermute(basis, "row", shift_y(n_row, d)) for d in (1, 2, 3)]
    other = [lax.ppermute(p, "row", swap_core(n_row)) for p in mine]
    own, *sends = call(
        forward_kernel,
        [jax.ShapeDtypeStruct((2, size, rank), F32)] * 4,
        [pltpu.VMEM((8, size, rank), BF16), pltpu.VMEM((8, size, rank), F32)],
        9,
        *table, block_values, *mine, *other,
    )
    got = [lax.ppermute(s.astype(F16), "col", shift_x(n_col, d)) for d, s in zip((1, 2, 3), sends)]
    x_sum = own + (got[0].astype(F32) + got[1].astype(F32) + got[2].astype(F32)) * (1 / SCALE_X)
    nz = n_col // NX
    parts = (x_sum * SCALE_Z).astype(F16).reshape(nz, 2 * size // nz, rank)
    parts = lax.all_to_all(parts, "col", 0, 0, tiled=True, axis_index_groups=z_groups(n_col))
    share = (jnp.sum(parts.astype(F32), axis=0) * (1 / SCALE_Z)).astype(BF16)

    copies = jnp.broadcast_to(share[None], (nz, *share.shape))
    chunk = lax.all_to_all(copies, "col", 0, 0, tiled=True, axis_index_groups=z_groups(n_col))
    chunk = chunk.reshape(2, size, rank)
    chunks = [chunk] + [lax.ppermute(chunk, "col", shift_x(n_col, d)) for d in (1, 2, 3)]
    own, send = call(
        backward_kernel,
        [jax.ShapeDtypeStruct((4, size, rank), F32), jax.ShapeDtypeStruct((4, size, rank), BF16)],
        [pltpu.VMEM((8, size, rank), BF16), pltpu.VMEM((8, size, rank), F32)],
        5,
        *table, block_values, *chunks,
    )
    pair = own + lax.ppermute(send, "row", swap_core(n_row)).astype(F32)
    y = lax.axis_index("row") // CORES
    pick = lambda d: lax.dynamic_index_in_dim(pair, (y + d) % 4, 0, keepdims=False)
    got = [lax.ppermute(pick(d).astype(BF16), "row", shift_y(n_row, d)) for d in (1, 2, 3)]
    return pick(0) + got[0].astype(F32) + got[1].astype(F32) + got[2].astype(F32)


def solution(mesh):
    in_specs = (
        P("row", "col", None, None, None),
        P("row", "col", None),
        P("row", "col", None),
        P("row", "col"),
        P(("col", "row"), None),
    )
    out_specs = P(("col", "row"), None)
    return jax.shard_map(body, mesh=mesh, in_specs=in_specs, out_specs=out_specs, check_vma=False)
```

time: 189 us -> 104 us (0.55)
  the two profiles are of different devices: /device:TPU:1 before, /device:TPU:2 now
where the time goes in v1:
time: 104 us; the launch traced here: 103 us
  waiting for transfers between devices  37.8 us (36%)
  blocking collectives  33.9 us (33%)
  starting transfers between devices  19.6 us (19%)
  Pallas kernels  5.6 us (5%)
  local copies, waits for them, and re-layouts  4.17 us (4%)
  other arithmetic  1.2 us (1%)
    all_to_all x1, blocking collectives, body(): lax.all_to_all(parts, 'col', 0, 0, tiled=True, axis_index_groups=z_groups...  19.3 us
    all_to_all x1, blocking collectives, body(): lax.all_to_all(copies, 'col', 0, 0, tiled=True, axis_index_groups=z_group...  14.6 us
    ppermute x3, waiting for transfers between devices, body(): lax.ppermute(s.astype(F16), 'col', shift_x(n_col, d))  13 us
    ppermute x3, waiting for transfers between devices, body(): lax.ppermute(chunk, 'col', shift_x(n_col, d))  10.9 us
    ppermute x3, waiting for transfers between devices, body(): lax.ppermute(pick(d).astype(BF16), 'row', shift_y(n_row, d))  7.16 us
    ppermute x3, starting transfers between devices, body(): lax.ppermute(basis, 'row', shift_y(n_row, d))  5.83 us
    pallas_call x2, Pallas kernels, call(): pl.pallas_call(kernel, out_shape=outs, in_specs=smem(3) + vmem(n_vmem), o...  5.6 us
    ppermute x3, starting transfers between devices, body(): lax.ppermute(s.astype(F16), 'col', shift_x(n_col, d))  5 us
  transfers between devices with their start and end apart: 17, of which 12 were waited for; matrix products, arithmetic and copies ran while one was open for 0% of the time, Pallas kernels for 0%

profile of v1, /device:TPU:2, one launch (start us, length us, event | category | flops | bytes accessed | tf_op | source)
XLA Modules:
  0.0 103.1 jit_solution(18240062014689131308)
XLA Ops:
  0.0 1.6 %collective-permute-start = (bf16[256,256]{1,0:T(8,128)(2,1)}, bf16[256,256]{1,0:T(8,128)(2,1)S(1)}, u32[]{:S(2)}, u32[]{:S(2)}) collective-permute-start(bf16[256,256]{1,0:T(8,128)(2,1)} %refs_0_.1), channel_id=1, source_target_pairs={{0,64},{32,96},{64,128},{96,160},{128,192},{160,224},{192,0},{224,... | collective-permute-start | bytes 393224 | tf_op jit(solution)/shard_map/ppermute | solution.py:107
  1.6 2.9 %collective-permute-start.1 = (bf16[256,256]{1,0:T(8,128)(2,1)}, bf16[256,256]{1,0:T(8,128)(2,1)S(1)}, u32[]{:S(2)}, u32[]{:S(2)}) collective-permute-start(bf16[256,256]{1,0:T(8,128)(2,1)} %refs_0_.1), channel_id=1, source_target_pairs={{0,128},{32,160},{64,192},{96,224},{128,0},{160,32},{192,64},{224,... | collective-permute-start | bytes 393224 | tf_op jit(solution)/shard_map/ppermute | solution.py:107
  4.5 1.3 %collective-permute-start.2 = (bf16[256,256]{1,0:T(8,128)(2,1)}, bf16[256,256]{1,0:T(8,128)(2,1)S(1)}, u32[]{:S(2)}, u32[]{:S(2)}) collective-permute-start(bf16[256,256]{1,0:T(8,128)(2,1)} %refs_0_.1), channel_id=1, source_target_pairs={{0,192},{32,224},{64,0},{96,32},{128,64},{160,96},{192,128},{224,1... | collective-permute-start | bytes 393224 | tf_op jit(solution)/shard_map/ppermute | solution.py:107
  5.8 0.0 collective-permute-start.3
  5.8 0.9 collective-permute-done.refs_1_
  6.7 0.0 collective-permute-start.4
  6.7 4.0 %collective-permute-done.1.refs_2_ = bf16[256,256]{1,0:T(8,128)(2,1)S(1)} collective-permute-done((bf16[256,256]{1,0:T(8,128)(2,1)}, bf16[256,256]{1,0:T(8,128)(2,1)S(1)}, u32[]{:S(2)}, u32[]{:S(2)}) %collective-permute-start.1) | collective-permute-done | bytes 131104 | tf_op jit(solution)/shard_map/ppermute | solution.py:107
  10.7 0.0 collective-permute-start.5
  10.7 0.0 collective-permute-done.2.refs_3_
  10.7 0.5 collective-permute-start.6
  11.9 0.0 collective-permute-done.3.refs_4_
  11.9 0.0 collective-permute-done.4.refs_5_
  11.9 0.2 collective-permute-done.5.refs_6_
  12.1 0.2 collective-permute-done.6.refs_7_
  12.2 0.0 copy-start
  12.2 1.9 %copy-done = bf16[1,1,24,256,256]{4,3,2,1,0:T(8,128)(2,1)S(1)} copy-done((bf16[1,1,24,256,256]{4,3,2,1,0:T(8,128)(2,1)S(1)}, bf16[1,1,24,256,256]{4,3,2,1,0:T(8,128)(2,1)}, u32[]{:S(2)}) %copy-start) | copy-done | bytes 3145752
  14.1 0.0 copy-start.1
  14.1 0.9 copy-done.1
  15.0 0.0 copy-start.2
  15.0 0.7 copy-done.2
  15.7 0.0 copy-start.3
  15.7 0.7 copy-done.3
  16.4 2.6 %shard_map.55 = (f32[2,256,256]{2,1,0:T(8,128)S(1)}, f32[2,256,256]{2,1,0:T(8,128)S(1)}, f32[2,256,256]{2,1,0:T(8,128)S(1)}, f32[2,256,256]{2,1,0:T(8,128)S(1)}) custom-call(s32[1,1,24]{2,1,0:T(1,128)S(1)} %copy-done.2, s32[1,1,24]{2,1,0:T(1,128)S(1)} %copy-done.3, s32[1,1]{1,0:T(1,128)S(6)} %copy.6.count, bf16[1,1,24,256,256]{4,3,2,1,0:T(8,128)(2,1)S(1)} %copy-done, ...), custom_call_target="tpu_custom_call" | custom-call | tf_op jit(solution)/shard_map/pallas_call | solution.py:92
  19.0 2.2 %collective-permute-start.7 = (f16[2,256,256]{2,1,0:T(8,128)(2,1)S(1)}, f16[2,256,256]{2,1,0:T(8,128)(2,1)S(1)}, u32[]{:S(2)}, u32[]{:S(2)}) collective-permute-start(f16[2,256,256]{2,1,0:T(8,128)(2,1)S(1)} %convert_element_type.61), channel_id=1, source_target_pairs={{0,1},{1,2},{2,3},{3,0},{4,5},{5,6},{6,7},{7,4},{8,9},{9,10},{10,1... | collective-permute-start | bytes 786440 | tf_op jit(solution)/shard_map/ppermute | solution.py:116
  21.2 1.2 %collective-permute-start.8 = (f16[2,256,256]{2,1,0:T(8,128)(2,1)S(1)}, f16[2,256,256]{2,1,0:T(8,128)(2,1)S(1)}, u32[]{:S(2)}, u32[]{:S(2)}) collective-permute-start(f16[2,256,256]{2,1,0:T(8,128)(2,1)S(1)} %convert_element_type.63), channel_id=1, source_target_pairs={{0,2},{1,3},{2,0},{3,1},{4,6},{5,7},{6,4},{7,5},{8,10},{9,11},{10,... | collective-permute-start | bytes 786440 | tf_op jit(solution)/shard_map/ppermute | solution.py:116
  22.4 1.7 %collective-permute-start.9 = (f16[2,256,256]{2,1,0:T(8,128)(2,1)S(1)}, f16[2,256,256]{2,1,0:T(8,128)(2,1)S(1)}, u32[]{:S(2)}, u32[]{:S(2)}) collective-permute-start(f16[2,256,256]{2,1,0:T(8,128)(2,1)S(1)} %convert_element_type.65), channel_id=1, source_target_pairs={{0,3},{1,0},{2,1},{3,2},{4,7},{5,4},{6,5},{7,6},{8,11},{9,8},{10,9... | collective-permute-start | bytes 786440 | tf_op jit(solution)/shard_map/ppermute | solution.py:116
  24.1 9.1 %collective-permute-done.7 = f16[2,256,256]{2,1,0:T(8,128)(2,1)S(1)} collective-permute-done((f16[2,256,256]{2,1,0:T(8,128)(2,1)S(1)}, f16[2,256,256]{2,1,0:T(8,128)(2,1)S(1)}, u32[]{:S(2)}, u32[]{:S(2)}) %collective-permute-start.7) | collective-permute-done | bytes 262176 | tf_op jit(solution)/shard_map/ppermute | solution.py:116
  33.2 0.0 collective-permute-done.8
  33.2 3.9 %collective-permute-done.9 = f16[2,256,256]{2,1,0:T(8,128)(2,1)S(1)} collective-permute-done((f16[2,256,256]{2,1,0:T(8,128)(2,1)S(1)}, f16[2,256,256]{2,1,0:T(8,128)(2,1)S(1)}, u32[]{:S(2)}, u32[]{:S(2)}) %collective-permute-start.9) | collective-permute-done | bytes 262176 | tf_op jit(solution)/shard_map/ppermute | solution.py:116
  37.1 0.2 multiply_convert_fusion
  37.3 19.3 %all_to_all.10 = f16[8,64,256]{2,1,0:T(8,128)(2,1)S(1)} all-to-all(f16[8,64,256]{2,1,0:T(8,128)(2,1)S(1)} %bitcast.18), channel_id=1, replica_groups={{0,4,8,12,16,20,24,28},{1,5,9,13,17,21,25,29},{2,6,10,14,18,22,26,30},{..., dimensions={0} | all-to-all | bytes 524288 | tf_op jit(solution)/shard_map/all_to_all | solution.py:120
  56.7 14.6 %all_to_all.11 = bf16[8,64,256]{2,1,0:T(8,128)(2,1)S(1)} all-to-all(bf16[8,64,256]{2,1,0:T(8,128)(2,1)S(1)} %broadcast_in_dim.2), channel_id=1, replica_groups={{0,4,8,12,16,20,24,28},{1,5,9,13,17,21,25,29},{2,6,10,14,18,22,26,30},{..., dimensions={0} | all-to-all | bytes 524288 | tf_op jit(solution)/shard_map/all_to_all | solution.py:124
  71.3 0.1 collective-permute-start.10
  71.3 0.5 collective-permute-start.11
  71.8 2.4 %collective-permute-start.12 = (bf16[2,256,256]{2,1,0:T(8,128)(2,1)S(1)}, bf16[2,256,256]{2,1,0:T(8,128)(2,1)S(1)}, u32[]{:S(2)}, u32[]{:S(2)}) collective-permute-start(bf16[2,256,256]{2,1,0:T(8,128)(2,1)S(1)} %bitcast.16), channel_id=1, source_target_pairs={{0,3},{1,0},{2,1},{3,2},{4,7},{5,4},{6,5},{7,6},{8,11},{9,8},{10,9... | collective-permute-start | bytes 786440 | tf_op jit(solution)/shard_map/ppermute | solution.py:126
  74.2 6.3 %collective-permute-done.10.refs_1_ = bf16[2,256,256]{2,1,0:T(8,128)(2,1)S(1)} collective-permute-done((bf16[2,256,256]{2,1,0:T(8,128)(2,1)S(1)}, bf16[2,256,256]{2,1,0:T(8,128)(2,1)S(1)}, u32[]{:S(2)}, u32[]{:S(2)}) %collective-permute-start.10) | collective-permute-done | bytes 262176 | tf_op jit(solution)/shard_map/ppermute | solution.py:126
  80.5 1.6 %collective-permute-done.11.refs_2_ = bf16[2,256,256]{2,1,0:T(8,128)(2,1)S(1)} collective-permute-done((bf16[2,256,256]{2,1,0:T(8,128)(2,1)S(1)}, bf16[2,256,256]{2,1,0:T(8,128)(2,1)S(1)}, u32[]{:S(2)}, u32[]{:S(2)}) %collective-permute-start.11) | collective-permute-done | bytes 262176 | tf_op jit(solution)/shard_map/ppermute | solution.py:126
  82.1 3.0 %collective-permute-done.12.refs_3_ = bf16[2,256,256]{2,1,0:T(8,128)(2,1)S(1)} collective-permute-done((bf16[2,256,256]{2,1,0:T(8,128)(2,1)S(1)}, bf16[2,256,256]{2,1,0:T(8,128)(2,1)S(1)}, u32[]{:S(2)}, u32[]{:S(2)}) %collective-permute-start.12) | collective-permute-done | bytes 262176 | tf_op jit(solution)/shard_map/ppermute | solution.py:126
  85.1 3.0 %shard_map.56 = (f32[4,256,256]{2,1,0:T(8,128)S(1)}, bf16[4,256,256]{2,1,0:T(8,128)(2,1)S(1)}) custom-call(s32[1,1,24]{2,1,0:T(1,128)S(1)} %copy-done.2, s32[1,1,24]{2,1,0:T(1,128)S(1)} %copy-done.3, s32[1,1]{1,0:T(1,128)S(6)} %copy.6.count, bf16[1,1,24,256,256]{4,3,2,1,0:T(8,128)(2,1)S(1)} %copy-done, bf16[2,256,256]{2,1,0:T(8,128)(2,1)S(1)} %bitcast.17, ...), custom_call_target="tpu_custom_call" | custom-call | tf_op jit(solution)/shard_map/pallas_call | solution.py:92
  88.1 2.0 %collective-permute-start.13 = (bf16[4,256,256]{2,1,0:T(8,128)(2,1)S(1)}, bf16[4,256,256]{2,1,0:T(8,128)(2,1)S(1)}, u32[]{:S(2)}, u32[]{:S(2)}) collective-permute-start(bf16[4,256,256]{2,1,0:T(8,128)(2,1)S(1)} %get-tuple-element.16), channel_id=1, source_target_pairs={{0,32},{32,0},{64,96},{96,64},{128,160},{160,128},{192,224},{224,1... | collective-permute-start | bytes 1572872 | tf_op jit(solution)/shard_map/ppermute | solution.py:134
  90.1 1.5 %collective-permute-done.13 = bf16[4,256,256]{2,1,0:T(8,128)(2,1)S(1)} collective-permute-done((bf16[4,256,256]{2,1,0:T(8,128)(2,1)S(1)}, bf16[4,256,256]{2,1,0:T(8,128)(2,1)S(1)}, u32[]{:S(2)}, u32[]{:S(2)}) %collective-permute-start.13) | collective-permute-done | bytes 524320 | tf_op jit(solution)/shard_map/ppermute | solution.py:134
  91.7 0.1 convert_add_fusion
  91.8 0.1 fusion.2
  91.8 0.1 collective-permute-start.14
  91.9 0.1 collective-permute-start.15
  92.0 3.1 %collective-permute-start.16 = (bf16[256,256]{1,0:T(8,128)(2,1)S(1)}, bf16[256,256]{1,0:T(8,128)(2,1)S(1)}, u32[]{:S(2)}, u32[]{:S(2)}) collective-permute-start(bf16[256,256]{1,0:T(8,128)(2,1)S(1)} %get-tuple-element.18), channel_id=1, source_target_pairs={{0,192},{32,224},{64,0},{96,32},{128,64},{160,96},{192,128},{224,1... | collective-permute-start | bytes 393224 | tf_op jit(solution)/shard_map/ppermute | solution.py:137
  95.2 6.5 %collective-permute-done.14 = bf16[256,256]{1,0:T(8,128)(2,1)S(1)} collective-permute-done((bf16[256,256]{1,0:T(8,128)(2,1)S(1)}, bf16[256,256]{1,0:T(8,128)(2,1)S(1)}, u32[]{:S(2)}, u32[]{:S(2)}) %collective-permute-start.14) | collective-permute-done | bytes 131104 | tf_op jit(solution)/shard_map/ppermute | solution.py:137
  101.7 0.0 collective-permute-done.15
  101.7 0.6 collective-permute-done.16
  102.3 0.8 fusion.1
  (6 shorter events, 0.2 us)
Async XLA Ops:
  0.0 6.7 %collective-permute-start = (bf16[256,256]{1,0:T(8,128)(2,1)}, bf16[256,256]{1,0:T(8,128)(2,1)S(1)}, u32[]{:S(2)}, u32[]{:S(2)}) collective-permute-start(bf16[256,256]{1,0:T(8,128)(2,1)} %refs_0_.1), channel_id=1, source_target_pairs={{0,64},{32,96},{64,128},{96,160},{128,192},{160,224},{192,0},{224,... | collective-permute-start | bytes 393224 | tf_op jit(solution)/shard_map/ppermute | solution.py:107
  1.6 9.1 %collective-permute-start.1 = (bf16[256,256]{1,0:T(8,128)(2,1)}, bf16[256,256]{1,0:T(8,128)(2,1)S(1)}, u32[]{:S(2)}, u32[]{:S(2)}) collective-permute-start(bf16[256,256]{1,0:T(8,128)(2,1)} %refs_0_.1), channel_id=1, source_target_pairs={{0,128},{32,160},{64,192},{96,224},{128,0},{160,32},{192,64},{224,... | collective-permute-start | bytes 393224 | tf_op jit(solution)/shard_map/ppermute | solution.py:107
  4.5 6.2 %collective-permute-start.2 = (bf16[256,256]{1,0:T(8,128)(2,1)}, bf16[256,256]{1,0:T(8,128)(2,1)S(1)}, u32[]{:S(2)}, u32[]{:S(2)}) collective-permute-start(bf16[256,256]{1,0:T(8,128)(2,1)} %refs_0_.1), channel_id=1, source_target_pairs={{0,192},{32,224},{64,0},{96,32},{128,64},{160,96},{192,128},{224,1... | collective-permute-start | bytes 393224 | tf_op jit(solution)/shard_map/ppermute | solution.py:107
  5.8 6.0 %collective-permute-start.3 = (bf16[256,256]{1,0:T(8,128)(2,1)}, bf16[256,256]{1,0:T(8,128)(2,1)S(1)}, u32[]{:S(2)}, u32[]{:S(2)}) collective-permute-start(bf16[256,256]{1,0:T(8,128)(2,1)} %refs_0_.1), channel_id=1, source_target_pairs={{0,32},{32,0},{64,96},{96,64},{128,160},{160,128},{192,224},{224,1... | collective-permute-start | bytes 393224 | tf_op jit(solution)/shard_map/ppermute | solution.py:108
  6.7 5.2 %collective-permute-start.4 = (bf16[256,256]{1,0:T(8,128)(2,1)S(1)}, bf16[256,256]{1,0:T(8,128)(2,1)S(1)}, u32[]{:S(2)}, u32[]{:S(2)}) collective-permute-start(bf16[256,256]{1,0:T(8,128)(2,1)S(1)} %collective-permute-done.refs_1_), channel_id=1, source_target_pairs={{0,32},{32,0},{64,96},{96,64},{128,160},{160,128},{192,224},{224,1... | collective-permute-start | bytes 393224 | tf_op jit(solution)/shard_map/ppermute | solution.py:108
  10.7 1.3 %collective-permute-start.5 = (bf16[256,256]{1,0:T(8,128)(2,1)S(1)}, bf16[256,256]{1,0:T(8,128)(2,1)S(1)}, u32[]{:S(2)}, u32[]{:S(2)}) collective-permute-start(bf16[256,256]{1,0:T(8,128)(2,1)S(1)} %collective-permute-done.1.refs_2_), channel_id=1, source_target_pairs={{0,32},{32,0},{64,96},{96,64},{128,160},{160,128},{192,224},{224,1... | collective-permute-start | bytes 393224 | tf_op jit(solution)/shard_map/ppermute | solution.py:108
  10.7 1.5 %collective-permute-start.6 = (bf16[256,256]{1,0:T(8,128)(2,1)S(1)}, bf16[256,256]{1,0:T(8,128)(2,1)S(1)}, u32[]{:S(2)}, u32[]{:S(2)}) collective-permute-start(bf16[256,256]{1,0:T(8,128)(2,1)S(1)} %collective-permute-done.2.refs_3_), channel_id=1, source_target_pairs={{0,32},{32,0},{64,96},{96,64},{128,160},{160,128},{192,224},{224,1... | collective-permute-start | bytes 393224 | tf_op jit(solution)/shard_map/ppermute | solution.py:108
  12.2 1.9 %copy-start = (bf16[1,1,24,256,256]{4,3,2,1,0:T(8,128)(2,1)S(1)}, bf16[1,1,24,256,256]{4,3,2,1,0:T(8,128)(2,1)}, u32[]{:S(2)}) copy-start(bf16[1,1,24,256,256]{4,3,2,1,0:T(8,128)(2,1)} %blocks.3) | copy-start | bytes 9437188
  14.1 0.9 copy-start.1
  15.0 0.7 copy-start.2
  15.7 0.7 copy-start.3
  19.0 14.2 %collective-permute-start.7 = (f16[2,256,256]{2,1,0:T(8,128)(2,1)S(1)}, f16[2,256,256]{2,1,0:T(8,128)(2,1)S(1)}, u32[]{:S(2)}, u32[]{:S(2)}) collective-permute-start(f16[2,256,256]{2,1,0:T(8,128)(2,1)S(1)} %convert_element_type.61), channel_id=1, source_target_pairs={{0,1},{1,2},{2,3},{3,0},{4,5},{5,6},{6,7},{7,4},{8,9},{9,10},{10,1... | collective-permute-start | bytes 786440 | tf_op jit(solution)/shard_map/ppermute | solution.py:116
  21.2 12.0 %collective-permute-start.8 = (f16[2,256,256]{2,1,0:T(8,128)(2,1)S(1)}, f16[2,256,256]{2,1,0:T(8,128)(2,1)S(1)}, u32[]{:S(2)}, u32[]{:S(2)}) collective-permute-start(f16[2,256,256]{2,1,0:T(8,128)(2,1)S(1)} %convert_element_type.63), channel_id=1, source_target_pairs={{0,2},{1,3},{2,0},{3,1},{4,6},{5,7},{6,4},{7,5},{8,10},{9,11},{10,... | collective-permute-start | bytes 786440 | tf_op jit(solution)/shard_map/ppermute | solution.py:116
  22.4 14.7 %collective-permute-start.9 = (f16[2,256,256]{2,1,0:T(8,128)(2,1)S(1)}, f16[2,256,256]{2,1,0:T(8,128)(2,1)S(1)}, u32[]{:S(2)}, u32[]{:S(2)}) collective-permute-start(f16[2,256,256]{2,1,0:T(8,128)(2,1)S(1)} %convert_element_type.65), channel_id=1, source_target_pairs={{0,3},{1,0},{2,1},{3,2},{4,7},{5,4},{6,5},{7,6},{8,11},{9,8},{10,9... | collective-permute-start | bytes 786440 | tf_op jit(solution)/shard_map/ppermute | solution.py:116
  71.3 9.2 %collective-permute-start.10 = (bf16[2,256,256]{2,1,0:T(8,128)(2,1)S(1)}, bf16[2,256,256]{2,1,0:T(8,128)(2,1)S(1)}, u32[]{:S(2)}, u32[]{:S(2)}) collective-permute-start(bf16[2,256,256]{2,1,0:T(8,128)(2,1)S(1)} %bitcast.14), channel_id=1, source_target_pairs={{0,1},{1,2},{2,3},{3,0},{4,5},{5,6},{6,7},{7,4},{8,9},{9,10},{10,1... | collective-permute-start | bytes 786440 | tf_op jit(solution)/shard_map/ppermute | solution.py:126
  71.3 10.8 %collective-permute-start.11 = (bf16[2,256,256]{2,1,0:T(8,128)(2,1)S(1)}, bf16[2,256,256]{2,1,0:T(8,128)(2,1)S(1)}, u32[]{:S(2)}, u32[]{:S(2)}) collective-permute-start(bf16[2,256,256]{2,1,0:T(8,128)(2,1)S(1)} %bitcast.15), channel_id=1, source_target_pairs={{0,2},{1,3},{2,0},{3,1},{4,6},{5,7},{6,4},{7,5},{8,10},{9,11},{10,... | collective-permute-start | bytes 786440 | tf_op jit(solution)/shard_map/ppermute | solution.py:126
  71.8 13.3 %collective-permute-start.12 = (bf16[2,256,256]{2,1,0:T(8,128)(2,1)S(1)}, bf16[2,256,256]{2,1,0:T(8,128)(2,1)S(1)}, u32[]{:S(2)}, u32[]{:S(2)}) collective-permute-start(bf16[2,256,256]{2,1,0:T(8,128)(2,1)S(1)} %bitcast.16), channel_id=1, source_target_pairs={{0,3},{1,0},{2,1},{3,2},{4,7},{5,4},{6,5},{7,6},{8,11},{9,8},{10,9... | collective-permute-start | bytes 786440 | tf_op jit(solution)/shard_map/ppermute | solution.py:126
  88.1 3.6 %collective-permute-start.13 = (bf16[4,256,256]{2,1,0:T(8,128)(2,1)S(1)}, bf16[4,256,256]{2,1,0:T(8,128)(2,1)S(1)}, u32[]{:S(2)}, u32[]{:S(2)}) collective-permute-start(bf16[4,256,256]{2,1,0:T(8,128)(2,1)S(1)} %get-tuple-element.16), channel_id=1, source_target_pairs={{0,32},{32,0},{64,96},{96,64},{128,160},{160,128},{192,224},{224,1... | collective-permute-start | bytes 1572872 | tf_op jit(solution)/shard_map/ppermute | solution.py:134
  91.8 9.9 %collective-permute-start.14 = (bf16[256,256]{1,0:T(8,128)(2,1)S(1)}, bf16[256,256]{1,0:T(8,128)(2,1)S(1)}, u32[]{:S(2)}, u32[]{:S(2)}) collective-permute-start(bf16[256,256]{1,0:T(8,128)(2,1)S(1)} %get-tuple-element.17), channel_id=1, source_target_pairs={{0,64},{32,96},{64,128},{96,160},{128,192},{160,224},{192,0},{224,... | collective-permute-start | bytes 393224 | tf_op jit(solution)/shard_map/ppermute | solution.py:137
  91.9 9.8 %collective-permute-start.15 = (bf16[256,256]{1,0:T(8,128)(2,1)S(1)}, bf16[256,256]{1,0:T(8,128)(2,1)S(1)}, u32[]{:S(2)}, u32[]{:S(2)}) collective-permute-start(bf16[256,256]{1,0:T(8,128)(2,1)S(1)} %get-tuple-element.19), channel_id=1, source_target_pairs={{0,128},{32,160},{64,192},{96,224},{128,0},{160,32},{192,64},{224,... | collective-permute-start | bytes 393224 | tf_op jit(solution)/shard_map/ppermute | solution.py:137
  92.0 10.3 %collective-permute-start.16 = (bf16[256,256]{1,0:T(8,128)(2,1)S(1)}, bf16[256,256]{1,0:T(8,128)(2,1)S(1)}, u32[]{:S(2)}, u32[]{:S(2)}) collective-permute-start(bf16[256,256]{1,0:T(8,128)(2,1)S(1)} %get-tuple-element.18), channel_id=1, source_target_pairs={{0,192},{32,224},{64,0},{96,32},{128,64},{160,96},{192,128},{224,1... | collective-permute-start | bytes 393224 | tf_op jit(solution)/shard_map/ppermute | solution.py:137

commit v2 on v0

v2 whole, which is shorter than its diff:
```python
import jax
import jax.numpy as jnp
from jax import lax
from jax.experimental import pallas as pl
from jax.experimental.pallas import tpu as pltpu
from jax.sharding import PartitionSpec as P

BF16 = jnp.bfloat16
F32 = jnp.float32
F16 = jnp.float16
CORES = 2
RING = 4
SCALE_X = 32.0
SCALE_Z = 16.0


def swap_core(v):
    return lax.ppermute(v, "row", [(i, i ^ 1) for i in range(lax.axis_size("row"))])


def swap_y(v, way):
    n = lax.axis_size("row")
    return lax.ppermute(v, "row", [(i, ring_partner(i // CORES, way) * CORES + i % CORES) for i in range(n)])


def swap_x(v, way):
    n = lax.axis_size("col")
    return lax.ppermute(v, "col", [(i, i // RING * RING + ring_partner(i % RING, way)) for i in range(n)])


def ring_partner(u, way):
    return u ^ 1 if way == "a" else 3 - u


def z_groups():
    n = lax.axis_size("col")
    return [[z * RING + x for z in range(n // RING)] for x in range(RING)]


def partners(u):
    return u + 1 - 2 * (u % 2), 3 - u, (u + 2) % RING


def fetch_kernel(blocks, basis, blocks_out, basis_out, sems):
    copies = [
        pltpu.make_async_copy(blocks, blocks_out, sems.at[0]),
        pltpu.make_async_copy(basis, basis_out, sems.at[1]),
    ]
    for copy in copies:
        copy.start()
    for copy in copies:
        copy.wait()


def fetch(blocks, basis):
    return pl.pallas_call(
        fetch_kernel,
        out_shape=[jax.ShapeDtypeStruct(blocks.shape, blocks.dtype), jax.ShapeDtypeStruct(basis.shape, basis.dtype)],
        in_specs=[pl.BlockSpec(memory_space=pltpu.HBM)] * 2,
        out_specs=[pl.BlockSpec(memory_space=pltpu.VMEM)] * 2,
        scratch_shapes=[pltpu.SemaphoreType.DMA((2,))],
        compiler_params=pltpu.CompilerParams(vmem_limit_bytes=16 << 20),
        cost_estimate=pl.CostEstimate(flops=0, bytes_accessed=8 << 20, transcendentals=0),
    )(blocks, basis)


def forward_kernel(table, count, blocks, *refs):
    pieces, (keep0, keep1, send_a, send_b), (basis, acc) = refs[:10], refs[10:14], refs[14:]
    half = basis.shape[1] // 2
    y, k = lax.axis_index("row") // CORES, lax.axis_index("row") % CORES
    x = lax.axis_index("col") % RING
    ya, yb, yo = partners(y)
    for core, group in ((k, pieces[:5]), (1 - k, pieces[5:])):
        for at, piece in zip((y, ya, yb), group[:3]):
            basis[at * CORES + core] = piece[...]
        basis[yo * CORES + core, :half] = group[3][...]
        basis[yo * CORES + core, half:] = group[4][...]
    acc[...] = jnp.zeros_like(acc)

    def visit(s, carry):
        r, c = table[s] // 8, table[s] % 8
        acc[r] += jnp.dot(blocks[0, 0, s], basis[c], preferred_element_type=F32)
        return carry

    lax.fori_loop(0, count[0, 0], visit, 0)
    xa, xb, xo = partners(x)
    keep0[0], keep0[1] = acc[2 * x], acc[2 * xb]
    keep1[0], keep1[1] = acc[2 * x + 1], acc[2 * xa + 1]
    send_a[0], send_a[1] = acc[2 * xa] * SCALE_X, acc[2 * xo] * SCALE_X
    send_b[0], send_b[1] = acc[2 * xb + 1] * SCALE_X, acc[2 * xo + 1] * SCALE_X


def backward_kernel(table, count, blocks, own, from_a, from_b, far0, far1, keep, send, basis, acc):
    y, k = lax.axis_index("row") // CORES, lax.axis_index("row") % CORES
    x = lax.axis_index("col") % RING
    xa, xb, xo = partners(x)
    for at, piece in zip((x, xa, xb), (own, from_a, from_b)):
        basis[2 * at], basis[2 * at + 1] = piece[0], piece[1]
    basis[2 * xo], basis[2 * xo + 1] = far0[0], far1[0]
    acc[...] = jnp.zeros_like(acc)

    def visit(s, carry):
        r, c = table[s] // 8, table[s] % 8
        acc[c] += lax.dot_general(
            blocks[0, 0, s], basis[r], (((0,), (0,)), ((), ())), preferred_element_type=F32
        )
        return carry

    lax.fori_loop(0, count[0, 0], visit, 0)
    for j in range(RING):
        keep[j] = acc[j * CORES + k]
        send[j] = acc[j * CORES + 1 - k].astype(send.dtype)


def pair_kernel(own, other, keep0, keep1, send_a, send_b):
    y = lax.axis_index("row") // CORES
    ya, yb, yo = partners(y)
    half = own.shape[1] // 2
    first, second = slice(0, half), slice(half, None)

    def both(at, rows):
        return own[at, rows] + other[at, rows].astype(F32)

    keep0[0], keep0[1] = both(y, first), both(yb, first)
    keep1[0], keep1[1] = both(y, second), both(ya, second)
    send_a[0], send_a[1] = both(ya, first).astype(BF16), both(yo, first).astype(BF16)
    send_b[0], send_b[1] = both(yb, second).astype(BF16), both(yo, second).astype(BF16)


def call(kernel, outs, scratch, n_smem, flops, *args):
    spec = pl.BlockSpec(memory_space=pltpu.VMEM)
    return pl.pallas_call(
        kernel,
        out_shape=[jax.ShapeDtypeStruct(shape, dtype) for shape, dtype in outs],
        in_specs=[pl.BlockSpec(memory_space=pltpu.SMEM)] * n_smem + [spec] * (len(args) - n_smem),
        out_specs=[spec] * len(outs),
        scratch_shapes=[pltpu.VMEM(shape, dtype) for shape, dtype in scratch],
        compiler_params=pltpu.CompilerParams(vmem_limit_bytes=24 << 20),
        cost_estimate=pl.CostEstimate(flops=flops, bytes_accessed=1 << 20, transcendentals=0),
    )(*args)


def body(block_values, block_rows, block_cols, block_count, basis):
    nz = lax.axis_size("col") // RING
    size, rank = basis.shape
    half = size // 2
    table = block_rows[0, 0] * 8 + block_cols[0, 0]
    flops = 2 * 24 * size * size * rank

    from_a, from_b = swap_y(basis, "a"), swap_y(basis, "b")
    blocks, mine = fetch(block_values, basis)
    from_a, from_b, blocks, mine = lax.optimization_barrier((from_a, from_b, blocks, mine))
    far0, far1 = swap_y(from_b[:half], "a"), swap_y(from_a[half:], "b")
    group = [from_a, from_b, far0, far1]
    other = [swap_core(basis)] + [swap_core(p) for p in group]

    two = (2, size, rank)
    keep0, keep1, send_a, send_b = call(
        forward_kernel, [(two, F32)] * 4, [((8, size, rank), BF16), ((8, size, rank), F32)], 2, flops,
        table, block_count, blocks, mine, *group, *other,
    )
    sum0 = keep0 + swap_x(send_a.astype(F16), "a").astype(F32) * (1 / SCALE_X)
    sum1 = keep1 + swap_x(send_b.astype(F16), "b").astype(F32) * (1 / SCALE_X)
    got0 = swap_x((sum0[1] * SCALE_Z).astype(F16), "b").astype(F32)
    got1 = swap_x((sum1[1] * SCALE_Z).astype(F16), "a").astype(F32)
    parts = jnp.concatenate([sum0[0] * SCALE_Z + got0, sum1[0] * SCALE_Z + got1], 0)
    parts = parts.astype(F16).reshape(nz, 2 * size // nz, rank)
    parts = lax.all_to_all(parts, "col", 0, 0, tiled=True, axis_index_groups=z_groups())
    share = (jnp.sum(parts.astype(F32), axis=0) * (1 / SCALE_Z)).astype(BF16)

    copies = jnp.broadcast_to(share[None], (nz, *share.shape))
    chunk = lax.all_to_all(copies, "col", 0, 0, tiled=True, axis_index_groups=z_groups()).reshape(two)
    from_a, from_b = swap_x(chunk, "a"), swap_x(chunk, "b")
    far0, far1 = swap_x(from_b[:1], "a"), swap_x(from_a[1:], "b")
    four = (RING, size, rank)
    keep, send = call(
        backward_kernel, [(four, F32), (four, BF16)], [((8, size, rank), BF16), ((8, size, rank), F32)], 2, flops,
        table, block_count, blocks, chunk, from_a, from_b, far0, far1,
    )
    part = (2, half, rank)
    keep0, keep1, send_a, send_b = call(
        pair_kernel, [(part, F32)] * 2 + [(part, BF16)] * 2, [], 0, 1 << 20, keep, swap_core(send)
    )
    sum0 = keep0 + swap_y(send_a, "a").astype(F32)
    sum1 = keep1 + swap_y(send_b, "b").astype(F32)
    out0 = sum0[0] + swap_y(sum0[1].astype(BF16), "b").astype(F32)
    out1 = sum1[0] + swap_y(sum1[1].astype(BF16), "a").astype(F32)
    return jnp.concatenate([out0, out1], 0)


def solution(mesh):
    in_specs = (
        P("row", "col", None, None, None),
        P("row", "col", None),
        P("row", "col", None),
        P("row", "col"),
        P(("col", "row"), None),
    )
    out_specs = P(("col", "row"), None)
    return jax.shard_map(body, mesh=mesh, in_specs=in_specs, out_specs=out_specs, check_vma=False)
```

time: 189 us -> 103 us (0.54)
  blocking collectives: 93.1 us -> 29.5 us
  local copies, waits for them, and re-layouts: 62.9 us -> 2.87 us
  waiting for transfers between devices: 2.87 us -> 29.3 us
  starting transfers between devices: 13.2 us -> 29 us
  matrix products: 11.9 us -> 0 us
  Pallas kernels: 0 us -> 8.14 us
    all_to_all x2, blocking collectives: 93.1 us -> 29.5 us  [the longest x1 17.7 us: body(): lax.all_to_all(parts, 'col', 0, 0, tiled=True, axis_index_groups=z_groups())]
    ppermute x0 -> x22, waiting for transfers between devices: none -> 29.3 us  [the longest x8 21.1 us: swap_x(): lax.ppermute(v, 'col', [(i, i // RING * RING + ring_partner(i % RING, way...]
    ppermute x0 -> x22, starting transfers between devices: none -> 29 us  [the longest x6 11.7 us: swap_core(): lax.ppermute(v, 'row', [(i, i ^ 1) for i in range(lax.axis_size('row'))])]
    dot_general x2 -> x0, local copies, waits for them, and re-layouts: 25.8 us -> none  [the longest x1 13.5 us: body(): row_part = jnp.dot(matrix, column_basis, preferred_element_type=jnp.float32)]
    scatter x2 -> x0, local copies, waits for them, and re-layouts: 19.5 us -> none  [body(): placed = placed.at[row_ids, :, col_ids, :].set(masked)]
    all_to_all x2 -> x0, starting transfers between devices: 13.2 us -> none  [from_everyone(): lax.all_to_all(jnp.broadcast_to(value[None], (count, *value.shape)), axis...]
    dot_general x2 -> x0, matrix products: 11.9 us -> none  [the longest x1 6.09 us: body(): row_part = jnp.dot(matrix, column_basis, preferred_element_type=jnp.float32)]
    pallas_call x0 -> x4, Pallas kernels: none -> 8.14 us  [the longest x3 7.74 us: call(): pl.pallas_call(kernel, out_shape=[jax.ShapeDtypeStruct(shape, dtype) for...]
  transfers between devices with their start and end apart: 2 -> 22, of which waited for: 1 -> 13; matrix products, arithmetic and copies ran while one was open for 33% -> 0% of each run, Pallas kernels for 0% -> 0%
where the time goes in v2:
time: 103 us; the launch traced here: 101 us
  blocking collectives  29.5 us (29%)
  waiting for transfers between devices  29.3 us (28%)
  starting transfers between devices  29 us (28%)
  Pallas kernels  8.14 us (8%)
  local copies, waits for them, and re-layouts  2.87 us (3%)
  other arithmetic  1.26 us (1%)
    ppermute x8, waiting for transfers between devices, swap_x(): lax.ppermute(v, 'col', [(i, i // RING * RING + ring_partner(i % RING, way...  21.1 us
    all_to_all x1, blocking collectives, body(): lax.all_to_all(parts, 'col', 0, 0, tiled=True, axis_index_groups=z_groups())  17.7 us
    all_to_all x1, blocking collectives, body(): lax.all_to_all(copies, 'col', 0, 0, tiled=True, axis_index_groups=z_group...  11.8 us
    ppermute x6, starting transfers between devices, swap_core(): lax.ppermute(v, 'row', [(i, i ^ 1) for i in range(lax.axis_size('row'))])  11.7 us
    ppermute x8, starting transfers between devices, swap_y(): lax.ppermute(v, 'row', [(i, ring_partner(i // CORES, way) * CORES + i % C...  10.3 us
    pallas_call x3, Pallas kernels, call(): pl.pallas_call(kernel, out_shape=[jax.ShapeDtypeStruct(shape, dtype) for...  7.74 us
    ppermute x8, starting transfers between devices, swap_x(): lax.ppermute(v, 'col', [(i, i // RING * RING + ring_partner(i % RING, way...  6.94 us
    ppermute x8, waiting for transfers between devices, swap_y(): lax.ppermute(v, 'row', [(i, ring_partner(i // CORES, way) * CORES + i % C...  6.41 us
  transfers between devices with their start and end apart: 22, of which 13 were waited for; matrix products, arithmetic and copies ran while one was open for 0% of the time, Pallas kernels for 0%

profile of v2, /device:TPU:1, one launch (start us, length us, event | category | flops | bytes accessed | tf_op | source)
XLA Modules:
  0.0 101.0 jit_solution(13833902413140650971)
XLA Ops:
  0.0 3.6 %collective-permute-start.1 = (bf16[256,256]{1,0:T(8,128)(2,1)}, bf16[256,256]{1,0:T(8,128)(2,1)S(1)}, u32[]{:S(2)}, u32[]{:S(2)}) collective-permute-start(bf16[256,256]{1,0:T(8,128)(2,1)} %basis.1), channel_id=1, source_target_pairs={{0,192},{32,224},{64,128},{96,160},{128,64},{160,96},{192,0},{224,... | collective-permute-start | bytes 393224 | tf_op jit(solution)/shard_map/ppermute | solution.py:23
  3.6 0.0 collective-permute-start
  3.6 0.0 copy-start
  3.6 1.9 %copy-done = bf16[1,1,24,256,256]{4,3,2,1,0:T(8,128)(2,1)S(1)} copy-done((bf16[1,1,24,256,256]{4,3,2,1,0:T(8,128)(2,1)S(1)}, bf16[1,1,24,256,256]{4,3,2,1,0:T(8,128)(2,1)}, u32[]{:S(2)}) %copy-start) | copy-done | bytes 3145752
  5.5 0.0 copy-start.1
  5.5 0.9 copy-done.1
  6.4 0.0 copy-start.2
  6.4 0.0 copy-start.3
  6.4 0.4 shard_map.55
  6.8 0.0 collective-permute-done.1.refs_2_
  6.8 1.1 %collective-permute-done.refs_1_ = bf16[256,256]{1,0:T(8,128)(2,1)S(1)} collective-permute-done((bf16[256,256]{1,0:T(8,128)(2,1)}, bf16[256,256]{1,0:T(8,128)(2,1)S(1)}, u32[]{:S(2)}, u32[]{:S(2)}) %collective-permute-start) | collective-permute-done | bytes 131104 | tf_op jit(solution)/shard_map/ppermute | solution.py:23
  7.9 0.5 collective-permute-start.2
  8.4 1.2 %collective-permute-start.3 = (bf16[128,256]{1,0:T(8,128)(2,1)S(1)}, bf16[128,256]{1,0:T(8,128)(2,1)S(1)}, u32[]{:S(2)}, u32[]{:S(2)}) collective-permute-start(bf16[128,256]{1,0:T(8,128)(2,1)S(1)} %slice.39), channel_id=1, source_target_pairs={{0,192},{32,224},{64,128},{96,160},{128,64},{160,96},{192,0},{224,... | collective-permute-start | bytes 196616 | tf_op jit(solution)/shard_map/ppermute | solution.py:23
  9.6 2.3 %collective-permute-start.4 = (bf16[256,256]{1,0:T(8,128)(2,1)S(1)}, bf16[256,256]{1,0:T(8,128)(2,1)S(1)}, u32[]{:S(2)}, u32[]{:S(2)}) collective-permute-start(bf16[256,256]{1,0:T(8,128)(2,1)S(1)} %copy-done.1), channel_id=1, source_target_pairs={{0,32},{32,0},{64,96},{96,64},{128,160},{160,128},{192,224},{224,1... | collective-permute-start | bytes 393224 | tf_op jit(solution)/shard_map/ppermute | solution.py:18
  11.8 0.0 collective-permute-start.5
  11.8 0.5 collective-permute-start.6
  12.3 0.0 collective-permute-done.2.refs_3_
  12.3 1.7 %collective-permute-start.7 = (bf16[128,256]{1,0:T(8,128)(2,1)S(1)}, bf16[128,256]{1,0:T(8,128)(2,1)S(1)}, u32[]{:S(2)}, u32[]{:S(2)}) collective-permute-start(bf16[128,256]{1,0:T(8,128)(2,1)S(1)} %collective-permute-done.2.refs_3_), channel_id=1, source_target_pairs={{0,32},{32,0},{64,96},{96,64},{128,160},{160,128},{192,224},{224,1... | collective-permute-start | bytes 196616 | tf_op jit(solution)/shard_map/ppermute | solution.py:18
  14.0 0.0 collective-permute-done.3.refs_4_
  14.0 1.5 %collective-permute-start.8 = (bf16[128,256]{1,0:T(8,128)(2,1)S(1)}, bf16[128,256]{1,0:T(8,128)(2,1)S(1)}, u32[]{:S(2)}, u32[]{:S(2)}) collective-permute-start(bf16[128,256]{1,0:T(8,128)(2,1)S(1)} %collective-permute-done.3.refs_4_), channel_id=1, source_target_pairs={{0,32},{32,0},{64,96},{96,64},{128,160},{160,128},{192,224},{224,1... | collective-permute-start | bytes 196616 | tf_op jit(solution)/shard_map/ppermute | solution.py:18
  15.5 0.0 copy-done.2
  15.5 0.0 copy-done.3
  16.2 0.0 collective-permute-done.4.refs_5_
  16.2 0.0 collective-permute-done.7.refs_8_
  16.2 0.2 collective-permute-done.8.refs_9_
  16.4 0.0 collective-permute-done.5.refs_6_
  16.4 0.0 collective-permute-done.6.refs_7_
  16.4 3.6 %shard_map.56 = (f32[2,256,256]{2,1,0:T(8,128)S(1)}, f32[2,256,256]{2,1,0:T(8,128)S(1)}, f32[2,256,256]{2,1,0:T(8,128)S(1)}, f32[2,256,256]{2,1,0:T(8,128)S(1)}) custom-call(s32[24]{0:T(128)S(1)} %add_bitcast_fusion.table, s32[1,1]{1,0:T(1,128)S(6)} %copy.6.count, bf16[1,1,24,256,256]{4,3,2,1,0:T(8,128)(2,1)S(1)} %get-tuple-element.23.blocks, ...), custom_call_target="tpu_custom_call" | custom-call | flops 805306368 | bytes 1048576 | tf_op jit(solution)/shard_map/pallas_call | solution.py:132
  20.1 2.0 %collective-permute-start.11 = (f16[2,256,256]{2,1,0:T(8,128)(2,1)S(1)}, f16[2,256,256]{2,1,0:T(8,128)(2,1)S(1)}, u32[]{:S(2)}, u32[]{:S(2)}) collective-permute-start(f16[2,256,256]{2,1,0:T(8,128)(2,1)S(1)} %convert_element_type.70), channel_id=1, source_target_pairs={{0,3},{1,2},{2,1},{3,0},{4,7},{5,6},{6,5},{7,4},{8,11},{9,10},{10,... | collective-permute-start | bytes 786440 | tf_op jit(solution)/shard_map/ppermute | solution.py:28
  22.1 0.1 collective-permute-start.9
  22.2 6.9 %collective-permute-done.11 = f16[2,256,256]{2,1,0:T(8,128)(2,1)S(1)} collective-permute-done((f16[2,256,256]{2,1,0:T(8,128)(2,1)S(1)}, f16[2,256,256]{2,1,0:T(8,128)(2,1)S(1)}, u32[]{:S(2)}, u32[]{:S(2)}) %collective-permute-start.11) | collective-permute-done | bytes 262176 | tf_op jit(solution)/shard_map/ppermute | solution.py:28
  29.1 0.1 multiply_add_fusion
  29.2 0.1 collective-permute-start.12
  29.3 0.8 collective-permute-done.9
  30.1 0.1 multiply_add_fusion.1
  30.2 1.6 %collective-permute-start.10 = (f16[256,256]{1,0:T(8,128)(2,1)S(1)}, f16[256,256]{1,0:T(8,128)(2,1)S(1)}, u32[]{:S(2)}, u32[]{:S(2)}) collective-permute-start(f16[256,256]{1,0:T(8,128)(2,1)S(1)} %fusion.8), channel_id=1, source_target_pairs={{0,3},{1,2},{2,1},{3,0},{4,7},{5,6},{6,5},{7,4},{8,11},{9,10},{10,... | collective-permute-start | bytes 393224 | tf_op jit(solution)/shard_map/ppermute | solution.py:28
  31.7 2.2 %collective-permute-done.12 = f16[256,256]{1,0:T(8,128)(2,1)S(1)} collective-permute-done((f16[256,256]{1,0:T(8,128)(2,1)S(1)}, f16[256,256]{1,0:T(8,128)(2,1)S(1)}, u32[]{:S(2)}, u32[]{:S(2)}) %collective-permute-start.12) | collective-permute-done | bytes 131104 | tf_op jit(solution)/shard_map/ppermute | solution.py:28
  34.0 1.6 %collective-permute-done.10 = f16[256,256]{1,0:T(8,128)(2,1)S(1)} collective-permute-done((f16[256,256]{1,0:T(8,128)(2,1)S(1)}, f16[256,256]{1,0:T(8,128)(2,1)S(1)}, u32[]{:S(2)}, u32[]{:S(2)}) %collective-permute-start.10) | collective-permute-done | bytes 131104 | tf_op jit(solution)/shard_map/ppermute | solution.py:28
  35.6 0.1 fusion.7
  35.7 0.1 pad_maximum_fusion
  35.8 17.7 %all_to_all.10 = f16[8,64,256]{2,1,0:T(8,128)(2,1)S(1)} all-to-all(f16[8,64,256]{2,1,0:T(8,128)(2,1)S(1)} %bitcast.35), channel_id=1, replica_groups={{0,4,8,12,16,20,24,28},{1,5,9,13,17,21,25,29},{2,6,10,14,18,22,26,30},{..., dimensions={0} | all-to-all | bytes 524288 | tf_op jit(solution)/shard_map/all_to_all | solution.py:168
  53.5 11.8 %all_to_all.11 = bf16[8,64,256]{2,1,0:T(8,128)(2,1)S(1)} all-to-all(bf16[8,64,256]{2,1,0:T(8,128)(2,1)S(1)} %broadcast_in_dim.2), channel_id=1, replica_groups={{0,4,8,12,16,20,24,28},{1,5,9,13,17,21,25,29},{2,6,10,14,18,22,26,30},{..., dimensions={0} | all-to-all | bytes 524288 | tf_op jit(solution)/shard_map/all_to_all | solution.py:172
  65.4 0.9 collective-permute-start.14
  66.2 0.8 collective-permute-start.13
  67.0 4.8 %collective-permute-done.14.from_b = bf16[2,256,256]{2,1,0:T(8,128)(2,1)S(1)} collective-permute-done((bf16[2,256,256]{2,1,0:T(8,128)(2,1)S(1)}, bf16[2,256,256]{2,1,0:T(8,128)(2,1)S(1)}, u32[]{:S(2)}, u32[]{:S(2)}) %collective-permute-start.14) | collective-permute-done | bytes 262176 | tf_op jit(solution)/shard_map/ppermute | solution.py:28
  71.8 0.5 collective-permute-start.15
  72.3 0.0 collective-permute-done.13.from_a
  72.4 1.0 %collective-permute-start.16 = (bf16[1,256,256]{2,1,0:T(8,128)(2,1)S(1)}, bf16[1,256,256]{2,1,0:T(8,128)(2,1)S(1)}, u32[]{:S(2)}, u32[]{:S(2)}) collective-permute-start(bf16[1,256,256]{2,1,0:T(8,128)(2,1)S(1)} %slice.55), channel_id=1, source_target_pairs={{0,3},{1,2},{2,1},{3,0},{4,7},{5,6},{6,5},{7,4},{8,11},{9,10},{10,... | collective-permute-start | bytes 393224 | tf_op jit(solution)/shard_map/ppermute | solution.py:28
  73.4 4.0 %collective-permute-done.15.far0 = bf16[1,256,256]{2,1,0:T(8,128)(2,1)S(1)} collective-permute-done((bf16[1,256,256]{2,1,0:T(8,128)(2,1)S(1)}, bf16[1,256,256]{2,1,0:T(8,128)(2,1)S(1)}, u32[]{:S(2)}, u32[]{:S(2)}) %collective-permute-start.15) | collective-permute-done | bytes 131104 | tf_op jit(solution)/shard_map/ppermute | solution.py:28
  77.4 0.8 collective-permute-done.16.far1
  78.2 4.0 %shard_map.57 = (f32[4,256,256]{2,1,0:T(8,128)S(1)}, bf16[4,256,256]{2,1,0:T(8,128)(2,1)S(1)}) custom-call(s32[24]{0:T(128)S(1)} %add_bitcast_fusion.table, s32[1,1]{1,0:T(1,128)S(6)} %copy.6.count, bf16[1,1,24,256,256]{4,3,2,1,0:T(8,128)(2,1)S(1)} %get-tuple-element.23.blocks, bf16[2,256,256]{2,1,0:T(8,128)(2,1)S(1)} %bitcast.34, ...), custom_call_target="tpu_custom_call" | custom-call | flops 805306368 | bytes 1048576 | tf_op jit(solution)/shard_map/pallas_call | solution.py:132
  82.3 5.8 %collective-permute-start.17 = (bf16[4,256,256]{2,1,0:T(8,128)(2,1)S(1)}, bf16[4,256,256]{2,1,0:T(8,128)(2,1)S(1)}, u32[]{:S(2)}, u32[]{:S(2)}) collective-permute-start(bf16[4,256,256]{2,1,0:T(8,128)(2,1)S(1)} %get-tuple-element.32), channel_id=1, source_target_pairs={{0,32},{32,0},{64,96},{96,64},{128,160},{160,128},{192,224},{224,1... | collective-permute-start | bytes 1572872 | tf_op jit(solution)/shard_map/ppermute | solution.py:18
  88.1 1.5 %collective-permute-done.17.other = bf16[4,256,256]{2,1,0:T(8,128)(2,1)S(1)} collective-permute-done((bf16[4,256,256]{2,1,0:T(8,128)(2,1)S(1)}, bf16[4,256,256]{2,1,0:T(8,128)(2,1)S(1)}, u32[]{:S(2)}, u32[]{:S(2)}) %collective-permute-start.17) | collective-permute-done | bytes 524320 | tf_op jit(solution)/shard_map/ppermute | solution.py:18
  89.6 0.1 shard_map.58
  89.7 0.1 collective-permute-start.18
  89.9 2.7 %collective-permute-start.20 = (bf16[2,128,256]{2,1,0:T(8,128)(2,1)S(1)}, bf16[2,128,256]{2,1,0:T(8,128)(2,1)S(1)}, u32[]{:S(2)}, u32[]{:S(2)}) collective-permute-start(bf16[2,128,256]{2,1,0:T(8,128)(2,1)S(1)} %get-tuple-element.36), channel_id=1, source_target_pairs={{0,192},{32,224},{64,128},{96,160},{128,64},{160,96},{192,0},{224,... | collective-permute-start | bytes 393224 | tf_op jit(solution)/shard_map/ppermute | solution.py:23
  92.5 2.0 %collective-permute-done.18 = bf16[2,128,256]{2,1,0:T(8,128)(2,1)S(1)} collective-permute-done((bf16[2,128,256]{2,1,0:T(8,128)(2,1)S(1)}, bf16[2,128,256]{2,1,0:T(8,128)(2,1)S(1)}, u32[]{:S(2)}, u32[]{:S(2)}) %collective-permute-start.18) | collective-permute-done | bytes 131104 | tf_op jit(solution)/shard_map/ppermute | solution.py:23
  94.6 2.1 %collective-permute-start.19 = (bf16[128,256]{1,0:T(8,128)(2,1)S(1)}, bf16[128,256]{1,0:T(8,128)(2,1)S(1)}, u32[]{:S(2)}, u32[]{:S(2)}) collective-permute-start(bf16[128,256]{1,0:T(8,128)(2,1)S(1)} %fusion.12), channel_id=1, source_target_pairs={{0,192},{32,224},{64,128},{96,160},{128,64},{160,96},{192,0},{224,... | collective-permute-start | bytes 196616 | tf_op jit(solution)/shard_map/ppermute | solution.py:23
  96.7 0.0 collective-permute-done.20
  96.8 0.2 collective-permute-start.21
  96.9 2.1 %collective-permute-done.19 = bf16[128,256]{1,0:T(8,128)(2,1)S(1)} collective-permute-done((bf16[128,256]{1,0:T(8,128)(2,1)S(1)}, bf16[128,256]{1,0:T(8,128)(2,1)S(1)}, u32[]{:S(2)}, u32[]{:S(2)}) %collective-permute-start.19) | collective-permute-done | bytes 65568 | tf_op jit(solution)/shard_map/ppermute | solution.py:23
  99.0 1.2 %collective-permute-done.21 = bf16[128,256]{1,0:T(8,128)(2,1)S(1)} collective-permute-done((bf16[128,256]{1,0:T(8,128)(2,1)S(1)}, bf16[128,256]{1,0:T(8,128)(2,1)S(1)}, u32[]{:S(2)}, u32[]{:S(2)}) %collective-permute-start.21) | collective-permute-done | bytes 65568 | tf_op jit(solution)/shard_map/ppermute | solution.py:23
  100.3 0.7 pad_maximum_fusion.1
  (19 shorter events, 0.4 us)
Async XLA Ops:
  0.0 6.8 %collective-permute-start.1 = (bf16[256,256]{1,0:T(8,128)(2,1)}, bf16[256,256]{1,0:T(8,128)(2,1)S(1)}, u32[]{:S(2)}, u32[]{:S(2)}) collective-permute-start(bf16[256,256]{1,0:T(8,128)(2,1)} %basis.1), channel_id=1, source_target_pairs={{0,192},{32,224},{64,128},{96,160},{128,64},{160,96},{192,0},{224,... | collective-permute-start | bytes 393224 | tf_op jit(solution)/shard_map/ppermute | solution.py:23
  3.6 4.3 %collective-permute-start = (bf16[256,256]{1,0:T(8,128)(2,1)}, bf16[256,256]{1,0:T(8,128)(2,1)S(1)}, u32[]{:S(2)}, u32[]{:S(2)}) collective-permute-start(bf16[256,256]{1,0:T(8,128)(2,1)} %basis.1), channel_id=1, source_target_pairs={{0,64},{32,96},{64,0},{96,32},{128,192},{160,224},{192,128},{224,1... | collective-permute-start | bytes 393224 | tf_op jit(solution)/shard_map/ppermute | solution.py:23
  3.6 1.9 %copy-start = (bf16[1,1,24,256,256]{4,3,2,1,0:T(8,128)(2,1)S(1)}, bf16[1,1,24,256,256]{4,3,2,1,0:T(8,128)(2,1)}, u32[]{:S(2)}) copy-start(bf16[1,1,24,256,256]{4,3,2,1,0:T(8,128)(2,1)} %blocks.1) | copy-start | bytes 9437188
  5.5 0.9 copy-start.1
  6.4 9.1 %copy-start.2 = (s32[1,1,24]{2,1,0:T(1,128)S(1)}, s32[1,1,24]{2,1,0:T(1,128)}, u32[]{:S(2)}) copy-start(s32[1,1,24]{2,1,0:T(1,128)} %param.7) | copy-start | bytes 292
  6.4 9.1 %copy-start.3 = (s32[1,1,24]{2,1,0:T(1,128)S(1)}, s32[1,1,24]{2,1,0:T(1,128)}, u32[]{:S(2)}) copy-start(s32[1,1,24]{2,1,0:T(1,128)} %param.6) | copy-start | bytes 292
  7.9 4.5 %collective-permute-start.2 = (bf16[128,256]{1,0:T(8,128)(2,1)S(1)}, bf16[128,256]{1,0:T(8,128)(2,1)S(1)}, u32[]{:S(2)}, u32[]{:S(2)}) collective-permute-start(bf16[128,256]{1,0:T(8,128)(2,1)S(1)} %slice.38), channel_id=1, source_target_pairs={{0,64},{32,96},{64,0},{96,32},{128,192},{160,224},{192,128},{224,1... | collective-permute-start | bytes 196616 | tf_op jit(solution)/shard_map/ppermute | solution.py:23
  8.4 5.7 %collective-permute-start.3 = (bf16[128,256]{1,0:T(8,128)(2,1)S(1)}, bf16[128,256]{1,0:T(8,128)(2,1)S(1)}, u32[]{:S(2)}, u32[]{:S(2)}) collective-permute-start(bf16[128,256]{1,0:T(8,128)(2,1)S(1)} %slice.39), channel_id=1, source_target_pairs={{0,192},{32,224},{64,128},{96,160},{128,64},{160,96},{192,0},{224,... | collective-permute-start | bytes 196616 | tf_op jit(solution)/shard_map/ppermute | solution.py:23
  9.6 6.6 %collective-permute-start.4 = (bf16[256,256]{1,0:T(8,128)(2,1)S(1)}, bf16[256,256]{1,0:T(8,128)(2,1)S(1)}, u32[]{:S(2)}, u32[]{:S(2)}) collective-permute-start(bf16[256,256]{1,0:T(8,128)(2,1)S(1)} %copy-done.1), channel_id=1, source_target_pairs={{0,32},{32,0},{64,96},{96,64},{128,160},{160,128},{192,224},{224,1... | collective-permute-start | bytes 393224 | tf_op jit(solution)/shard_map/ppermute | solution.py:18
  11.8 4.6 %collective-permute-start.5 = (bf16[256,256]{1,0:T(8,128)(2,1)S(1)}, bf16[256,256]{1,0:T(8,128)(2,1)S(1)}, u32[]{:S(2)}, u32[]{:S(2)}) collective-permute-start(bf16[256,256]{1,0:T(8,128)(2,1)S(1)} %collective-permute-done.refs_1_), channel_id=1, source_target_pairs={{0,32},{32,0},{64,96},{96,64},{128,160},{160,128},{192,224},{224,1... | collective-permute-start | bytes 393224 | tf_op jit(solution)/shard_map/ppermute | solution.py:18
  11.8 4.6 %collective-permute-start.6 = (bf16[256,256]{1,0:T(8,128)(2,1)S(1)}, bf16[256,256]{1,0:T(8,128)(2,1)S(1)}, u32[]{:S(2)}, u32[]{:S(2)}) collective-permute-start(bf16[256,256]{1,0:T(8,128)(2,1)S(1)} %collective-permute-done.1.refs_2_), channel_id=1, source_target_pairs={{0,32},{32,0},{64,96},{96,64},{128,160},{160,128},{192,224},{224,1... | collective-permute-start | bytes 393224 | tf_op jit(solution)/shard_map/ppermute | solution.py:18
  12.3 3.8 %collective-permute-start.7 = (bf16[128,256]{1,0:T(8,128)(2,1)S(1)}, bf16[128,256]{1,0:T(8,128)(2,1)S(1)}, u32[]{:S(2)}, u32[]{:S(2)}) collective-permute-start(bf16[128,256]{1,0:T(8,128)(2,1)S(1)} %collective-permute-done.2.refs_3_), channel_id=1, source_target_pairs={{0,32},{32,0},{64,96},{96,64},{128,160},{160,128},{192,224},{224,1... | collective-permute-start | bytes 196616 | tf_op jit(solution)/shard_map/ppermute | solution.py:18
  14.0 2.4 %collective-permute-start.8 = (bf16[128,256]{1,0:T(8,128)(2,1)S(1)}, bf16[128,256]{1,0:T(8,128)(2,1)S(1)}, u32[]{:S(2)}, u32[]{:S(2)}) collective-permute-start(bf16[128,256]{1,0:T(8,128)(2,1)S(1)} %collective-permute-done.3.refs_4_), channel_id=1, source_target_pairs={{0,32},{32,0},{64,96},{96,64},{128,160},{160,128},{192,224},{224,1... | collective-permute-start | bytes 196616 | tf_op jit(solution)/shard_map/ppermute | solution.py:18
  20.1 9.0 %collective-permute-start.11 = (f16[2,256,256]{2,1,0:T(8,128)(2,1)S(1)}, f16[2,256,256]{2,1,0:T(8,128)(2,1)S(1)}, u32[]{:S(2)}, u32[]{:S(2)}) collective-permute-start(f16[2,256,256]{2,1,0:T(8,128)(2,1)S(1)} %convert_element_type.70), channel_id=1, source_target_pairs={{0,3},{1,2},{2,1},{3,0},{4,7},{5,6},{6,5},{7,4},{8,11},{9,10},{10,... | collective-permute-start | bytes 786440 | tf_op jit(solution)/shard_map/ppermute | solution.py:28
  22.1 8.0 %collective-permute-start.9 = (f16[2,256,256]{2,1,0:T(8,128)(2,1)S(1)}, f16[2,256,256]{2,1,0:T(8,128)(2,1)S(1)}, u32[]{:S(2)}, u32[]{:S(2)}) collective-permute-start(f16[2,256,256]{2,1,0:T(8,128)(2,1)S(1)} %convert_element_type.65), channel_id=1, source_target_pairs={{0,1},{1,0},{2,3},{3,2},{4,5},{5,4},{6,7},{7,6},{8,9},{9,8},{10,11... | collective-permute-start | bytes 786440 | tf_op jit(solution)/shard_map/ppermute | solution.py:28
  29.2 4.8 %collective-permute-start.12 = (f16[256,256]{1,0:T(8,128)(2,1)S(1)}, f16[256,256]{1,0:T(8,128)(2,1)S(1)}, u32[]{:S(2)}, u32[]{:S(2)}) collective-permute-start(f16[256,256]{1,0:T(8,128)(2,1)S(1)} %fusion.9), channel_id=1, source_target_pairs={{0,1},{1,0},{2,3},{3,2},{4,5},{5,4},{6,7},{7,6},{8,9},{9,8},{10,11... | collective-permute-start | bytes 393224 | tf_op jit(solution)/shard_map/ppermute | solution.py:28
  30.2 5.5 %collective-permute-start.10 = (f16[256,256]{1,0:T(8,128)(2,1)S(1)}, f16[256,256]{1,0:T(8,128)(2,1)S(1)}, u32[]{:S(2)}, u32[]{:S(2)}) collective-permute-start(f16[256,256]{1,0:T(8,128)(2,1)S(1)} %fusion.8), channel_id=1, source_target_pairs={{0,3},{1,2},{2,1},{3,0},{4,7},{5,6},{6,5},{7,4},{8,11},{9,10},{10,... | collective-permute-start | bytes 393224 | tf_op jit(solution)/shard_map/ppermute | solution.py:28
  65.4 6.4 %collective-permute-start.14 = (bf16[2,256,256]{2,1,0:T(8,128)(2,1)S(1)}, bf16[2,256,256]{2,1,0:T(8,128)(2,1)S(1)}, u32[]{:S(2)}, u32[]{:S(2)}) collective-permute-start(bf16[2,256,256]{2,1,0:T(8,128)(2,1)S(1)} %bitcast.32), channel_id=1, source_target_pairs={{0,3},{1,2},{2,1},{3,0},{4,7},{5,6},{6,5},{7,4},{8,11},{9,10},{10,... | collective-permute-start | bytes 786440 | tf_op jit(solution)/shard_map/ppermute | solution.py:28
  66.2 6.1 %collective-permute-start.13 = (bf16[2,256,256]{2,1,0:T(8,128)(2,1)S(1)}, bf16[2,256,256]{2,1,0:T(8,128)(2,1)S(1)}, u32[]{:S(2)}, u32[]{:S(2)}) collective-permute-start(bf16[2,256,256]{2,1,0:T(8,128)(2,1)S(1)} %bitcast.33), channel_id=1, source_target_pairs={{0,1},{1,0},{2,3},{3,2},{4,5},{5,4},{6,7},{7,6},{8,9},{9,8},{10,11... | collective-permute-start | bytes 786440 | tf_op jit(solution)/shard_map/ppermute | solution.py:28
  71.8 5.6 %collective-permute-start.15 = (bf16[1,256,256]{2,1,0:T(8,128)(2,1)S(1)}, bf16[1,256,256]{2,1,0:T(8,128)(2,1)S(1)}, u32[]{:S(2)}, u32[]{:S(2)}) collective-permute-start(bf16[1,256,256]{2,1,0:T(8,128)(2,1)S(1)} %slice.54), channel_id=1, source_target_pairs={{0,1},{1,0},{2,3},{3,2},{4,5},{5,4},{6,7},{7,6},{8,9},{9,8},{10,11... | collective-permute-start | bytes 393224 | tf_op jit(solution)/shard_map/ppermute | solution.py:28
  72.4 5.9 %collective-permute-start.16 = (bf16[1,256,256]{2,1,0:T(8,128)(2,1)S(1)}, bf16[1,256,256]{2,1,0:T(8,128)(2,1)S(1)}, u32[]{:S(2)}, u32[]{:S(2)}) collective-permute-start(bf16[1,256,256]{2,1,0:T(8,128)(2,1)S(1)} %slice.55), channel_id=1, source_target_pairs={{0,3},{1,2},{2,1},{3,0},{4,7},{5,6},{6,5},{7,4},{8,11},{9,10},{10,... | collective-permute-start | bytes 393224 | tf_op jit(solution)/shard_map/ppermute | solution.py:28
  82.3 7.4 %collective-permute-start.17 = (bf16[4,256,256]{2,1,0:T(8,128)(2,1)S(1)}, bf16[4,256,256]{2,1,0:T(8,128)(2,1)S(1)}, u32[]{:S(2)}, u32[]{:S(2)}) collective-permute-start(bf16[4,256,256]{2,1,0:T(8,128)(2,1)S(1)} %get-tuple-element.32), channel_id=1, source_target_pairs={{0,32},{32,0},{64,96},{96,64},{128,160},{160,128},{192,224},{224,1... | collective-permute-start | bytes 1572872 | tf_op jit(solution)/shard_map/ppermute | solution.py:18
  89.7 4.8 %collective-permute-start.18 = (bf16[2,128,256]{2,1,0:T(8,128)(2,1)S(1)}, bf16[2,128,256]{2,1,0:T(8,128)(2,1)S(1)}, u32[]{:S(2)}, u32[]{:S(2)}) collective-permute-start(bf16[2,128,256]{2,1,0:T(8,128)(2,1)S(1)} %get-tuple-element.34), channel_id=1, source_target_pairs={{0,64},{32,96},{64,0},{96,32},{128,192},{160,224},{192,128},{224,1... | collective-permute-start | bytes 393224 | tf_op jit(solution)/shard_map/ppermute | solution.py:23
  89.9 6.8 %collective-permute-start.20 = (bf16[2,128,256]{2,1,0:T(8,128)(2,1)S(1)}, bf16[2,128,256]{2,1,0:T(8,128)(2,1)S(1)}, u32[]{:S(2)}, u32[]{:S(2)}) collective-permute-start(bf16[2,128,256]{2,1,0:T(8,128)(2,1)S(1)} %get-tuple-element.36), channel_id=1, source_target_pairs={{0,192},{32,224},{64,128},{96,160},{128,64},{160,96},{192,0},{224,... | collective-permute-start | bytes 393224 | tf_op jit(solution)/shard_map/ppermute | solution.py:23
  94.6 4.4 %collective-permute-start.19 = (bf16[128,256]{1,0:T(8,128)(2,1)S(1)}, bf16[128,256]{1,0:T(8,128)(2,1)S(1)}, u32[]{:S(2)}, u32[]{:S(2)}) collective-permute-start(bf16[128,256]{1,0:T(8,128)(2,1)S(1)} %fusion.12), channel_id=1, source_target_pairs={{0,192},{32,224},{64,128},{96,160},{128,64},{160,96},{192,0},{224,... | collective-permute-start | bytes 196616 | tf_op jit(solution)/shard_map/ppermute | solution.py:23
  96.8 3.5 %collective-permute-start.21 = (bf16[128,256]{1,0:T(8,128)(2,1)S(1)}, bf16[128,256]{1,0:T(8,128)(2,1)S(1)}, u32[]{:S(2)}, u32[]{:S(2)}) collective-permute-start(bf16[128,256]{1,0:T(8,128)(2,1)S(1)} %fusion.13), channel_id=1, source_target_pairs={{0,64},{32,96},{64,0},{96,32},{128,192},{160,224},{192,128},{224,1... | collective-permute-start | bytes 196616 | tf_op jit(solution)/shard_map/ppermute | solution.py:23

commit v3 on v1

--- a/solution.py
+++ b/solution.py
@@ -12,6 +12,7 @@
 F16 = jnp.float16
 CORES = 2
 NX = 4
+UNROLL = 8
 SCALE_X = 64.0
 SCALE_Z = 16.0
 
@@ -41,7 +42,53 @@
     return [pl.BlockSpec(memory_space=pltpu.SMEM)] * n
 
 
-def forward_kernel(rows, cols, count, blocks, *refs):
+def fetch_kernel(blocks, basis, blocks_out, basis_out, sems):
+    copies = [
+        pltpu.make_async_copy(blocks, blocks_out, sems.at[0]),
+        pltpu.make_async_copy(basis, basis_out, sems.at[1]),
+    ]
+    for copy in copies:
+        copy.start()
+    for copy in copies:
+        copy.wait()
+
+
+def fetch(blocks, basis):
+    return pl.pallas_call(
+        fetch_kernel,
+        out_shape=[jax.ShapeDtypeStruct(blocks.shape, blocks.dtype), jax.ShapeDtypeStruct(basis.shape, basis.dtype)],
+        in_specs=[pl.BlockSpec(memory_space=pltpu.HBM)] * 2,
+        out_specs=[pl.BlockSpec(memory_space=pltpu.VMEM)] * 2,
+        scratch_shapes=[pltpu.SemaphoreType.DMA((2,))],
+        compiler_params=pltpu.CompilerParams(vmem_limit_bytes=16 << 20),
+        cost_estimate=pl.CostEstimate(flops=0, bytes_accessed=8 << 20, transcendentals=0),
+    )(blocks, basis)
+
+
+def add_products(table, count, blocks, basis, acc, transposed):
+    live, spare = count[0, 0], acc.shape[0] - 1
+    acc[...] = jnp.zeros_like(acc)
+
+    def visit(step, carry):
+        products, targets = [], []
+        for u in range(UNROLL):
+            s = step * UNROLL + u
+            r, c = table[s] // 8, table[s] % 8
+            source, target, dim = (r, c, 0) if transposed else (c, r, 1)
+            products.append(
+                lax.dot_general(
+                    blocks[0, 0, s], basis[source], (((dim,), (0,)), ((), ())), preferred_element_type=F32
+                )
+            )
+            targets.append(jnp.where(s < live, target, spare))
+        for target, product in zip(targets, products):
+            acc[target] += product
+        return carry
+
+    lax.fori_loop(0, (live + UNROLL - 1) // UNROLL, visit, 0)
+
+
+def forward_kernel(table, count, blocks, *refs):
     pieces, (own, *sends), (basis, acc) = refs[:8], refs[8:12], refs[12:]
     y, k = lax.axis_index("row") // CORES, lax.axis_index("row") % CORES
     x = lax.axis_index("col") % NX
@@ -49,14 +96,7 @@
         at = (y + 4 - d) % 4
         basis[at * CORES + k] = pieces[d][...]
         basis[at * CORES + 1 - k] = pieces[4 + d][...]
-    acc[...] = jnp.zeros_like(acc)
-
-    def visit(s, carry):
-        r, c = rows[0, 0, s], cols[0, 0, s]
-        acc[r] += jnp.dot(blocks[0, 0, s], basis[c], preferred_element_type=F32)
-        return carry
-
-    lax.fori_loop(0, count[0, 0], visit, 0)
+    add_products(table, count, blocks, basis, acc, False)
     for h in range(2):
         own[h] = acc[x * 2 + h]
     for d in range(1, 4):
@@ -65,7 +105,7 @@
             sends[d - 1][h] = acc[to * 2 + h] * SCALE_X
 
 
-def backward_kernel(rows, cols, count, blocks, *refs):
+def backward_kernel(table, count, blocks, *refs):
     pieces, (own, send), (basis, acc) = refs[:4], refs[4:6], refs[6:]
     k = lax.axis_index("row") % CORES
     x = lax.axis_index("col") % NX
@@ -73,45 +113,40 @@
         at = (x + 4 - d) % 4
         for h in range(2):
             basis[at * 2 + h] = pieces[d][h]
-    acc[...] = jnp.zeros_like(acc)
-
-    def visit(s, carry):
-        r, c = rows[0, 0, s], cols[0, 0, s]
-        acc[c] += lax.dot_general(
-            blocks[0, 0, s], basis[r], (((0,), (0,)), ((), ())), preferred_element_type=F32
-        )
-        return carry
-
-    lax.fori_loop(0, count[0, 0], visit, 0)
+    add_products(table, count, blocks, basis, acc, True)
     for y in range(4):
         own[y] = acc[y * CORES + k]
         send[y] = acc[y * CORES + 1 - k].astype(send.dtype)
 
 
 def call(kernel, outs, scratch, n_vmem, *args):
+    flops = 2 * 24 * 256**3
     return pl.pallas_call(
         kernel,
         out_shape=outs,
-        in_specs=smem(3) + vmem(n_vmem),
+        in_specs=smem(2) + vmem(n_vmem),
         out_specs=vmem(len(outs)),
         scratch_shapes=scratch,
-        compiler_params=pltpu.CompilerParams(vmem_limit_bytes=24 << 20),
+        compiler_params=pltpu.CompilerParams(vmem_limit_bytes=28 << 20),
+        cost_estimate=pl.CostEstimate(flops=flops, bytes_accessed=1 << 20, transcendentals=0),
     )(*args)
 
 
 def body(block_values, block_rows, block_cols, block_count, basis):
     n_row, n_col = lax.axis_size("row"), lax.axis_size("col")
     size, rank = basis.shape
-    table = (block_rows, block_cols, block_count)
+    table = (block_rows[0, 0] * 8 + block_cols[0, 0], block_count)
 
     mine = [basis] + [lax.ppermute(basis, "row", shift_y(n_row, d)) for d in (1, 2, 3)]
+    blocks, own = fetch(block_values, basis)
+    mine[1], blocks, own = lax.optimization_barrier((mine[1], blocks, own))
     other = [lax.ppermute(p, "row", swap_core(n_row)) for p in mine]
     own, *sends = call(
         forward_kernel,
         [jax.ShapeDtypeStruct((2, size, rank), F32)] * 4,
-        [pltpu.VMEM((8, size, rank), BF16), pltpu.VMEM((8, size, rank), F32)],
+        [pltpu.VMEM((8, size, rank), BF16), pltpu.VMEM((9, size, rank), F32)],
         9,
-        *table, block_values, *mine, *other,
+        *table, blocks, own, *mine[1:], *other,
     )
     got = [lax.ppermute(s.astype(F16), "col", shift_x(n_col, d)) for d, s in zip((1, 2, 3), sends)]
     x_sum = own + (got[0].astype(F32) + got[1].astype(F32) + got[2].astype(F32)) * (1 / SCALE_X)
@@ -127,9 +162,9 @@
     own, send = call(
         backward_kernel,
         [jax.ShapeDtypeStruct((4, size, rank), F32), jax.ShapeDtypeStruct((4, size, rank), BF16)],
-        [pltpu.VMEM((8, size, rank), BF16), pltpu.VMEM((8, size, rank), F32)],
+        [pltpu.VMEM((8, size, rank), BF16), pltpu.VMEM((9, size, rank), F32)],
         5,
-        *table, block_values, *chunks,
+        *table, blocks, *chunks,
     )
     pair = own + lax.ppermute(send, "row", swap_core(n_row)).astype(F32)
     y = lax.axis_index("row") // CORES

time: 104 us -> 92.5 us (0.89)
  the two profiles are of different devices: /device:TPU:2 before, /device:TPU:1 now
where the time goes in v3:
time: 92.5 us; the launch traced here: 91.8 us
  blocking collectives  30 us (32%)
  starting transfers between devices  28.5 us (31%)
  waiting for transfers between devices  25.2 us (27%)
  Pallas kernels  3.21 us (3%)
  local copies, waits for them, and re-layouts  2.87 us (3%)
  other arithmetic  1.23 us (1%)
    all_to_all x1, blocking collectives, body(): lax.all_to_all(parts, 'col', 0, 0, tiled=True, axis_index_groups=z_groups...  18 us
    all_to_all x1, blocking collectives, body(): lax.all_to_all(copies, 'col', 0, 0, tiled=True, axis_index_groups=z_group...  12 us
    ppermute x3, waiting for transfers between devices, body(): lax.ppermute(s.astype(F16), 'col', shift_x(n_col, d))  10.9 us
    ppermute x3, waiting for transfers between devices, body(): lax.ppermute(chunk, 'col', shift_x(n_col, d))  6.59 us
    ppermute x3, starting transfers between devices, body(): lax.ppermute(basis, 'row', shift_y(n_row, d))  5.81 us
    ppermute x3, starting transfers between devices, body(): lax.ppermute(s.astype(F16), 'col', shift_x(n_col, d))  5.14 us
    ppermute x3, starting transfers between devices, body(): lax.ppermute(chunk, 'col', shift_x(n_col, d))  5.14 us
    ppermute x3, waiting for transfers between devices, body(): lax.ppermute(pick(d).astype(BF16), 'row', shift_y(n_row, d))  5.09 us
  transfers between devices with their start and end apart: 17, of which 10 were waited for; matrix products, arithmetic and copies ran while one was open for 0% of the time, Pallas kernels for 0%

profile of v3, /device:TPU:1, one launch (start us, length us, event | category | flops | bytes accessed | tf_op | source)
XLA Modules:
  0.0 91.8 jit_solution(17122404476517981618)
XLA Ops:
  0.0 2.1 %collective-permute-start = (bf16[256,256]{1,0:T(8,128)(2,1)}, bf16[256,256]{1,0:T(8,128)(2,1)S(1)}, u32[]{:S(2)}, u32[]{:S(2)}) collective-permute-start(bf16[256,256]{1,0:T(8,128)(2,1)} %basis.1), channel_id=1, source_target_pairs={{0,64},{32,96},{64,128},{96,160},{128,192},{160,224},{192,0},{224,... | collective-permute-start | bytes 393224 | tf_op jit(solution)/shard_map/ppermute | solution.py:140
  2.1 2.6 %collective-permute-start.1 = (bf16[256,256]{1,0:T(8,128)(2,1)}, bf16[256,256]{1,0:T(8,128)(2,1)S(1)}, u32[]{:S(2)}, u32[]{:S(2)}) collective-permute-start(bf16[256,256]{1,0:T(8,128)(2,1)} %basis.1), channel_id=1, source_target_pairs={{0,128},{32,160},{64,192},{96,224},{128,0},{160,32},{192,64},{224,... | collective-permute-start | bytes 393224 | tf_op jit(solution)/shard_map/ppermute | solution.py:140
  4.7 1.1 %collective-permute-start.2 = (bf16[256,256]{1,0:T(8,128)(2,1)}, bf16[256,256]{1,0:T(8,128)(2,1)S(1)}, u32[]{:S(2)}, u32[]{:S(2)}) collective-permute-start(bf16[256,256]{1,0:T(8,128)(2,1)} %basis.1), channel_id=1, source_target_pairs={{0,192},{32,224},{64,0},{96,32},{128,64},{160,96},{192,128},{224,1... | collective-permute-start | bytes 393224 | tf_op jit(solution)/shard_map/ppermute | solution.py:140
  5.8 1.5 %collective-permute-start.3 = (bf16[256,256]{1,0:T(8,128)(2,1)}, bf16[256,256]{1,0:T(8,128)(2,1)S(1)}, u32[]{:S(2)}, u32[]{:S(2)}) collective-permute-start(bf16[256,256]{1,0:T(8,128)(2,1)} %basis.1), channel_id=1, source_target_pairs={{0,32},{32,0},{64,96},{96,64},{128,160},{160,128},{192,224},{224,1... | collective-permute-start | bytes 393224 | tf_op jit(solution)/shard_map/ppermute | solution.py:143
  7.3 0.0 copy-start
  7.3 1.9 %copy-done = bf16[1,1,24,256,256]{4,3,2,1,0:T(8,128)(2,1)S(1)} copy-done((bf16[1,1,24,256,256]{4,3,2,1,0:T(8,128)(2,1)S(1)}, bf16[1,1,24,256,256]{4,3,2,1,0:T(8,128)(2,1)}, u32[]{:S(2)}) %copy-start) | copy-done | bytes 3145752
  9.2 0.0 copy-start.1
  9.2 0.9 copy-done.1
  10.1 0.0 copy-start.2
  10.1 0.0 copy-start.3
  10.1 0.4 shard_map.55
  11.2 0.0 collective-permute-done.refs_1_
  11.2 1.2 %collective-permute-start.4 = (bf16[256,256]{1,0:T(8,128)(2,1)S(1)}, bf16[256,256]{1,0:T(8,128)(2,1)S(1)}, u32[]{:S(2)}, u32[]{:S(2)}) collective-permute-start(bf16[256,256]{1,0:T(8,128)(2,1)S(1)} %collective-permute-done.refs_1_), channel_id=1, source_target_pairs={{0,32},{32,0},{64,96},{96,64},{128,160},{160,128},{192,224},{224,1... | collective-permute-start | bytes 393224 | tf_op jit(solution)/shard_map/ppermute | solution.py:143
  12.4 0.0 collective-permute-done.1.refs_2_
  12.4 0.0 collective-permute-start.5
  12.4 0.0 collective-permute-done.2.refs_3_
  12.5 0.5 collective-permute-start.6
  13.0 0.0 copy-done.2
  13.0 0.0 copy-done.3
  13.0 0.0 collective-permute-done.3.refs_4_
  13.0 0.4 collective-permute-done.4.refs_5_
  13.4 0.4 collective-permute-done.5.refs_6_
  13.8 0.2 collective-permute-done.6.refs_7_
  14.0 1.4 %shard_map.56 = (f32[2,256,256]{2,1,0:T(8,128)S(1)}, f32[2,256,256]{2,1,0:T(8,128)S(1)}, f32[2,256,256]{2,1,0:T(8,128)S(1)}, f32[2,256,256]{2,1,0:T(8,128)S(1)}) custom-call(s32[24]{0:T(128)S(1)} %add_bitcast_fusion.table, s32[1,1]{1,0:T(1,128)S(6)} %copy.6.count, bf16[1,1,24,256,256]{4,3,2,1,0:T(8,128)(2,1)S(1)} %get-tuple-element.18.blocks, ...), custom_call_target="tpu_custom_call" | custom-call | flops 805306368 | bytes 1048576 | tf_op jit(solution)/shard_map/pallas_call | solution.py:124
  15.4 0.9 collective-permute-start.7
  16.4 3.0 %collective-permute-start.8 = (f16[2,256,256]{2,1,0:T(8,128)(2,1)S(1)}, f16[2,256,256]{2,1,0:T(8,128)(2,1)S(1)}, u32[]{:S(2)}, u32[]{:S(2)}) collective-permute-start(f16[2,256,256]{2,1,0:T(8,128)(2,1)S(1)} %convert_element_type.63), channel_id=1, source_target_pairs={{0,2},{1,3},{2,0},{3,1},{4,6},{5,7},{6,4},{7,5},{8,10},{9,11},{10,... | collective-permute-start | bytes 786440 | tf_op jit(solution)/shard_map/ppermute | solution.py:151
  19.4 1.2 %collective-permute-start.9 = (f16[2,256,256]{2,1,0:T(8,128)(2,1)S(1)}, f16[2,256,256]{2,1,0:T(8,128)(2,1)S(1)}, u32[]{:S(2)}, u32[]{:S(2)}) collective-permute-start(f16[2,256,256]{2,1,0:T(8,128)(2,1)S(1)} %convert_element_type.65), channel_id=1, source_target_pairs={{0,3},{1,0},{2,1},{3,2},{4,7},{5,4},{6,5},{7,6},{8,11},{9,8},{10,9... | collective-permute-start | bytes 786440 | tf_op jit(solution)/shard_map/ppermute | solution.py:151
  20.7 3.6 %collective-permute-done.7 = f16[2,256,256]{2,1,0:T(8,128)(2,1)S(1)} collective-permute-done((f16[2,256,256]{2,1,0:T(8,128)(2,1)S(1)}, f16[2,256,256]{2,1,0:T(8,128)(2,1)S(1)}, u32[]{:S(2)}, u32[]{:S(2)}) %collective-permute-start.7) | collective-permute-done | bytes 262176 | tf_op jit(solution)/shard_map/ppermute | solution.py:151
  24.3 7.3 %collective-permute-done.8 = f16[2,256,256]{2,1,0:T(8,128)(2,1)S(1)} collective-permute-done((f16[2,256,256]{2,1,0:T(8,128)(2,1)S(1)}, f16[2,256,256]{2,1,0:T(8,128)(2,1)S(1)}, u32[]{:S(2)}, u32[]{:S(2)}) %collective-permute-start.8) | collective-permute-done | bytes 262176 | tf_op jit(solution)/shard_map/ppermute | solution.py:151
  31.6 0.0 collective-permute-done.9
  31.6 0.2 multiply_convert_fusion
  31.8 18.0 %all_to_all.10 = f16[8,64,256]{2,1,0:T(8,128)(2,1)S(1)} all-to-all(f16[8,64,256]{2,1,0:T(8,128)(2,1)S(1)} %bitcast.20), channel_id=1, replica_groups={{0,4,8,12,16,20,24,28},{1,5,9,13,17,21,25,29},{2,6,10,14,18,22,26,30},{..., dimensions={0} | all-to-all | bytes 524288 | tf_op jit(solution)/shard_map/all_to_all | solution.py:155
  49.9 12.0 %all_to_all.11 = bf16[8,64,256]{2,1,0:T(8,128)(2,1)S(1)} all-to-all(bf16[8,64,256]{2,1,0:T(8,128)(2,1)S(1)} %broadcast_in_dim.2), channel_id=1, replica_groups={{0,4,8,12,16,20,24,28},{1,5,9,13,17,21,25,29},{2,6,10,14,18,22,26,30},{..., dimensions={0} | all-to-all | bytes 524288 | tf_op jit(solution)/shard_map/all_to_all | solution.py:159
  61.9 1.4 %collective-permute-start.10 = (bf16[2,256,256]{2,1,0:T(8,128)(2,1)S(1)}, bf16[2,256,256]{2,1,0:T(8,128)(2,1)S(1)}, u32[]{:S(2)}, u32[]{:S(2)}) collective-permute-start(bf16[2,256,256]{2,1,0:T(8,128)(2,1)S(1)} %bitcast.16), channel_id=1, source_target_pairs={{0,1},{1,2},{2,3},{3,0},{4,5},{5,6},{6,7},{7,4},{8,9},{9,10},{10,1... | collective-permute-start | bytes 786440 | tf_op jit(solution)/shard_map/ppermute | solution.py:161
  63.3 2.2 %collective-permute-start.11 = (bf16[2,256,256]{2,1,0:T(8,128)(2,1)S(1)}, bf16[2,256,256]{2,1,0:T(8,128)(2,1)S(1)}, u32[]{:S(2)}, u32[]{:S(2)}) collective-permute-start(bf16[2,256,256]{2,1,0:T(8,128)(2,1)S(1)} %bitcast.17), channel_id=1, source_target_pairs={{0,2},{1,3},{2,0},{3,1},{4,6},{5,7},{6,4},{7,5},{8,10},{9,11},{10,... | collective-permute-start | bytes 786440 | tf_op jit(solution)/shard_map/ppermute | solution.py:161
  65.5 1.5 %collective-permute-start.12 = (bf16[2,256,256]{2,1,0:T(8,128)(2,1)S(1)}, bf16[2,256,256]{2,1,0:T(8,128)(2,1)S(1)}, u32[]{:S(2)}, u32[]{:S(2)}) collective-permute-start(bf16[2,256,256]{2,1,0:T(8,128)(2,1)S(1)} %bitcast.18), channel_id=1, source_target_pairs={{0,3},{1,0},{2,1},{3,2},{4,7},{5,4},{6,5},{7,6},{8,11},{9,8},{10,9... | collective-permute-start | bytes 786440 | tf_op jit(solution)/shard_map/ppermute | solution.py:161
  67.0 1.3 %collective-permute-done.10.refs_1_ = bf16[2,256,256]{2,1,0:T(8,128)(2,1)S(1)} collective-permute-done((bf16[2,256,256]{2,1,0:T(8,128)(2,1)S(1)}, bf16[2,256,256]{2,1,0:T(8,128)(2,1)S(1)}, u32[]{:S(2)}, u32[]{:S(2)}) %collective-permute-start.10) | collective-permute-done | bytes 262176 | tf_op jit(solution)/shard_map/ppermute | solution.py:161
  68.3 5.3 %collective-permute-done.11.refs_2_ = bf16[2,256,256]{2,1,0:T(8,128)(2,1)S(1)} collective-permute-done((bf16[2,256,256]{2,1,0:T(8,128)(2,1)S(1)}, bf16[2,256,256]{2,1,0:T(8,128)(2,1)S(1)}, u32[]{:S(2)}, u32[]{:S(2)}) %collective-permute-start.11) | collective-permute-done | bytes 262176 | tf_op jit(solution)/shard_map/ppermute | solution.py:161
  73.6 0.0 collective-permute-done.12.refs_3_
  73.6 1.4 %shard_map.57 = (f32[4,256,256]{2,1,0:T(8,128)S(1)}, bf16[4,256,256]{2,1,0:T(8,128)(2,1)S(1)}) custom-call(s32[24]{0:T(128)S(1)} %add_bitcast_fusion.table, s32[1,1]{1,0:T(1,128)S(6)} %copy.6.count, bf16[1,1,24,256,256]{4,3,2,1,0:T(8,128)(2,1)S(1)} %get-tuple-element.18.blocks, bf16[2,256,256]{2,1,0:T(8,128)(2,1)S(1)} %bitcast.19, ...), custom_call_target="tpu_custom_call" | custom-call | flops 805306368 | bytes 1048576 | tf_op jit(solution)/shard_map/pallas_call | solution.py:124
  75.0 4.8 %collective-permute-start.13 = (bf16[4,256,256]{2,1,0:T(8,128)(2,1)S(1)}, bf16[4,256,256]{2,1,0:T(8,128)(2,1)S(1)}, u32[]{:S(2)}, u32[]{:S(2)}) collective-permute-start(bf16[4,256,256]{2,1,0:T(8,128)(2,1)S(1)} %get-tuple-element.26), channel_id=1, source_target_pairs={{0,32},{32,0},{64,96},{96,64},{128,160},{160,128},{192,224},{224,1... | collective-permute-start | bytes 1572872 | tf_op jit(solution)/shard_map/ppermute | solution.py:169
  79.9 1.5 %collective-permute-done.13 = bf16[4,256,256]{2,1,0:T(8,128)(2,1)S(1)} collective-permute-done((bf16[4,256,256]{2,1,0:T(8,128)(2,1)S(1)}, bf16[4,256,256]{2,1,0:T(8,128)(2,1)S(1)}, u32[]{:S(2)}, u32[]{:S(2)}) %collective-permute-start.13) | collective-permute-done | bytes 524320 | tf_op jit(solution)/shard_map/ppermute | solution.py:169
  81.4 0.1 convert_add_fusion
  81.5 0.1 fusion.2
  81.6 1.0 %collective-permute-start.14 = (bf16[256,256]{1,0:T(8,128)(2,1)S(1)}, bf16[256,256]{1,0:T(8,128)(2,1)S(1)}, u32[]{:S(2)}, u32[]{:S(2)}) collective-permute-start(bf16[256,256]{1,0:T(8,128)(2,1)S(1)} %get-tuple-element.27), channel_id=1, source_target_pairs={{0,64},{32,96},{64,128},{96,160},{128,192},{160,224},{192,0},{224,... | collective-permute-start | bytes 393224 | tf_op jit(solution)/shard_map/ppermute | solution.py:172
  82.6 2.3 %collective-permute-start.15 = (bf16[256,256]{1,0:T(8,128)(2,1)S(1)}, bf16[256,256]{1,0:T(8,128)(2,1)S(1)}, u32[]{:S(2)}, u32[]{:S(2)}) collective-permute-start(bf16[256,256]{1,0:T(8,128)(2,1)S(1)} %get-tuple-element.29), channel_id=1, source_target_pairs={{0,128},{32,160},{64,192},{96,224},{128,0},{160,32},{192,64},{224,... | collective-permute-start | bytes 393224 | tf_op jit(solution)/shard_map/ppermute | solution.py:172
  85.0 1.0 %collective-permute-start.16 = (bf16[256,256]{1,0:T(8,128)(2,1)S(1)}, bf16[256,256]{1,0:T(8,128)(2,1)S(1)}, u32[]{:S(2)}, u32[]{:S(2)}) collective-permute-start(bf16[256,256]{1,0:T(8,128)(2,1)S(1)} %get-tuple-element.28), channel_id=1, source_target_pairs={{0,192},{32,224},{64,0},{96,32},{128,64},{160,96},{192,128},{224,1... | collective-permute-start | bytes 393224 | tf_op jit(solution)/shard_map/ppermute | solution.py:172
  85.9 1.7 %collective-permute-done.14 = bf16[256,256]{1,0:T(8,128)(2,1)S(1)} collective-permute-done((bf16[256,256]{1,0:T(8,128)(2,1)S(1)}, bf16[256,256]{1,0:T(8,128)(2,1)S(1)}, u32[]{:S(2)}, u32[]{:S(2)}) %collective-permute-start.14) | collective-permute-done | bytes 131104 | tf_op jit(solution)/shard_map/ppermute | solution.py:172
  87.6 3.4 %collective-permute-done.15 = bf16[256,256]{1,0:T(8,128)(2,1)S(1)} collective-permute-done((bf16[256,256]{1,0:T(8,128)(2,1)S(1)}, bf16[256,256]{1,0:T(8,128)(2,1)S(1)}, u32[]{:S(2)}, u32[]{:S(2)}) %collective-permute-start.15) | collective-permute-done | bytes 131104 | tf_op jit(solution)/shard_map/ppermute | solution.py:172
  91.0 0.0 collective-permute-done.16
  91.0 0.8 fusion.1
  (7 shorter events, 0.2 us)
Async XLA Ops:
  0.0 11.2 %collective-permute-start = (bf16[256,256]{1,0:T(8,128)(2,1)}, bf16[256,256]{1,0:T(8,128)(2,1)S(1)}, u32[]{:S(2)}, u32[]{:S(2)}) collective-permute-start(bf16[256,256]{1,0:T(8,128)(2,1)} %basis.1), channel_id=1, source_target_pairs={{0,64},{32,96},{64,128},{96,160},{128,192},{160,224},{192,0},{224,... | collective-permute-start | bytes 393224 | tf_op jit(solution)/shard_map/ppermute | solution.py:140
  2.1 10.3 %collective-permute-start.1 = (bf16[256,256]{1,0:T(8,128)(2,1)}, bf16[256,256]{1,0:T(8,128)(2,1)S(1)}, u32[]{:S(2)}, u32[]{:S(2)}) collective-permute-start(bf16[256,256]{1,0:T(8,128)(2,1)} %basis.1), channel_id=1, source_target_pairs={{0,128},{32,160},{64,192},{96,224},{128,0},{160,32},{192,64},{224,... | collective-permute-start | bytes 393224 | tf_op jit(solution)/shard_map/ppermute | solution.py:140
  4.7 7.7 %collective-permute-start.2 = (bf16[256,256]{1,0:T(8,128)(2,1)}, bf16[256,256]{1,0:T(8,128)(2,1)S(1)}, u32[]{:S(2)}, u32[]{:S(2)}) collective-permute-start(bf16[256,256]{1,0:T(8,128)(2,1)} %basis.1), channel_id=1, source_target_pairs={{0,192},{32,224},{64,0},{96,32},{128,64},{160,96},{192,128},{224,1... | collective-permute-start | bytes 393224 | tf_op jit(solution)/shard_map/ppermute | solution.py:140
  5.8 7.2 %collective-permute-start.3 = (bf16[256,256]{1,0:T(8,128)(2,1)}, bf16[256,256]{1,0:T(8,128)(2,1)S(1)}, u32[]{:S(2)}, u32[]{:S(2)}) collective-permute-start(bf16[256,256]{1,0:T(8,128)(2,1)} %basis.1), channel_id=1, source_target_pairs={{0,32},{32,0},{64,96},{96,64},{128,160},{160,128},{192,224},{224,1... | collective-permute-start | bytes 393224 | tf_op jit(solution)/shard_map/ppermute | solution.py:143
  7.3 1.9 %copy-start = (bf16[1,1,24,256,256]{4,3,2,1,0:T(8,128)(2,1)S(1)}, bf16[1,1,24,256,256]{4,3,2,1,0:T(8,128)(2,1)}, u32[]{:S(2)}) copy-start(bf16[1,1,24,256,256]{4,3,2,1,0:T(8,128)(2,1)} %blocks.1) | copy-start | bytes 9437188
  9.2 0.9 copy-start.1
  10.1 2.8 %copy-start.2 = (s32[1,1,24]{2,1,0:T(1,128)S(1)}, s32[1,1,24]{2,1,0:T(1,128)}, u32[]{:S(2)}) copy-start(s32[1,1,24]{2,1,0:T(1,128)} %param.7) | copy-start | bytes 292
  10.1 2.8 %copy-start.3 = (s32[1,1,24]{2,1,0:T(1,128)S(1)}, s32[1,1,24]{2,1,0:T(1,128)}, u32[]{:S(2)}) copy-start(s32[1,1,24]{2,1,0:T(1,128)} %param.6) | copy-start | bytes 292
  11.2 2.2 %collective-permute-start.4 = (bf16[256,256]{1,0:T(8,128)(2,1)S(1)}, bf16[256,256]{1,0:T(8,128)(2,1)S(1)}, u32[]{:S(2)}, u32[]{:S(2)}) collective-permute-start(bf16[256,256]{1,0:T(8,128)(2,1)S(1)} %collective-permute-done.refs_1_), channel_id=1, source_target_pairs={{0,32},{32,0},{64,96},{96,64},{128,160},{160,128},{192,224},{224,1... | collective-permute-start | bytes 393224 | tf_op jit(solution)/shard_map/ppermute | solution.py:143
  12.4 1.3 %collective-permute-start.5 = (bf16[256,256]{1,0:T(8,128)(2,1)S(1)}, bf16[256,256]{1,0:T(8,128)(2,1)S(1)}, u32[]{:S(2)}, u32[]{:S(2)}) collective-permute-start(bf16[256,256]{1,0:T(8,128)(2,1)S(1)} %collective-permute-done.1.refs_2_), channel_id=1, source_target_pairs={{0,32},{32,0},{64,96},{96,64},{128,160},{160,128},{192,224},{224,1... | collective-permute-start | bytes 393224 | tf_op jit(solution)/shard_map/ppermute | solution.py:143
  12.5 1.5 %collective-permute-start.6 = (bf16[256,256]{1,0:T(8,128)(2,1)S(1)}, bf16[256,256]{1,0:T(8,128)(2,1)S(1)}, u32[]{:S(2)}, u32[]{:S(2)}) collective-permute-start(bf16[256,256]{1,0:T(8,128)(2,1)S(1)} %collective-permute-done.2.refs_3_), channel_id=1, source_target_pairs={{0,32},{32,0},{64,96},{96,64},{128,160},{160,128},{192,224},{224,1... | collective-permute-start | bytes 393224 | tf_op jit(solution)/shard_map/ppermute | solution.py:143
  15.4 8.9 %collective-permute-start.7 = (f16[2,256,256]{2,1,0:T(8,128)(2,1)S(1)}, f16[2,256,256]{2,1,0:T(8,128)(2,1)S(1)}, u32[]{:S(2)}, u32[]{:S(2)}) collective-permute-start(f16[2,256,256]{2,1,0:T(8,128)(2,1)S(1)} %convert_element_type.61), channel_id=1, source_target_pairs={{0,1},{1,2},{2,3},{3,0},{4,5},{5,6},{6,7},{7,4},{8,9},{9,10},{10,1... | collective-permute-start | bytes 786440 | tf_op jit(solution)/shard_map/ppermute | solution.py:151
  16.4 15.3 %collective-permute-start.8 = (f16[2,256,256]{2,1,0:T(8,128)(2,1)S(1)}, f16[2,256,256]{2,1,0:T(8,128)(2,1)S(1)}, u32[]{:S(2)}, u32[]{:S(2)}) collective-permute-start(f16[2,256,256]{2,1,0:T(8,128)(2,1)S(1)} %convert_element_type.63), channel_id=1, source_target_pairs={{0,2},{1,3},{2,0},{3,1},{4,6},{5,7},{6,4},{7,5},{8,10},{9,11},{10,... | collective-permute-start | bytes 786440 | tf_op jit(solution)/shard_map/ppermute | solution.py:151
  19.4 12.2 %collective-permute-start.9 = (f16[2,256,256]{2,1,0:T(8,128)(2,1)S(1)}, f16[2,256,256]{2,1,0:T(8,128)(2,1)S(1)}, u32[]{:S(2)}, u32[]{:S(2)}) collective-permute-start(f16[2,256,256]{2,1,0:T(8,128)(2,1)S(1)} %convert_element_type.65), channel_id=1, source_target_pairs={{0,3},{1,0},{2,1},{3,2},{4,7},{5,4},{6,5},{7,6},{8,11},{9,8},{10,9... | collective-permute-start | bytes 786440 | tf_op jit(solution)/shard_map/ppermute | solution.py:151
  61.9 6.4 %collective-permute-start.10 = (bf16[2,256,256]{2,1,0:T(8,128)(2,1)S(1)}, bf16[2,256,256]{2,1,0:T(8,128)(2,1)S(1)}, u32[]{:S(2)}, u32[]{:S(2)}) collective-permute-start(bf16[2,256,256]{2,1,0:T(8,128)(2,1)S(1)} %bitcast.16), channel_id=1, source_target_pairs={{0,1},{1,2},{2,3},{3,0},{4,5},{5,6},{6,7},{7,4},{8,9},{9,10},{10,1... | collective-permute-start | bytes 786440 | tf_op jit(solution)/shard_map/ppermute | solution.py:161
  63.3 10.3 %collective-permute-start.11 = (bf16[2,256,256]{2,1,0:T(8,128)(2,1)S(1)}, bf16[2,256,256]{2,1,0:T(8,128)(2,1)S(1)}, u32[]{:S(2)}, u32[]{:S(2)}) collective-permute-start(bf16[2,256,256]{2,1,0:T(8,128)(2,1)S(1)} %bitcast.17), channel_id=1, source_target_pairs={{0,2},{1,3},{2,0},{3,1},{4,6},{5,7},{6,4},{7,5},{8,10},{9,11},{10,... | collective-permute-start | bytes 786440 | tf_op jit(solution)/shard_map/ppermute | solution.py:161
  65.5 8.1 %collective-permute-start.12 = (bf16[2,256,256]{2,1,0:T(8,128)(2,1)S(1)}, bf16[2,256,256]{2,1,0:T(8,128)(2,1)S(1)}, u32[]{:S(2)}, u32[]{:S(2)}) collective-permute-start(bf16[2,256,256]{2,1,0:T(8,128)(2,1)S(1)} %bitcast.18), channel_id=1, source_target_pairs={{0,3},{1,0},{2,1},{3,2},{4,7},{5,4},{6,5},{7,6},{8,11},{9,8},{10,9... | collective-permute-start | bytes 786440 | tf_op jit(solution)/shard_map/ppermute | solution.py:161
  75.0 6.4 %collective-permute-start.13 = (bf16[4,256,256]{2,1,0:T(8,128)(2,1)S(1)}, bf16[4,256,256]{2,1,0:T(8,128)(2,1)S(1)}, u32[]{:S(2)}, u32[]{:S(2)}) collective-permute-start(bf16[4,256,256]{2,1,0:T(8,128)(2,1)S(1)} %get-tuple-element.26), channel_id=1, source_target_pairs={{0,32},{32,0},{64,96},{96,64},{128,160},{160,128},{192,224},{224,1... | collective-permute-start | bytes 1572872 | tf_op jit(solution)/shard_map/ppermute | solution.py:169
  81.6 6.0 %collective-permute-start.14 = (bf16[256,256]{1,0:T(8,128)(2,1)S(1)}, bf16[256,256]{1,0:T(8,128)(2,1)S(1)}, u32[]{:S(2)}, u32[]{:S(2)}) collective-permute-start(bf16[256,256]{1,0:T(8,128)(2,1)S(1)} %get-tuple-element.27), channel_id=1, source_target_pairs={{0,64},{32,96},{64,128},{96,160},{128,192},{160,224},{192,0},{224,... | collective-permute-start | bytes 393224 | tf_op jit(solution)/shard_map/ppermute | solution.py:172
  82.6 8.4 %collective-permute-start.15 = (bf16[256,256]{1,0:T(8,128)(2,1)S(1)}, bf16[256,256]{1,0:T(8,128)(2,1)S(1)}, u32[]{:S(2)}, u32[]{:S(2)}) collective-permute-start(bf16[256,256]{1,0:T(8,128)(2,1)S(1)} %get-tuple-element.29), channel_id=1, source_target_pairs={{0,128},{32,160},{64,192},{96,224},{128,0},{160,32},{192,64},{224,... | collective-permute-start | bytes 393224 | tf_op jit(solution)/shard_map/ppermute | solution.py:172
  85.0 6.1 %collective-permute-start.16 = (bf16[256,256]{1,0:T(8,128)(2,1)S(1)}, bf16[256,256]{1,0:T(8,128)(2,1)S(1)}, u32[]{:S(2)}, u32[]{:S(2)}) collective-permute-start(bf16[256,256]{1,0:T(8,128)(2,1)S(1)} %get-tuple-element.28), channel_id=1, source_target_pairs={{0,192},{32,224},{64,0},{96,32},{128,64},{160,96},{192,128},{224,1... | collective-permute-start | bytes 393224 | tf_op jit(solution)/shard_map/ppermute | solution.py:172

commit v4 on v3

--- a/solution.py
+++ b/solution.py
@@ -1,5 +1,3 @@
-import functools
-
 import jax
 import jax.numpy as jnp
 from jax import lax
@@ -13,6 +11,7 @@
 CORES = 2
 NX = 4
 UNROLL = 8
+SHIFTS_A, SHIFTS_B, SHIFTS_C, SHIFTS_D = (1, 3, 2), (1, 3, 2), (1, 3, 2), (1, 3, 2)
 SCALE_X = 64.0
 SCALE_Z = 16.0
 
@@ -32,6 +31,14 @@
 
 def z_groups(count):
     return [[z * NX + x for z in range(count // NX)] for x in range(NX)]
+
+
+def x_groups(count):
+    return [[z * NX + x for x in range(NX)] for z in range(count // NX)]
+
+
+def y_groups(count):
+    return [[y * CORES + k for y in range(count // CORES)] for k in range(CORES)]
 
 
 def vmem(n):
@@ -62,7 +69,7 @@
         scratch_shapes=[pltpu.SemaphoreType.DMA((2,))],
         compiler_params=pltpu.CompilerParams(vmem_limit_bytes=16 << 20),
         cost_estimate=pl.CostEstimate(flops=0, bytes_accessed=8 << 20, transcendentals=0),
-    )(blocks, basis)
+    )(pltpu.with_memory_space_constraint(blocks, pltpu.HBM), pltpu.with_memory_space_constraint(basis, pltpu.HBM))
 
 
 def add_products(table, count, blocks, basis, acc, transposed):
@@ -92,27 +99,27 @@
     pieces, (own, *sends), (basis, acc) = refs[:8], refs[8:12], refs[12:]
     y, k = lax.axis_index("row") // CORES, lax.axis_index("row") % CORES
     x = lax.axis_index("col") % NX
-    for d in range(4):
+    for i, d in enumerate((0,) + SHIFTS_A):
         at = (y + 4 - d) % 4
-        basis[at * CORES + k] = pieces[d][...]
-        basis[at * CORES + 1 - k] = pieces[4 + d][...]
+        basis[at * CORES + k] = pieces[i][...]
+        basis[at * CORES + 1 - k] = pieces[4 + i][...]
     add_products(table, count, blocks, basis, acc, False)
     for h in range(2):
         own[h] = acc[x * 2 + h]
-    for d in range(1, 4):
+    for send, d in zip(sends, SHIFTS_B):
         to = (x + d) % NX
         for h in range(2):
-            sends[d - 1][h] = acc[to * 2 + h] * SCALE_X
+            send[h] = acc[to * 2 + h] * SCALE_X
 
 
 def backward_kernel(table, count, blocks, *refs):
     pieces, (own, send), (basis, acc) = refs[:4], refs[4:6], refs[6:]
     k = lax.axis_index("row") % CORES
     x = lax.axis_index("col") % NX
-    for d in range(4):
+    for i, d in enumerate((0,) + SHIFTS_C):
         at = (x + 4 - d) % 4
         for h in range(2):
-            basis[at * 2 + h] = pieces[d][h]
+            basis[at * 2 + h] = pieces[i][h]
     add_products(table, count, blocks, basis, acc, True)
     for y in range(4):
         own[y] = acc[y * CORES + k]
@@ -137,7 +144,7 @@
     size, rank = basis.shape
     table = (block_rows[0, 0] * 8 + block_cols[0, 0], block_count)
 
-    mine = [basis] + [lax.ppermute(basis, "row", shift_y(n_row, d)) for d in (1, 2, 3)]
+    mine = [basis] + [lax.ppermute(basis, "row", shift_y(n_row, d)) for d in SHIFTS_A]
     blocks, own = fetch(block_values, basis)
     mine[1], blocks, own = lax.optimization_barrier((mine[1], blocks, own))
     other = [lax.ppermute(p, "row", swap_core(n_row)) for p in mine]
@@ -148,7 +155,7 @@
         9,
         *table, blocks, own, *mine[1:], *other,
     )
-    got = [lax.ppermute(s.astype(F16), "col", shift_x(n_col, d)) for d, s in zip((1, 2, 3), sends)]
+    got = [lax.ppermute(s.astype(F16), "col", shift_x(n_col, d)) for d, s in zip(SHIFTS_B, sends)]
     x_sum = own + (got[0].astype(F32) + got[1].astype(F32) + got[2].astype(F32)) * (1 / SCALE_X)
     nz = n_col // NX
     parts = (x_sum * SCALE_Z).astype(F16).reshape(nz, 2 * size // nz, rank)
@@ -158,7 +165,7 @@
     copies = jnp.broadcast_to(share[None], (nz, *share.shape))
     chunk = lax.all_to_all(copies, "col", 0, 0, tiled=True, axis_index_groups=z_groups(n_col))
     chunk = chunk.reshape(2, size, rank)
-    chunks = [chunk] + [lax.ppermute(chunk, "col", shift_x(n_col, d)) for d in (1, 2, 3)]
+    chunks = [chunk] + [lax.ppermute(chunk, "col", shift_x(n_col, d)) for d in SHIFTS_C]
     own, send = call(
         backward_kernel,
         [jax.ShapeDtypeStruct((4, size, rank), F32), jax.ShapeDtypeStruct((4, size, rank), BF16)],
@@ -169,7 +176,7 @@
     pair = own + lax.ppermute(send, "row", swap_core(n_row)).astype(F32)
     y = lax.axis_index("row") // CORES
     pick = lambda d: lax.dynamic_index_in_dim(pair, (y + d) % 4, 0, keepdims=False)
-    got = [lax.ppermute(pick(d).astype(BF16), "row", shift_y(n_row, d)) for d in (1, 2, 3)]
+    got = [lax.ppermute(pick(d).astype(BF16), "row", shift_y(n_row, d)) for d in SHIFTS_D]
     return pick(0) + got[0].astype(F32) + got[1].astype(F32) + got[2].astype(F32)
 
 

time: 92.5 us -> 91.5 us (0.989); the launches traced: 91.8 us -> 91.8 us
  waiting for transfers between devices: 25.2 us -> 28.3 us
  local copies, waits for them, and re-layouts: 2.87 us -> 0.08 us
  Pallas kernels: 3.21 us -> 5.73 us
  starting transfers between devices: 28.5 us -> 26.7 us
    unnamed x8 -> x4, local copies, waits for them, and re-layouts: 2.8 us -> 0.01 us
    ppermute x4, starting transfers between devices: 3.27 us -> 5.37 us  [body(): other = [lax.ppermute(p, 'row', swap_core(n_row)) for p in mine]]
    ppermute x3, waiting for transfers between devices: 6.59 us -> 8.38 us  [body(): lax.ppermute(chunk, 'col', shift_x(n_col, d))]
    ppermute x3, starting transfers between devices: 5.14 us -> 3.5 us  [body(): lax.ppermute(s.astype(F16), 'col', shift_x(n_col, d))]
    pallas_call x1, Pallas kernels: 0.39 us -> 1.91 us  [fetch(): pl.pallas_call(fetch_kernel, out_shape=[jax.ShapeDtypeStruct(blocks.shape...]
    pallas_call x2, Pallas kernels: 2.81 us -> 3.82 us  [call(): pl.pallas_call(kernel, out_shape=outs, in_specs=smem(2) + vmem(n_vmem), o...]
    ppermute x3, waiting for transfers between devices: 5.09 us -> 6.05 us  [body(): lax.ppermute(pick(d).astype(BF16), 'row', shift_y(n_row, d))]
    ppermute x3, starting transfers between devices: 5.14 us -> 4.2 us  [body(): lax.ppermute(chunk, 'col', shift_x(n_col, d))]
  transfers between devices with their start and end apart: 17 -> 17, of which waited for: 10 -> 9; matrix products, arithmetic and copies ran while one was open for 0% -> 0% of each run, Pallas kernels for 0% -> 2%
where the time goes in v4:
time: 91.5 us; the launch traced here: 91.8 us
  blocking collectives  29.1 us (32%)
  waiting for transfers between devices  28.3 us (31%)
  starting transfers between devices  26.7 us (29%)
  Pallas kernels  5.73 us (6%)
  other arithmetic  1.23 us (1%)
    all_to_all x1, blocking collectives, body(): lax.all_to_all(parts, 'col', 0, 0, tiled=True, axis_index_groups=z_groups...  17.2 us
    all_to_all x1, blocking collectives, body(): lax.all_to_all(copies, 'col', 0, 0, tiled=True, axis_index_groups=z_group...  11.9 us
    ppermute x3, waiting for transfers between devices, body(): lax.ppermute(s.astype(F16), 'col', shift_x(n_col, d))  11.4 us
    ppermute x3, waiting for transfers between devices, body(): lax.ppermute(chunk, 'col', shift_x(n_col, d))  8.38 us
    ppermute x3, waiting for transfers between devices, body(): lax.ppermute(pick(d).astype(BF16), 'row', shift_y(n_row, d))  6.05 us
    ppermute x4, starting transfers between devices, body(): other = [lax.ppermute(p, 'row', swap_core(n_row)) for p in mine]  5.37 us
    ppermute x3, starting transfers between devices, body(): lax.ppermute(basis, 'row', shift_y(n_row, d))  5.21 us
    ppermute x1, starting transfers between devices, body(): pair = own + lax.ppermute(send, 'row', swap_core(n_row)).astype(F32)  4.61 us
  transfers between devices with their start and end apart: 17, of which 9 were waited for; matrix products, arithmetic and copies ran while one was open for 0% of the time, Pallas kernels for 2%

profile of v4, /device:TPU:1, one launch (start us, length us, event | category | flops | bytes accessed | tf_op | source)
XLA Modules:
  0.0 91.8 jit_solution(1619666394536314922)
XLA Ops:
  0.0 0.0 copy-start.1
  0.0 0.0 copy-start
  0.0 2.1 %collective-permute-start = (bf16[256,256]{1,0:T(8,128)(2,1)}, bf16[256,256]{1,0:T(8,128)(2,1)S(1)}, u32[]{:S(2)}, u32[]{:S(2)}) collective-permute-start(bf16[256,256]{1,0:T(8,128)(2,1)} %basis.1), channel_id=1, source_target_pairs={{0,64},{32,96},{64,128},{96,160},{128,192},{160,224},{192,0},{224,... | collective-permute-start | bytes 393224 | tf_op jit(solution)/shard_map/ppermute | solution.py:147
  2.1 1.5 %collective-permute-start.1 = (bf16[256,256]{1,0:T(8,128)(2,1)}, bf16[256,256]{1,0:T(8,128)(2,1)S(1)}, u32[]{:S(2)}, u32[]{:S(2)}) collective-permute-start(bf16[256,256]{1,0:T(8,128)(2,1)} %basis.1), channel_id=1, source_target_pairs={{0,192},{32,224},{64,0},{96,32},{128,64},{160,96},{192,128},{224,1... | collective-permute-start | bytes 393224 | tf_op jit(solution)/shard_map/ppermute | solution.py:147
  3.7 1.6 %collective-permute-start.2 = (bf16[256,256]{1,0:T(8,128)(2,1)}, bf16[256,256]{1,0:T(8,128)(2,1)S(1)}, u32[]{:S(2)}, u32[]{:S(2)}) collective-permute-start(bf16[256,256]{1,0:T(8,128)(2,1)} %basis.1), channel_id=1, source_target_pairs={{0,128},{32,160},{64,192},{96,224},{128,0},{160,32},{192,64},{224,... | collective-permute-start | bytes 393224 | tf_op jit(solution)/shard_map/ppermute | solution.py:147
  5.2 1.5 %collective-permute-start.3 = (bf16[256,256]{1,0:T(8,128)(2,1)}, bf16[256,256]{1,0:T(8,128)(2,1)S(1)}, u32[]{:S(2)}, u32[]{:S(2)}) collective-permute-start(bf16[256,256]{1,0:T(8,128)(2,1)} %basis.1), channel_id=1, source_target_pairs={{0,32},{32,0},{64,96},{96,64},{128,160},{160,128},{192,224},{224,1... | collective-permute-start | bytes 393224 | tf_op jit(solution)/shard_map/ppermute | solution.py:150
  6.7 1.9 %shard_map.55 = (bf16[1,1,24,256,256]{4,3,2,1,0:T(8,128)(2,1)S(1)}, bf16[256,256]{1,0:T(8,128)(2,1)S(1)}) custom-call(bf16[1,1,24,256,256]{4,3,2,1,0:T(8,128)(2,1)} %blocks.1, bf16[256,256]{1,0:T(8,128)(2,1)} %basis.1), custom_call_target="tpu_custom_call" | custom-call | bytes 8388608 | tf_op jit(solution)/shard_map/pallas_call | solution.py:64
  9.3 0.0 collective-permute-done.refs_1_
  9.3 1.7 %collective-permute-start.4 = (bf16[256,256]{1,0:T(8,128)(2,1)S(1)}, bf16[256,256]{1,0:T(8,128)(2,1)S(1)}, u32[]{:S(2)}, u32[]{:S(2)}) collective-permute-start(bf16[256,256]{1,0:T(8,128)(2,1)S(1)} %collective-permute-done.refs_1_), channel_id=1, source_target_pairs={{0,32},{32,0},{64,96},{96,64},{128,160},{160,128},{192,224},{224,1... | collective-permute-start | bytes 393224 | tf_op jit(solution)/shard_map/ppermute | solution.py:150
  11.0 0.0 collective-permute-done.1.refs_2_
  11.0 0.4 collective-permute-start.5
  11.4 0.0 collective-permute-done.2.refs_3_
  11.4 1.7 %collective-permute-start.6 = (bf16[256,256]{1,0:T(8,128)(2,1)S(1)}, bf16[256,256]{1,0:T(8,128)(2,1)S(1)}, u32[]{:S(2)}, u32[]{:S(2)}) collective-permute-start(bf16[256,256]{1,0:T(8,128)(2,1)S(1)} %collective-permute-done.2.refs_3_), channel_id=1, source_target_pairs={{0,32},{32,0},{64,96},{96,64},{128,160},{160,128},{192,224},{224,1... | collective-permute-start | bytes 393224 | tf_op jit(solution)/shard_map/ppermute | solution.py:150
  13.2 0.0 copy-done.1
  13.2 0.0 copy-done
  13.2 0.0 collective-permute-done.3.refs_4_
  13.2 0.0 collective-permute-done.4.refs_5_
  13.2 0.0 collective-permute-done.5.refs_6_
  13.2 0.9 %collective-permute-done.6.refs_7_ = bf16[256,256]{1,0:T(8,128)(2,1)S(1)} collective-permute-done((bf16[256,256]{1,0:T(8,128)(2,1)S(1)}, bf16[256,256]{1,0:T(8,128)(2,1)S(1)}, u32[]{:S(2)}, u32[]{:S(2)}) %collective-permute-start.6) | collective-permute-done | bytes 131104 | tf_op jit(solution)/shard_map/ppermute | solution.py:150
  14.2 1.9 %shard_map.56 = (f32[2,256,256]{2,1,0:T(8,128)S(1)}, f32[2,256,256]{2,1,0:T(8,128)S(1)}, f32[2,256,256]{2,1,0:T(8,128)S(1)}, f32[2,256,256]{2,1,0:T(8,128)S(1)}) custom-call(s32[24]{0:T(128)S(1)} %add_bitcast_fusion.table, s32[1,1]{1,0:T(1,128)S(6)} %copy.6.count, bf16[1,1,24,256,256]{4,3,2,1,0:T(8,128)(2,1)S(1)} %get-tuple-element.18.blocks, ...), custom_call_target="tpu_custom_call" | custom-call | flops 805306368 | bytes 1048576 | tf_op jit(solution)/shard_map/pallas_call | solution.py:131
  16.1 0.3 collective-permute-start.7
  16.5 2.5 %collective-permute-start.8 = (f16[2,256,256]{2,1,0:T(8,128)(2,1)S(1)}, f16[2,256,256]{2,1,0:T(8,128)(2,1)S(1)}, u32[]{:S(2)}, u32[]{:S(2)}) collective-permute-start(f16[2,256,256]{2,1,0:T(8,128)(2,1)S(1)} %convert_element_type.63), channel_id=1, source_target_pairs={{0,3},{1,0},{2,1},{3,2},{4,7},{5,4},{6,5},{7,6},{8,11},{9,8},{10,9... | collective-permute-start | bytes 786440 | tf_op jit(solution)/shard_map/ppermute | solution.py:158
  19.0 0.7 collective-permute-start.9
  19.7 5.2 %collective-permute-done.7 = f16[2,256,256]{2,1,0:T(8,128)(2,1)S(1)} collective-permute-done((f16[2,256,256]{2,1,0:T(8,128)(2,1)S(1)}, f16[2,256,256]{2,1,0:T(8,128)(2,1)S(1)}, u32[]{:S(2)}, u32[]{:S(2)}) %collective-permute-start.7) | collective-permute-done | bytes 262176 | tf_op jit(solution)/shard_map/ppermute | solution.py:158
  24.9 0.0 collective-permute-done.8
  24.9 6.1 %collective-permute-done.9 = f16[2,256,256]{2,1,0:T(8,128)(2,1)S(1)} collective-permute-done((f16[2,256,256]{2,1,0:T(8,128)(2,1)S(1)}, f16[2,256,256]{2,1,0:T(8,128)(2,1)S(1)}, u32[]{:S(2)}, u32[]{:S(2)}) %collective-permute-start.9) | collective-permute-done | bytes 262176 | tf_op jit(solution)/shard_map/ppermute | solution.py:158
  31.1 0.2 multiply_convert_fusion
  31.3 17.2 %all_to_all.10 = f16[8,64,256]{2,1,0:T(8,128)(2,1)S(1)} all-to-all(f16[8,64,256]{2,1,0:T(8,128)(2,1)S(1)} %bitcast.20), channel_id=1, replica_groups={{0,4,8,12,16,20,24,28},{1,5,9,13,17,21,25,29},{2,6,10,14,18,22,26,30},{..., dimensions={0} | all-to-all | bytes 524288 | tf_op jit(solution)/shard_map/all_to_all | solution.py:162
  48.5 11.9 %all_to_all.11 = bf16[8,64,256]{2,1,0:T(8,128)(2,1)S(1)} all-to-all(bf16[8,64,256]{2,1,0:T(8,128)(2,1)S(1)} %broadcast_in_dim.2), channel_id=1, replica_groups={{0,4,8,12,16,20,24,28},{1,5,9,13,17,21,25,29},{2,6,10,14,18,22,26,30},{..., dimensions={0} | all-to-all | bytes 524288 | tf_op jit(solution)/shard_map/all_to_all | solution.py:166
  60.4 0.4 collective-permute-start.10
  60.9 2.6 %collective-permute-start.11 = (bf16[2,256,256]{2,1,0:T(8,128)(2,1)S(1)}, bf16[2,256,256]{2,1,0:T(8,128)(2,1)S(1)}, u32[]{:S(2)}, u32[]{:S(2)}) collective-permute-start(bf16[2,256,256]{2,1,0:T(8,128)(2,1)S(1)} %bitcast.17), channel_id=1, source_target_pairs={{0,3},{1,0},{2,1},{3,2},{4,7},{5,4},{6,5},{7,6},{8,11},{9,8},{10,9... | collective-permute-start | bytes 786440 | tf_op jit(solution)/shard_map/ppermute | solution.py:168
  63.4 1.2 %collective-permute-start.12 = (bf16[2,256,256]{2,1,0:T(8,128)(2,1)S(1)}, bf16[2,256,256]{2,1,0:T(8,128)(2,1)S(1)}, u32[]{:S(2)}, u32[]{:S(2)}) collective-permute-start(bf16[2,256,256]{2,1,0:T(8,128)(2,1)S(1)} %bitcast.18), channel_id=1, source_target_pairs={{0,2},{1,3},{2,0},{3,1},{4,6},{5,7},{6,4},{7,5},{8,10},{9,11},{10,... | collective-permute-start | bytes 786440 | tf_op jit(solution)/shard_map/ppermute | solution.py:168
  64.6 2.6 %collective-permute-done.10.refs_1_ = bf16[2,256,256]{2,1,0:T(8,128)(2,1)S(1)} collective-permute-done((bf16[2,256,256]{2,1,0:T(8,128)(2,1)S(1)}, bf16[2,256,256]{2,1,0:T(8,128)(2,1)S(1)}, u32[]{:S(2)}, u32[]{:S(2)}) %collective-permute-start.10) | collective-permute-done | bytes 262176 | tf_op jit(solution)/shard_map/ppermute | solution.py:168
  67.2 2.7 %collective-permute-done.11.refs_2_ = bf16[2,256,256]{2,1,0:T(8,128)(2,1)S(1)} collective-permute-done((bf16[2,256,256]{2,1,0:T(8,128)(2,1)S(1)}, bf16[2,256,256]{2,1,0:T(8,128)(2,1)S(1)}, u32[]{:S(2)}, u32[]{:S(2)}) %collective-permute-start.11) | collective-permute-done | bytes 262176 | tf_op jit(solution)/shard_map/ppermute | solution.py:168
  69.8 3.2 %collective-permute-done.12.refs_3_ = bf16[2,256,256]{2,1,0:T(8,128)(2,1)S(1)} collective-permute-done((bf16[2,256,256]{2,1,0:T(8,128)(2,1)S(1)}, bf16[2,256,256]{2,1,0:T(8,128)(2,1)S(1)}, u32[]{:S(2)}, u32[]{:S(2)}) %collective-permute-start.12) | collective-permute-done | bytes 262176 | tf_op jit(solution)/shard_map/ppermute | solution.py:168
  73.0 1.9 %shard_map.57 = (f32[4,256,256]{2,1,0:T(8,128)S(1)}, bf16[4,256,256]{2,1,0:T(8,128)(2,1)S(1)}) custom-call(s32[24]{0:T(128)S(1)} %add_bitcast_fusion.table, s32[1,1]{1,0:T(1,128)S(6)} %copy.6.count, bf16[1,1,24,256,256]{4,3,2,1,0:T(8,128)(2,1)S(1)} %get-tuple-element.18.blocks, bf16[2,256,256]{2,1,0:T(8,128)(2,1)S(1)} %bitcast.19, ...), custom_call_target="tpu_custom_call" | custom-call | flops 805306368 | bytes 1048576 | tf_op jit(solution)/shard_map/pallas_call | solution.py:131
  74.9 4.6 %collective-permute-start.13 = (bf16[4,256,256]{2,1,0:T(8,128)(2,1)S(1)}, bf16[4,256,256]{2,1,0:T(8,128)(2,1)S(1)}, u32[]{:S(2)}, u32[]{:S(2)}) collective-permute-start(bf16[4,256,256]{2,1,0:T(8,128)(2,1)S(1)} %get-tuple-element.26), channel_id=1, source_target_pairs={{0,32},{32,0},{64,96},{96,64},{128,160},{160,128},{192,224},{224,1... | collective-permute-start | bytes 1572872 | tf_op jit(solution)/shard_map/ppermute | solution.py:176
  79.5 1.5 %collective-permute-done.13 = bf16[4,256,256]{2,1,0:T(8,128)(2,1)S(1)} collective-permute-done((bf16[4,256,256]{2,1,0:T(8,128)(2,1)S(1)}, bf16[4,256,256]{2,1,0:T(8,128)(2,1)S(1)}, u32[]{:S(2)}, u32[]{:S(2)}) %collective-permute-start.13) | collective-permute-done | bytes 524320 | tf_op jit(solution)/shard_map/ppermute | solution.py:176
  81.1 0.1 convert_add_fusion
  81.2 0.1 fusion.2
  81.2 0.3 collective-permute-start.14
  81.6 2.4 %collective-permute-start.15 = (bf16[256,256]{1,0:T(8,128)(2,1)S(1)}, bf16[256,256]{1,0:T(8,128)(2,1)S(1)}, u32[]{:S(2)}, u32[]{:S(2)}) collective-permute-start(bf16[256,256]{1,0:T(8,128)(2,1)S(1)} %get-tuple-element.29), channel_id=1, source_target_pairs={{0,192},{32,224},{64,0},{96,32},{128,64},{160,96},{192,128},{224,1... | collective-permute-start | bytes 393224 | tf_op jit(solution)/shard_map/ppermute | solution.py:179
  84.0 1.0 %collective-permute-start.16 = (bf16[256,256]{1,0:T(8,128)(2,1)S(1)}, bf16[256,256]{1,0:T(8,128)(2,1)S(1)}, u32[]{:S(2)}, u32[]{:S(2)}) collective-permute-start(bf16[256,256]{1,0:T(8,128)(2,1)S(1)} %get-tuple-element.28), channel_id=1, source_target_pairs={{0,128},{32,160},{64,192},{96,224},{128,0},{160,32},{192,64},{224,... | collective-permute-start | bytes 393224 | tf_op jit(solution)/shard_map/ppermute | solution.py:179
  85.0 2.2 %collective-permute-done.14 = bf16[256,256]{1,0:T(8,128)(2,1)S(1)} collective-permute-done((bf16[256,256]{1,0:T(8,128)(2,1)S(1)}, bf16[256,256]{1,0:T(8,128)(2,1)S(1)}, u32[]{:S(2)}, u32[]{:S(2)}) %collective-permute-start.14) | collective-permute-done | bytes 131104 | tf_op jit(solution)/shard_map/ppermute | solution.py:179
  87.2 0.0 collective-permute-done.15
  87.3 3.8 %collective-permute-done.16 = bf16[256,256]{1,0:T(8,128)(2,1)S(1)} collective-permute-done((bf16[256,256]{1,0:T(8,128)(2,1)S(1)}, bf16[256,256]{1,0:T(8,128)(2,1)S(1)}, u32[]{:S(2)}, u32[]{:S(2)}) %collective-permute-start.16) | collective-permute-done | bytes 131104 | tf_op jit(solution)/shard_map/ppermute | solution.py:179
  91.1 0.8 fusion.1
  (7 shorter events, 0.2 us)
Async XLA Ops:
  0.0 13.2 %copy-start.1 = (s32[1,1,24]{2,1,0:T(1,128)S(1)}, s32[1,1,24]{2,1,0:T(1,128)}, u32[]{:S(2)}) copy-start(s32[1,1,24]{2,1,0:T(1,128)} %param.6) | copy-start | bytes 292
  0.0 13.2 %copy-start = (s32[1,1,24]{2,1,0:T(1,128)S(1)}, s32[1,1,24]{2,1,0:T(1,128)}, u32[]{:S(2)}) copy-start(s32[1,1,24]{2,1,0:T(1,128)} %param.7) | copy-start | bytes 292
  0.0 9.3 %collective-permute-start = (bf16[256,256]{1,0:T(8,128)(2,1)}, bf16[256,256]{1,0:T(8,128)(2,1)S(1)}, u32[]{:S(2)}, u32[]{:S(2)}) collective-permute-start(bf16[256,256]{1,0:T(8,128)(2,1)} %basis.1), channel_id=1, source_target_pairs={{0,64},{32,96},{64,128},{96,160},{128,192},{160,224},{192,0},{224,... | collective-permute-start | bytes 393224 | tf_op jit(solution)/shard_map/ppermute | solution.py:147
  2.1 8.9 %collective-permute-start.1 = (bf16[256,256]{1,0:T(8,128)(2,1)}, bf16[256,256]{1,0:T(8,128)(2,1)S(1)}, u32[]{:S(2)}, u32[]{:S(2)}) collective-permute-start(bf16[256,256]{1,0:T(8,128)(2,1)} %basis.1), channel_id=1, source_target_pairs={{0,192},{32,224},{64,0},{96,32},{128,64},{160,96},{192,128},{224,1... | collective-permute-start | bytes 393224 | tf_op jit(solution)/shard_map/ppermute | solution.py:147
  3.7 7.8 %collective-permute-start.2 = (bf16[256,256]{1,0:T(8,128)(2,1)}, bf16[256,256]{1,0:T(8,128)(2,1)S(1)}, u32[]{:S(2)}, u32[]{:S(2)}) collective-permute-start(bf16[256,256]{1,0:T(8,128)(2,1)} %basis.1), channel_id=1, source_target_pairs={{0,128},{32,160},{64,192},{96,224},{128,0},{160,32},{192,64},{224,... | collective-permute-start | bytes 393224 | tf_op jit(solution)/shard_map/ppermute | solution.py:147
  5.2 8.0 %collective-permute-start.3 = (bf16[256,256]{1,0:T(8,128)(2,1)}, bf16[256,256]{1,0:T(8,128)(2,1)S(1)}, u32[]{:S(2)}, u32[]{:S(2)}) collective-permute-start(bf16[256,256]{1,0:T(8,128)(2,1)} %basis.1), channel_id=1, source_target_pairs={{0,32},{32,0},{64,96},{96,64},{128,160},{160,128},{192,224},{224,1... | collective-permute-start | bytes 393224 | tf_op jit(solution)/shard_map/ppermute | solution.py:150
  9.3 3.9 %collective-permute-start.4 = (bf16[256,256]{1,0:T(8,128)(2,1)S(1)}, bf16[256,256]{1,0:T(8,128)(2,1)S(1)}, u32[]{:S(2)}, u32[]{:S(2)}) collective-permute-start(bf16[256,256]{1,0:T(8,128)(2,1)S(1)} %collective-permute-done.refs_1_), channel_id=1, source_target_pairs={{0,32},{32,0},{64,96},{96,64},{128,160},{160,128},{192,224},{224,1... | collective-permute-start | bytes 393224 | tf_op jit(solution)/shard_map/ppermute | solution.py:150
  11.0 2.2 %collective-permute-start.5 = (bf16[256,256]{1,0:T(8,128)(2,1)S(1)}, bf16[256,256]{1,0:T(8,128)(2,1)S(1)}, u32[]{:S(2)}, u32[]{:S(2)}) collective-permute-start(bf16[256,256]{1,0:T(8,128)(2,1)S(1)} %collective-permute-done.1.refs_2_), channel_id=1, source_target_pairs={{0,32},{32,0},{64,96},{96,64},{128,160},{160,128},{192,224},{224,1... | collective-permute-start | bytes 393224 | tf_op jit(solution)/shard_map/ppermute | solution.py:150
  11.4 2.7 %collective-permute-start.6 = (bf16[256,256]{1,0:T(8,128)(2,1)S(1)}, bf16[256,256]{1,0:T(8,128)(2,1)S(1)}, u32[]{:S(2)}, u32[]{:S(2)}) collective-permute-start(bf16[256,256]{1,0:T(8,128)(2,1)S(1)} %collective-permute-done.2.refs_3_), channel_id=1, source_target_pairs={{0,32},{32,0},{64,96},{96,64},{128,160},{160,128},{192,224},{224,1... | collective-permute-start | bytes 393224 | tf_op jit(solution)/shard_map/ppermute | solution.py:150
  16.1 8.8 %collective-permute-start.7 = (f16[2,256,256]{2,1,0:T(8,128)(2,1)S(1)}, f16[2,256,256]{2,1,0:T(8,128)(2,1)S(1)}, u32[]{:S(2)}, u32[]{:S(2)}) collective-permute-start(f16[2,256,256]{2,1,0:T(8,128)(2,1)S(1)} %convert_element_type.61), channel_id=1, source_target_pairs={{0,1},{1,2},{2,3},{3,0},{4,5},{5,6},{6,7},{7,4},{8,9},{9,10},{10,1... | collective-permute-start | bytes 786440 | tf_op jit(solution)/shard_map/ppermute | solution.py:158
  16.5 8.4 %collective-permute-start.8 = (f16[2,256,256]{2,1,0:T(8,128)(2,1)S(1)}, f16[2,256,256]{2,1,0:T(8,128)(2,1)S(1)}, u32[]{:S(2)}, u32[]{:S(2)}) collective-permute-start(f16[2,256,256]{2,1,0:T(8,128)(2,1)S(1)} %convert_element_type.63), channel_id=1, source_target_pairs={{0,3},{1,0},{2,1},{3,2},{4,7},{5,4},{6,5},{7,6},{8,11},{9,8},{10,9... | collective-permute-start | bytes 786440 | tf_op jit(solution)/shard_map/ppermute | solution.py:158
  19.0 12.0 %collective-permute-start.9 = (f16[2,256,256]{2,1,0:T(8,128)(2,1)S(1)}, f16[2,256,256]{2,1,0:T(8,128)(2,1)S(1)}, u32[]{:S(2)}, u32[]{:S(2)}) collective-permute-start(f16[2,256,256]{2,1,0:T(8,128)(2,1)S(1)} %convert_element_type.65), channel_id=1, source_target_pairs={{0,2},{1,3},{2,0},{3,1},{4,6},{5,7},{6,4},{7,5},{8,10},{9,11},{10,... | collective-permute-start | bytes 786440 | tf_op jit(solution)/shard_map/ppermute | solution.py:158
  60.4 6.8 %collective-permute-start.10 = (bf16[2,256,256]{2,1,0:T(8,128)(2,1)S(1)}, bf16[2,256,256]{2,1,0:T(8,128)(2,1)S(1)}, u32[]{:S(2)}, u32[]{:S(2)}) collective-permute-start(bf16[2,256,256]{2,1,0:T(8,128)(2,1)S(1)} %bitcast.16), channel_id=1, source_target_pairs={{0,1},{1,2},{2,3},{3,0},{4,5},{5,6},{6,7},{7,4},{8,9},{9,10},{10,1... | collective-permute-start | bytes 786440 | tf_op jit(solution)/shard_map/ppermute | solution.py:168
  60.9 9.0 %collective-permute-start.11 = (bf16[2,256,256]{2,1,0:T(8,128)(2,1)S(1)}, bf16[2,256,256]{2,1,0:T(8,128)(2,1)S(1)}, u32[]{:S(2)}, u32[]{:S(2)}) collective-permute-start(bf16[2,256,256]{2,1,0:T(8,128)(2,1)S(1)} %bitcast.17), channel_id=1, source_target_pairs={{0,3},{1,0},{2,1},{3,2},{4,7},{5,4},{6,5},{7,6},{8,11},{9,8},{10,9... | collective-permute-start | bytes 786440 | tf_op jit(solution)/shard_map/ppermute | solution.py:168
  63.4 9.6 %collective-permute-start.12 = (bf16[2,256,256]{2,1,0:T(8,128)(2,1)S(1)}, bf16[2,256,256]{2,1,0:T(8,128)(2,1)S(1)}, u32[]{:S(2)}, u32[]{:S(2)}) collective-permute-start(bf16[2,256,256]{2,1,0:T(8,128)(2,1)S(1)} %bitcast.18), channel_id=1, source_target_pairs={{0,2},{1,3},{2,0},{3,1},{4,6},{5,7},{6,4},{7,5},{8,10},{9,11},{10,... | collective-permute-start | bytes 786440 | tf_op jit(solution)/shard_map/ppermute | solution.py:168
  74.9 6.2 %collective-permute-start.13 = (bf16[4,256,256]{2,1,0:T(8,128)(2,1)S(1)}, bf16[4,256,256]{2,1,0:T(8,128)(2,1)S(1)}, u32[]{:S(2)}, u32[]{:S(2)}) collective-permute-start(bf16[4,256,256]{2,1,0:T(8,128)(2,1)S(1)} %get-tuple-element.26), channel_id=1, source_target_pairs={{0,32},{32,0},{64,96},{96,64},{128,160},{160,128},{192,224},{224,1... | collective-permute-start | bytes 1572872 | tf_op jit(solution)/shard_map/ppermute | solution.py:176
  81.2 6.0 %collective-permute-start.14 = (bf16[256,256]{1,0:T(8,128)(2,1)S(1)}, bf16[256,256]{1,0:T(8,128)(2,1)S(1)}, u32[]{:S(2)}, u32[]{:S(2)}) collective-permute-start(bf16[256,256]{1,0:T(8,128)(2,1)S(1)} %get-tuple-element.27), channel_id=1, source_target_pairs={{0,64},{32,96},{64,128},{96,160},{128,192},{160,224},{192,0},{224,... | collective-permute-start | bytes 393224 | tf_op jit(solution)/shard_map/ppermute | solution.py:179
  81.6 5.7 %collective-permute-start.15 = (bf16[256,256]{1,0:T(8,128)(2,1)S(1)}, bf16[256,256]{1,0:T(8,128)(2,1)S(1)}, u32[]{:S(2)}, u32[]{:S(2)}) collective-permute-start(bf16[256,256]{1,0:T(8,128)(2,1)S(1)} %get-tuple-element.29), channel_id=1, source_target_pairs={{0,192},{32,224},{64,0},{96,32},{128,64},{160,96},{192,128},{224,1... | collective-permute-start | bytes 393224 | tf_op jit(solution)/shard_map/ppermute | solution.py:179
  84.0 7.1 %collective-permute-start.16 = (bf16[256,256]{1,0:T(8,128)(2,1)S(1)}, bf16[256,256]{1,0:T(8,128)(2,1)S(1)}, u32[]{:S(2)}, u32[]{:S(2)}) collective-permute-start(bf16[256,256]{1,0:T(8,128)(2,1)S(1)} %get-tuple-element.28), channel_id=1, source_target_pairs={{0,128},{32,160},{64,192},{96,224},{128,0},{160,32},{192,64},{224,... | collective-permute-start | bytes 393224 | tf_op jit(solution)/shard_map/ppermute | solution.py:179

commit v5 on v4

--- a/solution.py
+++ b/solution.py
@@ -12,8 +12,9 @@
 NX = 4
 UNROLL = 8
 SHIFTS_A, SHIFTS_B, SHIFTS_C, SHIFTS_D = (1, 3, 2), (1, 3, 2), (1, 3, 2), (1, 3, 2)
-SCALE_X = 64.0
-SCALE_Z = 16.0
+TOP = 13.0
+LEAST = -100.0
+EXTRA = 8
 
 
 def shift_y(count, d):
@@ -96,7 +97,7 @@
 
 
 def forward_kernel(table, count, blocks, *refs):
-    pieces, (own, *sends), (basis, acc) = refs[:8], refs[8:12], refs[12:]
+    pieces, (own_exponent, own, *sends), (basis, acc) = refs[:8], refs[8:13], refs[13:]
     y, k = lax.axis_index("row") // CORES, lax.axis_index("row") % CORES
     x = lax.axis_index("col") % NX
     for i, d in enumerate((0,) + SHIFTS_A):
@@ -104,12 +105,21 @@
         basis[at * CORES + k] = pieces[i][...]
         basis[at * CORES + 1 - k] = pieces[4 + i][...]
     add_products(table, count, blocks, basis, acc, False)
+    largest = jnp.abs(acc[0])
+    for r in range(1, 8):
+        largest = jnp.maximum(largest, jnp.abs(acc[r]))
+    largest = jnp.max(jnp.max(largest, axis=0, keepdims=True), axis=1, keepdims=True)
+    exponent = jnp.maximum(jnp.ceil(jnp.log2(jnp.maximum(largest, 2.0**LEAST))), LEAST)
+    scale = jnp.exp2(TOP - exponent)
+    own_exponent[...] = jnp.broadcast_to(exponent, own_exponent.shape)
+    size = acc.shape[1]
     for h in range(2):
         own[h] = acc[x * 2 + h]
     for send, d in zip(sends, SHIFTS_B):
         to = (x + d) % NX
         for h in range(2):
-            send[h] = acc[to * 2 + h] * SCALE_X
+            send[h * size : (h + 1) * size] = acc[to * 2 + h] * scale
+        send[2 * size :] = jnp.broadcast_to(exponent, (EXTRA, send.shape[1]))
 
 
 def backward_kernel(table, count, blocks, *refs):
@@ -148,19 +158,32 @@
     blocks, own = fetch(block_values, basis)
     mine[1], blocks, own = lax.optimization_barrier((mine[1], blocks, own))
     other = [lax.ppermute(p, "row", swap_core(n_row)) for p in mine]
-    own, *sends = call(
+    exponent, own, *sends = call(
         forward_kernel,
-        [jax.ShapeDtypeStruct((2, size, rank), F32)] * 4,
+        [
+            jax.ShapeDtypeStruct((EXTRA, rank), F32),
+            jax.ShapeDtypeStruct((2, size, rank), F32),
+            *[jax.ShapeDtypeStruct((2 * size + EXTRA, rank), F32)] * 3,
+        ],
         [pltpu.VMEM((8, size, rank), BF16), pltpu.VMEM((9, size, rank), F32)],
         9,
         *table, blocks, own, *mine[1:], *other,
     )
     got = [lax.ppermute(s.astype(F16), "col", shift_x(n_col, d)) for d, s in zip(SHIFTS_B, sends)]
-    x_sum = own + (got[0].astype(F32) + got[1].astype(F32) + got[2].astype(F32)) * (1 / SCALE_X)
+    x_sum = own.reshape(2 * size, rank)
+    exponent = exponent[:1]
+    for piece in got:
+        theirs = piece[2 * size : 2 * size + 1].astype(F32)
+        x_sum += piece[: 2 * size].astype(F32) * jnp.exp2(theirs - TOP)
+        exponent = jnp.maximum(exponent, theirs)
+    exponent = exponent + 2
     nz = n_col // NX
-    parts = (x_sum * SCALE_Z).astype(F16).reshape(nz, 2 * size // nz, rank)
+    rows = 2 * size // nz
+    parts = (x_sum * jnp.exp2(TOP - exponent)).astype(F16).reshape(nz, rows, rank)
+    parts = jnp.concatenate([parts, jnp.broadcast_to(exponent.astype(F16), (nz, EXTRA, rank))], 1)
     parts = lax.all_to_all(parts, "col", 0, 0, tiled=True, axis_index_groups=z_groups(n_col))
-    share = (jnp.sum(parts.astype(F32), axis=0) * (1 / SCALE_Z)).astype(BF16)
+    scale = jnp.exp2(parts[:, rows : rows + 1].astype(F32) - TOP)
+    share = jnp.sum(parts[:, :rows].astype(F32) * scale, axis=0).astype(BF16)
 
     copies = jnp.broadcast_to(share[None], (nz, *share.shape))
     chunk = lax.all_to_all(copies, "col", 0, 0, tiled=True, axis_index_groups=z_groups(n_col))

time: 91.5 us -> 94.5 us (1.033); the launches traced: 91.8 us -> 92.9 us
  starting transfers between devices: 26.7 us -> 21.5 us
  blocking collectives: 29.1 us -> 32.7 us
  Pallas kernels: 5.73 us -> 6.93 us
  waiting for transfers between devices: 28.3 us -> 29.5 us
    all_to_all x1, blocking collectives: 17.2 us -> 20.2 us  [body(): lax.all_to_all(parts, 'col', 0, 0, tiled=True, axis_index_groups=z_groups...]
    ppermute x1, starting transfers between devices: 4.61 us -> 2.49 us  [body(): pair = own + lax.ppermute(send, 'row', swap_core(n_row)).astype(F32)]
    ppermute x3, starting transfers between devices: 4.2 us -> 2.68 us  [body(): lax.ppermute(chunk, 'col', shift_x(n_col, d))]
    ppermute x3, waiting for transfers between devices: 8.38 us -> 9.74 us  [body(): lax.ppermute(chunk, 'col', shift_x(n_col, d))]
    pallas_call x2, Pallas kernels: 3.82 us -> 5.02 us  [call(): pl.pallas_call(kernel, out_shape=outs, in_specs=smem(2) + vmem(n_vmem), o...]
    ppermute x3, starting transfers between devices: 3.79 us -> 2.75 us  [body(): lax.ppermute(pick(d).astype(BF16), 'row', shift_y(n_row, d))]
where the time goes in v5:
time: 94.5 us; the launch traced here: 92.9 us
  blocking collectives  32.7 us (35%)
  waiting for transfers between devices  29.5 us (31%)
  starting transfers between devices  21.5 us (23%)
  Pallas kernels  6.93 us (7%)
  other arithmetic  1.41 us (1%)
    all_to_all x1, blocking collectives, body(): lax.all_to_all(parts, 'col', 0, 0, tiled=True, axis_index_groups=z_groups...  20.2 us
    all_to_all x1, blocking collectives, body(): lax.all_to_all(copies, 'col', 0, 0, tiled=True, axis_index_groups=z_group...  12.5 us
    ppermute x3, waiting for transfers between devices, body(): lax.ppermute(s.astype(F16), 'col', shift_x(n_col, d))  11.9 us
    ppermute x3, waiting for transfers between devices, body(): lax.ppermute(chunk, 'col', shift_x(n_col, d))  9.74 us
    ppermute x4, starting transfers between devices, body(): other = [lax.ppermute(p, 'row', swap_core(n_row)) for p in mine]  5.37 us
    ppermute x3, waiting for transfers between devices, body(): lax.ppermute(pick(d).astype(BF16), 'row', shift_y(n_row, d))  5.32 us
    ppermute x3, starting transfers between devices, body(): lax.ppermute(basis, 'row', shift_y(n_row, d))  5.21 us
    pallas_call x2, Pallas kernels, call(): pl.pallas_call(kernel, out_shape=outs, in_specs=smem(2) + vmem(n_vmem), o...  5.02 us
  transfers between devices with their start and end apart: 17, of which 9 were waited for; matrix products, arithmetic and copies ran while one was open for 0% of the time, Pallas kernels for 2%

profile of v5, /device:TPU:1, one launch (start us, length us, event | category | flops | bytes accessed | tf_op | source)
XLA Modules:
  0.0 92.9 jit_solution(9277831503399535974)
XLA Ops:
  0.0 0.0 copy-start.1
  0.0 0.0 copy-start
  0.0 2.1 %collective-permute-start = (bf16[256,256]{1,0:T(8,128)(2,1)}, bf16[256,256]{1,0:T(8,128)(2,1)S(1)}, u32[]{:S(2)}, u32[]{:S(2)}) collective-permute-start(bf16[256,256]{1,0:T(8,128)(2,1)} %basis.1), channel_id=1, source_target_pairs={{0,64},{32,96},{64,128},{96,160},{128,192},{160,224},{192,0},{224,... | collective-permute-start | bytes 393224 | tf_op jit(solution)/shard_map/ppermute | solution.py:157
  2.1 1.5 %collective-permute-start.1 = (bf16[256,256]{1,0:T(8,128)(2,1)}, bf16[256,256]{1,0:T(8,128)(2,1)S(1)}, u32[]{:S(2)}, u32[]{:S(2)}) collective-permute-start(bf16[256,256]{1,0:T(8,128)(2,1)} %basis.1), channel_id=1, source_target_pairs={{0,192},{32,224},{64,0},{96,32},{128,64},{160,96},{192,128},{224,1... | collective-permute-start | bytes 393224 | tf_op jit(solution)/shard_map/ppermute | solution.py:157
  3.7 1.6 %collective-permute-start.2 = (bf16[256,256]{1,0:T(8,128)(2,1)}, bf16[256,256]{1,0:T(8,128)(2,1)S(1)}, u32[]{:S(2)}, u32[]{:S(2)}) collective-permute-start(bf16[256,256]{1,0:T(8,128)(2,1)} %basis.1), channel_id=1, source_target_pairs={{0,128},{32,160},{64,192},{96,224},{128,0},{160,32},{192,64},{224,... | collective-permute-start | bytes 393224 | tf_op jit(solution)/shard_map/ppermute | solution.py:157
  5.2 1.5 %collective-permute-start.3 = (bf16[256,256]{1,0:T(8,128)(2,1)}, bf16[256,256]{1,0:T(8,128)(2,1)S(1)}, u32[]{:S(2)}, u32[]{:S(2)}) collective-permute-start(bf16[256,256]{1,0:T(8,128)(2,1)} %basis.1), channel_id=1, source_target_pairs={{0,32},{32,0},{64,96},{96,64},{128,160},{160,128},{192,224},{224,1... | collective-permute-start | bytes 393224 | tf_op jit(solution)/shard_map/ppermute | solution.py:160
  6.7 1.9 %shard_map.55 = (bf16[1,1,24,256,256]{4,3,2,1,0:T(8,128)(2,1)S(1)}, bf16[256,256]{1,0:T(8,128)(2,1)S(1)}) custom-call(bf16[1,1,24,256,256]{4,3,2,1,0:T(8,128)(2,1)} %blocks.1, bf16[256,256]{1,0:T(8,128)(2,1)} %basis.1), custom_call_target="tpu_custom_call" | custom-call | bytes 8388608 | tf_op jit(solution)/shard_map/pallas_call | solution.py:65
  9.3 0.0 collective-permute-done.refs_1_
  9.3 1.7 %collective-permute-start.4 = (bf16[256,256]{1,0:T(8,128)(2,1)S(1)}, bf16[256,256]{1,0:T(8,128)(2,1)S(1)}, u32[]{:S(2)}, u32[]{:S(2)}) collective-permute-start(bf16[256,256]{1,0:T(8,128)(2,1)S(1)} %collective-permute-done.refs_1_), channel_id=1, source_target_pairs={{0,32},{32,0},{64,96},{96,64},{128,160},{160,128},{192,224},{224,1... | collective-permute-start | bytes 393224 | tf_op jit(solution)/shard_map/ppermute | solution.py:160
  11.0 0.0 collective-permute-done.1.refs_2_
  11.0 0.4 collective-permute-start.5
  11.4 0.0 collective-permute-done.2.refs_3_
  11.4 1.7 %collective-permute-start.6 = (bf16[256,256]{1,0:T(8,128)(2,1)S(1)}, bf16[256,256]{1,0:T(8,128)(2,1)S(1)}, u32[]{:S(2)}, u32[]{:S(2)}) collective-permute-start(bf16[256,256]{1,0:T(8,128)(2,1)S(1)} %collective-permute-done.2.refs_3_), channel_id=1, source_target_pairs={{0,32},{32,0},{64,96},{96,64},{128,160},{160,128},{192,224},{224,1... | collective-permute-start | bytes 393224 | tf_op jit(solution)/shard_map/ppermute | solution.py:160
  13.2 0.0 copy-done.1
  13.2 0.0 copy-done
  13.2 0.0 collective-permute-done.3.refs_4_
  13.2 0.0 collective-permute-done.4.refs_5_
  13.2 0.0 collective-permute-done.5.refs_6_
  13.2 0.9 %collective-permute-done.6.refs_7_ = bf16[256,256]{1,0:T(8,128)(2,1)S(1)} collective-permute-done((bf16[256,256]{1,0:T(8,128)(2,1)S(1)}, bf16[256,256]{1,0:T(8,128)(2,1)S(1)}, u32[]{:S(2)}, u32[]{:S(2)}) %collective-permute-start.6) | collective-permute-done | bytes 131104 | tf_op jit(solution)/shard_map/ppermute | solution.py:160
  14.2 2.6 %shard_map.56 = (f32[8,256]{1,0:T(8,128)S(1)}, f32[2,256,256]{2,1,0:T(8,128)S(1)}, f32[520,256]{1,0:T(8,128)S(1)}, f32[520,256]{1,0:T(8,128)S(1)}, f32[520,256]{1,0:T(8,128)S(1)}) custom-call(s32[24]{0:T(128)S(1)} %add_bitcast_fusion.table, s32[1,1]{1,0:T(1,128)S(6)} %copy.10.count, bf16[1,1,24,256,256]{4,3,2,1,0:T(8,128)(2,1)S(1)} %get-tuple-element.19.blocks, ...), custom_call_target="tpu_custom_call" | custom-call | flops 805306368 | bytes 1048576 | tf_op jit(solution)/shard_map/pallas_call | solution.py:141
  16.8 0.1 collective-permute-start.7
  16.9 2.7 %collective-permute-start.8 = (f16[520,256]{1,0:T(8,128)(2,1)S(1)}, f16[520,256]{1,0:T(8,128)(2,1)S(1)}, u32[]{:S(2)}, u32[]{:S(2)}) collective-permute-start(f16[520,256]{1,0:T(8,128)(2,1)S(1)} %convert_element_type.81), channel_id=1, source_target_pairs={{0,3},{1,0},{2,1},{3,2},{4,7},{5,4},{6,5},{7,6},{8,11},{9,8},{10,9... | collective-permute-start | bytes 798728 | tf_op jit(solution)/shard_map/ppermute | solution.py:172
  19.7 0.2 collective-permute-start.9
  19.9 11.9 %collective-permute-done.7 = f16[520,256]{1,0:T(8,128)(2,1)S(1)} collective-permute-done((f16[520,256]{1,0:T(8,128)(2,1)S(1)}, f16[520,256]{1,0:T(8,128)(2,1)S(1)}, u32[]{:S(2)}, u32[]{:S(2)}) %collective-permute-start.7) | collective-permute-done | bytes 266272 | tf_op jit(solution)/shard_map/ppermute | solution.py:172
  31.8 0.0 collective-permute-done.8
  31.8 0.0 collective-permute-done.9
  31.8 0.2 fusion.3
  32.1 0.1 pad_maximum_fusion
  32.2 20.2 %all_to_all.10 = f16[8,72,256]{2,1,0:T(8,128)(2,1)S(1)} all-to-all(f16[8,72,256]{2,1,0:T(8,128)(2,1)S(1)} %pad_maximum_fusion), channel_id=1, replica_groups={{0,4,8,12,16,20,24,28},{1,5,9,13,17,21,25,29},{2,6,10,14,18,22,26,30},{..., dimensions={0} | all-to-all | bytes 589824 | tf_op jit(solution)/shard_map/all_to_all | solution.py:184
  52.4 0.1 multiply_reduce_fusion
  52.5 12.5 %all_to_all.11 = bf16[8,64,256]{2,1,0:T(8,128)(2,1)S(1)} all-to-all(bf16[8,64,256]{2,1,0:T(8,128)(2,1)S(1)} %broadcast_in_dim.5), channel_id=1, replica_groups={{0,4,8,12,16,20,24,28},{1,5,9,13,17,21,25,29},{2,6,10,14,18,22,26,30},{..., dimensions={0} | all-to-all | bytes 524288 | tf_op jit(solution)/shard_map/all_to_all | solution.py:189
  65.0 0.0 collective-permute-start.10
  65.0 2.7 %collective-permute-start.11 = (bf16[2,256,256]{2,1,0:T(8,128)(2,1)S(1)}, bf16[2,256,256]{2,1,0:T(8,128)(2,1)S(1)}, u32[]{:S(2)}, u32[]{:S(2)}) collective-permute-start(bf16[2,256,256]{2,1,0:T(8,128)(2,1)S(1)} %bitcast.33), channel_id=1, source_target_pairs={{0,3},{1,0},{2,1},{3,2},{4,7},{5,4},{6,5},{7,6},{8,11},{9,8},{10,9... | collective-permute-start | bytes 786440 | tf_op jit(solution)/shard_map/ppermute | solution.py:191
  67.7 0.0 collective-permute-start.12
  67.7 3.8 %collective-permute-done.10.refs_1_ = bf16[2,256,256]{2,1,0:T(8,128)(2,1)S(1)} collective-permute-done((bf16[2,256,256]{2,1,0:T(8,128)(2,1)S(1)}, bf16[2,256,256]{2,1,0:T(8,128)(2,1)S(1)}, u32[]{:S(2)}, u32[]{:S(2)}) %collective-permute-start.10) | collective-permute-done | bytes 262176 | tf_op jit(solution)/shard_map/ppermute | solution.py:191
  71.4 3.2 %collective-permute-done.11.refs_2_ = bf16[2,256,256]{2,1,0:T(8,128)(2,1)S(1)} collective-permute-done((bf16[2,256,256]{2,1,0:T(8,128)(2,1)S(1)}, bf16[2,256,256]{2,1,0:T(8,128)(2,1)S(1)}, u32[]{:S(2)}, u32[]{:S(2)}) %collective-permute-start.11) | collective-permute-done | bytes 262176 | tf_op jit(solution)/shard_map/ppermute | solution.py:191
  74.6 2.8 %collective-permute-done.12.refs_3_ = bf16[2,256,256]{2,1,0:T(8,128)(2,1)S(1)} collective-permute-done((bf16[2,256,256]{2,1,0:T(8,128)(2,1)S(1)}, bf16[2,256,256]{2,1,0:T(8,128)(2,1)S(1)}, u32[]{:S(2)}, u32[]{:S(2)}) %collective-permute-start.12) | collective-permute-done | bytes 262176 | tf_op jit(solution)/shard_map/ppermute | solution.py:191
  77.4 2.4 %shard_map.57 = (f32[4,256,256]{2,1,0:T(8,128)S(1)}, bf16[4,256,256]{2,1,0:T(8,128)(2,1)S(1)}) custom-call(s32[24]{0:T(128)S(1)} %add_bitcast_fusion.table, s32[1,1]{1,0:T(1,128)S(6)} %copy.10.count, bf16[1,1,24,256,256]{4,3,2,1,0:T(8,128)(2,1)S(1)} %get-tuple-element.19.blocks, bf16[2,256,256]{2,1,0:T(8,128)(2,1)S(1)} %bitcast.35, ...), custom_call_target="tpu_custom_call" | custom-call | flops 805306368 | bytes 1048576 | tf_op jit(solution)/shard_map/pallas_call | solution.py:141
  79.8 2.5 %collective-permute-start.13 = (bf16[4,256,256]{2,1,0:T(8,128)(2,1)S(1)}, bf16[4,256,256]{2,1,0:T(8,128)(2,1)S(1)}, u32[]{:S(2)}, u32[]{:S(2)}) collective-permute-start(bf16[4,256,256]{2,1,0:T(8,128)(2,1)S(1)} %get-tuple-element.28), channel_id=1, source_target_pairs={{0,32},{32,0},{64,96},{96,64},{128,160},{160,128},{192,224},{224,1... | collective-permute-start | bytes 1572872 | tf_op jit(solution)/shard_map/ppermute | solution.py:199
  82.3 1.5 %collective-permute-done.13 = bf16[4,256,256]{2,1,0:T(8,128)(2,1)S(1)} collective-permute-done((bf16[4,256,256]{2,1,0:T(8,128)(2,1)S(1)}, bf16[4,256,256]{2,1,0:T(8,128)(2,1)S(1)}, u32[]{:S(2)}, u32[]{:S(2)}) %collective-permute-start.13) | collective-permute-done | bytes 524320 | tf_op jit(solution)/shard_map/ppermute | solution.py:199
  83.9 0.1 convert_add_fusion
  84.0 0.1 fusion.6
  84.0 0.1 collective-permute-start.14
  84.1 2.7 %collective-permute-start.15 = (bf16[256,256]{1,0:T(8,128)(2,1)S(1)}, bf16[256,256]{1,0:T(8,128)(2,1)S(1)}, u32[]{:S(2)}, u32[]{:S(2)}) collective-permute-start(bf16[256,256]{1,0:T(8,128)(2,1)S(1)} %get-tuple-element.33), channel_id=1, source_target_pairs={{0,192},{32,224},{64,0},{96,32},{128,64},{160,96},{192,128},{224,1... | collective-permute-start | bytes 393224 | tf_op jit(solution)/shard_map/ppermute | solution.py:202
  86.8 0.0 collective-permute-start.16
  86.8 3.2 %collective-permute-done.14 = bf16[256,256]{1,0:T(8,128)(2,1)S(1)} collective-permute-done((bf16[256,256]{1,0:T(8,128)(2,1)S(1)}, bf16[256,256]{1,0:T(8,128)(2,1)S(1)}, u32[]{:S(2)}, u32[]{:S(2)}) %collective-permute-start.14) | collective-permute-done | bytes 131104 | tf_op jit(solution)/shard_map/ppermute | solution.py:202
  90.0 1.9 %collective-permute-done.15 = bf16[256,256]{1,0:T(8,128)(2,1)S(1)} collective-permute-done((bf16[256,256]{1,0:T(8,128)(2,1)S(1)}, bf16[256,256]{1,0:T(8,128)(2,1)S(1)}, u32[]{:S(2)}, u32[]{:S(2)}) %collective-permute-start.15) | collective-permute-done | bytes 131104 | tf_op jit(solution)/shard_map/ppermute | solution.py:202
  91.9 0.2 collective-permute-done.16
  92.1 0.8 fusion.5
  (10 shorter events, 0.2 us)
Async XLA Ops:
  0.0 13.2 %copy-start.1 = (s32[1,1,24]{2,1,0:T(1,128)S(1)}, s32[1,1,24]{2,1,0:T(1,128)}, u32[]{:S(2)}) copy-start(s32[1,1,24]{2,1,0:T(1,128)} %param.6) | copy-start | bytes 292
  0.0 13.2 %copy-start = (s32[1,1,24]{2,1,0:T(1,128)S(1)}, s32[1,1,24]{2,1,0:T(1,128)}, u32[]{:S(2)}) copy-start(s32[1,1,24]{2,1,0:T(1,128)} %param.7) | copy-start | bytes 292
  0.0 9.3 %collective-permute-start = (bf16[256,256]{1,0:T(8,128)(2,1)}, bf16[256,256]{1,0:T(8,128)(2,1)S(1)}, u32[]{:S(2)}, u32[]{:S(2)}) collective-permute-start(bf16[256,256]{1,0:T(8,128)(2,1)} %basis.1), channel_id=1, source_target_pairs={{0,64},{32,96},{64,128},{96,160},{128,192},{160,224},{192,0},{224,... | collective-permute-start | bytes 393224 | tf_op jit(solution)/shard_map/ppermute | solution.py:157
  2.1 8.9 %collective-permute-start.1 = (bf16[256,256]{1,0:T(8,128)(2,1)}, bf16[256,256]{1,0:T(8,128)(2,1)S(1)}, u32[]{:S(2)}, u32[]{:S(2)}) collective-permute-start(bf16[256,256]{1,0:T(8,128)(2,1)} %basis.1), channel_id=1, source_target_pairs={{0,192},{32,224},{64,0},{96,32},{128,64},{160,96},{192,128},{224,1... | collective-permute-start | bytes 393224 | tf_op jit(solution)/shard_map/ppermute | solution.py:157
  3.7 7.8 %collective-permute-start.2 = (bf16[256,256]{1,0:T(8,128)(2,1)}, bf16[256,256]{1,0:T(8,128)(2,1)S(1)}, u32[]{:S(2)}, u32[]{:S(2)}) collective-permute-start(bf16[256,256]{1,0:T(8,128)(2,1)} %basis.1), channel_id=1, source_target_pairs={{0,128},{32,160},{64,192},{96,224},{128,0},{160,32},{192,64},{224,... | collective-permute-start | bytes 393224 | tf_op jit(solution)/shard_map/ppermute | solution.py:157
  5.2 8.0 %collective-permute-start.3 = (bf16[256,256]{1,0:T(8,128)(2,1)}, bf16[256,256]{1,0:T(8,128)(2,1)S(1)}, u32[]{:S(2)}, u32[]{:S(2)}) collective-permute-start(bf16[256,256]{1,0:T(8,128)(2,1)} %basis.1), channel_id=1, source_target_pairs={{0,32},{32,0},{64,96},{96,64},{128,160},{160,128},{192,224},{224,1... | collective-permute-start | bytes 393224 | tf_op jit(solution)/shard_map/ppermute | solution.py:160
  9.3 3.9 %collective-permute-start.4 = (bf16[256,256]{1,0:T(8,128)(2,1)S(1)}, bf16[256,256]{1,0:T(8,128)(2,1)S(1)}, u32[]{:S(2)}, u32[]{:S(2)}) collective-permute-start(bf16[256,256]{1,0:T(8,128)(2,1)S(1)} %collective-permute-done.refs_1_), channel_id=1, source_target_pairs={{0,32},{32,0},{64,96},{96,64},{128,160},{160,128},{192,224},{224,1... | collective-permute-start | bytes 393224 | tf_op jit(solution)/shard_map/ppermute | solution.py:160
  11.0 2.2 %collective-permute-start.5 = (bf16[256,256]{1,0:T(8,128)(2,1)S(1)}, bf16[256,256]{1,0:T(8,128)(2,1)S(1)}, u32[]{:S(2)}, u32[]{:S(2)}) collective-permute-start(bf16[256,256]{1,0:T(8,128)(2,1)S(1)} %collective-permute-done.1.refs_2_), channel_id=1, source_target_pairs={{0,32},{32,0},{64,96},{96,64},{128,160},{160,128},{192,224},{224,1... | collective-permute-start | bytes 393224 | tf_op jit(solution)/shard_map/ppermute | solution.py:160
  11.4 2.7 %collective-permute-start.6 = (bf16[256,256]{1,0:T(8,128)(2,1)S(1)}, bf16[256,256]{1,0:T(8,128)(2,1)S(1)}, u32[]{:S(2)}, u32[]{:S(2)}) collective-permute-start(bf16[256,256]{1,0:T(8,128)(2,1)S(1)} %collective-permute-done.2.refs_3_), channel_id=1, source_target_pairs={{0,32},{32,0},{64,96},{96,64},{128,160},{160,128},{192,224},{224,1... | collective-permute-start | bytes 393224 | tf_op jit(solution)/shard_map/ppermute | solution.py:160
  16.8 15.0 %collective-permute-start.7 = (f16[520,256]{1,0:T(8,128)(2,1)S(1)}, f16[520,256]{1,0:T(8,128)(2,1)S(1)}, u32[]{:S(2)}, u32[]{:S(2)}) collective-permute-start(f16[520,256]{1,0:T(8,128)(2,1)S(1)} %convert_element_type.78), channel_id=1, source_target_pairs={{0,1},{1,2},{2,3},{3,0},{4,5},{5,6},{6,7},{7,4},{8,9},{9,10},{10,1... | collective-permute-start | bytes 798728 | tf_op jit(solution)/shard_map/ppermute | solution.py:172
  16.9 14.9 %collective-permute-start.8 = (f16[520,256]{1,0:T(8,128)(2,1)S(1)}, f16[520,256]{1,0:T(8,128)(2,1)S(1)}, u32[]{:S(2)}, u32[]{:S(2)}) collective-permute-start(f16[520,256]{1,0:T(8,128)(2,1)S(1)} %convert_element_type.81), channel_id=1, source_target_pairs={{0,3},{1,0},{2,1},{3,2},{4,7},{5,4},{6,5},{7,6},{8,11},{9,8},{10,9... | collective-permute-start | bytes 798728 | tf_op jit(solution)/shard_map/ppermute | solution.py:172
  19.7 12.1 %collective-permute-start.9 = (f16[520,256]{1,0:T(8,128)(2,1)S(1)}, f16[520,256]{1,0:T(8,128)(2,1)S(1)}, u32[]{:S(2)}, u32[]{:S(2)}) collective-permute-start(f16[520,256]{1,0:T(8,128)(2,1)S(1)} %convert_element_type.84), channel_id=1, source_target_pairs={{0,2},{1,3},{2,0},{3,1},{4,6},{5,7},{6,4},{7,5},{8,10},{9,11},{10,... | collective-permute-start | bytes 798728 | tf_op jit(solution)/shard_map/ppermute | solution.py:172
  65.0 6.4 %collective-permute-start.10 = (bf16[2,256,256]{2,1,0:T(8,128)(2,1)S(1)}, bf16[2,256,256]{2,1,0:T(8,128)(2,1)S(1)}, u32[]{:S(2)}, u32[]{:S(2)}) collective-permute-start(bf16[2,256,256]{2,1,0:T(8,128)(2,1)S(1)} %bitcast.32), channel_id=1, source_target_pairs={{0,1},{1,2},{2,3},{3,0},{4,5},{5,6},{6,7},{7,4},{8,9},{9,10},{10,1... | collective-permute-start | bytes 786440 | tf_op jit(solution)/shard_map/ppermute | solution.py:191
  65.0 9.7 %collective-permute-start.11 = (bf16[2,256,256]{2,1,0:T(8,128)(2,1)S(1)}, bf16[2,256,256]{2,1,0:T(8,128)(2,1)S(1)}, u32[]{:S(2)}, u32[]{:S(2)}) collective-permute-start(bf16[2,256,256]{2,1,0:T(8,128)(2,1)S(1)} %bitcast.33), channel_id=1, source_target_pairs={{0,3},{1,0},{2,1},{3,2},{4,7},{5,4},{6,5},{7,6},{8,11},{9,8},{10,9... | collective-permute-start | bytes 786440 | tf_op jit(solution)/shard_map/ppermute | solution.py:191
  67.7 9.7 %collective-permute-start.12 = (bf16[2,256,256]{2,1,0:T(8,128)(2,1)S(1)}, bf16[2,256,256]{2,1,0:T(8,128)(2,1)S(1)}, u32[]{:S(2)}, u32[]{:S(2)}) collective-permute-start(bf16[2,256,256]{2,1,0:T(8,128)(2,1)S(1)} %bitcast.34), channel_id=1, source_target_pairs={{0,2},{1,3},{2,0},{3,1},{4,6},{5,7},{6,4},{7,5},{8,10},{9,11},{10,... | collective-permute-start | bytes 786440 | tf_op jit(solution)/shard_map/ppermute | solution.py:191
  79.8 4.0 %collective-permute-start.13 = (bf16[4,256,256]{2,1,0:T(8,128)(2,1)S(1)}, bf16[4,256,256]{2,1,0:T(8,128)(2,1)S(1)}, u32[]{:S(2)}, u32[]{:S(2)}) collective-permute-start(bf16[4,256,256]{2,1,0:T(8,128)(2,1)S(1)} %get-tuple-element.28), channel_id=1, source_target_pairs={{0,32},{32,0},{64,96},{96,64},{128,160},{160,128},{192,224},{224,1... | collective-permute-start | bytes 1572872 | tf_op jit(solution)/shard_map/ppermute | solution.py:199
  84.0 6.0 %collective-permute-start.14 = (bf16[256,256]{1,0:T(8,128)(2,1)S(1)}, bf16[256,256]{1,0:T(8,128)(2,1)S(1)}, u32[]{:S(2)}, u32[]{:S(2)}) collective-permute-start(bf16[256,256]{1,0:T(8,128)(2,1)S(1)} %get-tuple-element.31), channel_id=1, source_target_pairs={{0,64},{32,96},{64,128},{96,160},{128,192},{160,224},{192,0},{224,... | collective-permute-start | bytes 393224 | tf_op jit(solution)/shard_map/ppermute | solution.py:202
  84.1 7.8 %collective-permute-start.15 = (bf16[256,256]{1,0:T(8,128)(2,1)S(1)}, bf16[256,256]{1,0:T(8,128)(2,1)S(1)}, u32[]{:S(2)}, u32[]{:S(2)}) collective-permute-start(bf16[256,256]{1,0:T(8,128)(2,1)S(1)} %get-tuple-element.33), channel_id=1, source_target_pairs={{0,192},{32,224},{64,0},{96,32},{128,64},{160,96},{192,128},{224,1... | collective-permute-start | bytes 393224 | tf_op jit(solution)/shard_map/ppermute | solution.py:202
  86.8 5.3 %collective-permute-start.16 = (bf16[256,256]{1,0:T(8,128)(2,1)S(1)}, bf16[256,256]{1,0:T(8,128)(2,1)S(1)}, u32[]{:S(2)}, u32[]{:S(2)}) collective-permute-start(bf16[256,256]{1,0:T(8,128)(2,1)S(1)} %get-tuple-element.32), channel_id=1, source_target_pairs={{0,128},{32,160},{64,192},{96,224},{128,0},{160,32},{192,64},{224,... | collective-permute-start | bytes 393224 | tf_op jit(solution)/shard_map/ppermute | solution.py:202

commit v6 on v5

--- a/solution.py
+++ b/solution.py
@@ -10,7 +10,7 @@
 F16 = jnp.float16
 CORES = 2
 NX = 4
-UNROLL = 8
+UNROLL = 12
 SHIFTS_A, SHIFTS_B, SHIFTS_C, SHIFTS_D = (1, 3, 2), (1, 3, 2), (1, 3, 2), (1, 3, 2)
 TOP = 13.0
 LEAST = -100.0

time: 94.5 us -> 93.4 us (0.988); the launches traced: 92.9 us -> 94.4 us
  starting transfers between devices: 21.5 us -> 25.5 us
  Pallas kernels: 6.93 us -> 5.24 us
    ppermute x1, starting transfers between devices: 2.49 us -> 4.85 us  [body(): pair = own + lax.ppermute(send, 'row', swap_core(n_row)).astype(F32)]
    pallas_call x2, Pallas kernels: 5.02 us -> 3.33 us  [call(): pl.pallas_call(kernel, out_shape=outs, in_specs=smem(2) + vmem(n_vmem), o...]
    ppermute x3, starting transfers between devices: 2.75 us -> 3.84 us  [body(): lax.ppermute(pick(d).astype(BF16), 'row', shift_y(n_row, d))]
where the time goes in v6:
time: 93.4 us; the launch traced here: 94.4 us
  blocking collectives  32.4 us (35%)
  waiting for transfers between devices  29 us (31%)
  starting transfers between devices  25.5 us (27%)
  Pallas kernels  5.24 us (6%)
  other arithmetic  1.41 us (2%)
    all_to_all x1, blocking collectives, body(): lax.all_to_all(parts, 'col', 0, 0, tiled=True, axis_index_groups=z_groups...  20.4 us
    all_to_all x1, blocking collectives, body(): lax.all_to_all(copies, 'col', 0, 0, tiled=True, axis_index_groups=z_group...  12 us
    ppermute x3, waiting for transfers between devices, body(): lax.ppermute(s.astype(F16), 'col', shift_x(n_col, d))  11.1 us
    ppermute x3, waiting for transfers between devices, body(): lax.ppermute(chunk, 'col', shift_x(n_col, d))  9.35 us
    ppermute x3, waiting for transfers between devices, body(): lax.ppermute(pick(d).astype(BF16), 'row', shift_y(n_row, d))  6.05 us
    ppermute x4, starting transfers between devices, body(): other = [lax.ppermute(p, 'row', swap_core(n_row)) for p in mine]  5.37 us
    ppermute x3, starting transfers between devices, body(): lax.ppermute(basis, 'row', shift_y(n_row, d))  5.21 us
    ppermute x1, starting transfers between devices, body(): pair = own + lax.ppermute(send, 'row', swap_core(n_row)).astype(F32)  4.85 us
  transfers between devices with their start and end apart: 17, of which 9 were waited for; matrix products, arithmetic and copies ran while one was open for 0% of the time, Pallas kernels for 2%

profile of v6, /device:TPU:1, one launch (start us, length us, event | category | flops | bytes accessed | tf_op | source)
XLA Modules:
  0.0 94.4 jit_solution(16204521381101896993)
XLA Ops:
  0.0 0.0 copy-start.1
  0.0 0.0 copy-start
  0.0 2.1 %collective-permute-start = (bf16[256,256]{1,0:T(8,128)(2,1)}, bf16[256,256]{1,0:T(8,128)(2,1)S(1)}, u32[]{:S(2)}, u32[]{:S(2)}) collective-permute-start(bf16[256,256]{1,0:T(8,128)(2,1)} %basis.1), channel_id=1, source_target_pairs={{0,64},{32,96},{64,128},{96,160},{128,192},{160,224},{192,0},{224,... | collective-permute-start | bytes 393224 | tf_op jit(solution)/shard_map/ppermute | solution.py:157
  2.1 1.5 %collective-permute-start.1 = (bf16[256,256]{1,0:T(8,128)(2,1)}, bf16[256,256]{1,0:T(8,128)(2,1)S(1)}, u32[]{:S(2)}, u32[]{:S(2)}) collective-permute-start(bf16[256,256]{1,0:T(8,128)(2,1)} %basis.1), channel_id=1, source_target_pairs={{0,192},{32,224},{64,0},{96,32},{128,64},{160,96},{192,128},{224,1... | collective-permute-start | bytes 393224 | tf_op jit(solution)/shard_map/ppermute | solution.py:157
  3.7 1.6 %collective-permute-start.2 = (bf16[256,256]{1,0:T(8,128)(2,1)}, bf16[256,256]{1,0:T(8,128)(2,1)S(1)}, u32[]{:S(2)}, u32[]{:S(2)}) collective-permute-start(bf16[256,256]{1,0:T(8,128)(2,1)} %basis.1), channel_id=1, source_target_pairs={{0,128},{32,160},{64,192},{96,224},{128,0},{160,32},{192,64},{224,... | collective-permute-start | bytes 393224 | tf_op jit(solution)/shard_map/ppermute | solution.py:157
  5.2 1.5 %collective-permute-start.3 = (bf16[256,256]{1,0:T(8,128)(2,1)}, bf16[256,256]{1,0:T(8,128)(2,1)S(1)}, u32[]{:S(2)}, u32[]{:S(2)}) collective-permute-start(bf16[256,256]{1,0:T(8,128)(2,1)} %basis.1), channel_id=1, source_target_pairs={{0,32},{32,0},{64,96},{96,64},{128,160},{160,128},{192,224},{224,1... | collective-permute-start | bytes 393224 | tf_op jit(solution)/shard_map/ppermute | solution.py:160
  6.7 1.9 %shard_map.55 = (bf16[1,1,24,256,256]{4,3,2,1,0:T(8,128)(2,1)S(1)}, bf16[256,256]{1,0:T(8,128)(2,1)S(1)}) custom-call(bf16[1,1,24,256,256]{4,3,2,1,0:T(8,128)(2,1)} %blocks.1, bf16[256,256]{1,0:T(8,128)(2,1)} %basis.1), custom_call_target="tpu_custom_call" | custom-call | bytes 8388608 | tf_op jit(solution)/shard_map/pallas_call | solution.py:65
  9.3 0.0 collective-permute-done.refs_1_
  9.3 1.7 %collective-permute-start.4 = (bf16[256,256]{1,0:T(8,128)(2,1)S(1)}, bf16[256,256]{1,0:T(8,128)(2,1)S(1)}, u32[]{:S(2)}, u32[]{:S(2)}) collective-permute-start(bf16[256,256]{1,0:T(8,128)(2,1)S(1)} %collective-permute-done.refs_1_), channel_id=1, source_target_pairs={{0,32},{32,0},{64,96},{96,64},{128,160},{160,128},{192,224},{224,1... | collective-permute-start | bytes 393224 | tf_op jit(solution)/shard_map/ppermute | solution.py:160
  11.0 0.0 collective-permute-done.1.refs_2_
  11.0 0.4 collective-permute-start.5
  11.4 0.0 collective-permute-done.2.refs_3_
  11.4 1.7 %collective-permute-start.6 = (bf16[256,256]{1,0:T(8,128)(2,1)S(1)}, bf16[256,256]{1,0:T(8,128)(2,1)S(1)}, u32[]{:S(2)}, u32[]{:S(2)}) collective-permute-start(bf16[256,256]{1,0:T(8,128)(2,1)S(1)} %collective-permute-done.2.refs_3_), channel_id=1, source_target_pairs={{0,32},{32,0},{64,96},{96,64},{128,160},{160,128},{192,224},{224,1... | collective-permute-start | bytes 393224 | tf_op jit(solution)/shard_map/ppermute | solution.py:160
  13.2 0.0 copy-done.1
  13.2 0.0 copy-done
  13.2 0.0 collective-permute-done.3.refs_4_
  13.2 0.0 collective-permute-done.4.refs_5_
  13.2 0.0 collective-permute-done.5.refs_6_
  13.2 0.9 collective-permute-done.6.refs_7_
  14.2 1.8 %shard_map.56 = (f32[8,256]{1,0:T(8,128)S(1)}, f32[2,256,256]{2,1,0:T(8,128)S(1)}, f32[520,256]{1,0:T(8,128)S(1)}, f32[520,256]{1,0:T(8,128)S(1)}, f32[520,256]{1,0:T(8,128)S(1)}) custom-call(s32[24]{0:T(128)S(1)} %add_bitcast_fusion.table, s32[1,1]{1,0:T(1,128)S(6)} %copy.10.count, bf16[1,1,24,256,256]{4,3,2,1,0:T(8,128)(2,1)S(1)} %get-tuple-element.19.blocks, ...), custom_call_target="tpu_custom_call" | custom-call | flops 805306368 | bytes 1048576 | tf_op jit(solution)/shard_map/pallas_call | solution.py:141
  16.0 0.3 collective-permute-start.7
  16.3 2.5 %collective-permute-start.8 = (f16[520,256]{1,0:T(8,128)(2,1)S(1)}, f16[520,256]{1,0:T(8,128)(2,1)S(1)}, u32[]{:S(2)}, u32[]{:S(2)}) collective-permute-start(f16[520,256]{1,0:T(8,128)(2,1)S(1)} %convert_element_type.81), channel_id=1, source_target_pairs={{0,3},{1,0},{2,1},{3,2},{4,7},{5,4},{6,5},{7,6},{8,11},{9,8},{10,9... | collective-permute-start | bytes 798728 | tf_op jit(solution)/shard_map/ppermute | solution.py:172
  18.9 0.7 collective-permute-start.9
  19.5 4.6 %collective-permute-done.7 = f16[520,256]{1,0:T(8,128)(2,1)S(1)} collective-permute-done((f16[520,256]{1,0:T(8,128)(2,1)S(1)}, f16[520,256]{1,0:T(8,128)(2,1)S(1)}, u32[]{:S(2)}, u32[]{:S(2)}) %collective-permute-start.7) | collective-permute-done | bytes 266272 | tf_op jit(solution)/shard_map/ppermute | solution.py:172
  24.1 0.0 collective-permute-done.8
  24.1 6.5 %collective-permute-done.9 = f16[520,256]{1,0:T(8,128)(2,1)S(1)} collective-permute-done((f16[520,256]{1,0:T(8,128)(2,1)S(1)}, f16[520,256]{1,0:T(8,128)(2,1)S(1)}, u32[]{:S(2)}, u32[]{:S(2)}) %collective-permute-start.9) | collective-permute-done | bytes 266272 | tf_op jit(solution)/shard_map/ppermute | solution.py:172
  30.6 0.2 fusion.3
  30.9 0.1 pad_maximum_fusion
  31.0 20.4 %all_to_all.10 = f16[8,72,256]{2,1,0:T(8,128)(2,1)S(1)} all-to-all(f16[8,72,256]{2,1,0:T(8,128)(2,1)S(1)} %pad_maximum_fusion), channel_id=1, replica_groups={{0,4,8,12,16,20,24,28},{1,5,9,13,17,21,25,29},{2,6,10,14,18,22,26,30},{..., dimensions={0} | all-to-all | bytes 589824 | tf_op jit(solution)/shard_map/all_to_all | solution.py:184
  51.4 0.1 multiply_reduce_fusion
  51.5 12.0 %all_to_all.11 = bf16[8,64,256]{2,1,0:T(8,128)(2,1)S(1)} all-to-all(bf16[8,64,256]{2,1,0:T(8,128)(2,1)S(1)} %broadcast_in_dim.5), channel_id=1, replica_groups={{0,4,8,12,16,20,24,28},{1,5,9,13,17,21,25,29},{2,6,10,14,18,22,26,30},{..., dimensions={0} | all-to-all | bytes 524288 | tf_op jit(solution)/shard_map/all_to_all | solution.py:189
  63.5 1.0 %collective-permute-start.10 = (bf16[2,256,256]{2,1,0:T(8,128)(2,1)S(1)}, bf16[2,256,256]{2,1,0:T(8,128)(2,1)S(1)}, u32[]{:S(2)}, u32[]{:S(2)}) collective-permute-start(bf16[2,256,256]{2,1,0:T(8,128)(2,1)S(1)} %bitcast.32), channel_id=1, source_target_pairs={{0,1},{1,2},{2,3},{3,0},{4,5},{5,6},{6,7},{7,4},{8,9},{9,10},{10,1... | collective-permute-start | bytes 786440 | tf_op jit(solution)/shard_map/ppermute | solution.py:191
  64.5 1.7 %collective-permute-start.11 = (bf16[2,256,256]{2,1,0:T(8,128)(2,1)S(1)}, bf16[2,256,256]{2,1,0:T(8,128)(2,1)S(1)}, u32[]{:S(2)}, u32[]{:S(2)}) collective-permute-start(bf16[2,256,256]{2,1,0:T(8,128)(2,1)S(1)} %bitcast.33), channel_id=1, source_target_pairs={{0,3},{1,0},{2,1},{3,2},{4,7},{5,4},{6,5},{7,6},{8,11},{9,8},{10,9... | collective-permute-start | bytes 786440 | tf_op jit(solution)/shard_map/ppermute | solution.py:191
  66.2 0.1 collective-permute-start.12
  66.3 3.7 %collective-permute-done.10.refs_1_ = bf16[2,256,256]{2,1,0:T(8,128)(2,1)S(1)} collective-permute-done((bf16[2,256,256]{2,1,0:T(8,128)(2,1)S(1)}, bf16[2,256,256]{2,1,0:T(8,128)(2,1)S(1)}, u32[]{:S(2)}, u32[]{:S(2)}) %collective-permute-start.10) | collective-permute-done | bytes 262176 | tf_op jit(solution)/shard_map/ppermute | solution.py:191
  69.9 1.1 %collective-permute-done.11.refs_2_ = bf16[2,256,256]{2,1,0:T(8,128)(2,1)S(1)} collective-permute-done((bf16[2,256,256]{2,1,0:T(8,128)(2,1)S(1)}, bf16[2,256,256]{2,1,0:T(8,128)(2,1)S(1)}, u32[]{:S(2)}, u32[]{:S(2)}) %collective-permute-start.11) | collective-permute-done | bytes 262176 | tf_op jit(solution)/shard_map/ppermute | solution.py:191
  71.1 4.5 %collective-permute-done.12.refs_3_ = bf16[2,256,256]{2,1,0:T(8,128)(2,1)S(1)} collective-permute-done((bf16[2,256,256]{2,1,0:T(8,128)(2,1)S(1)}, bf16[2,256,256]{2,1,0:T(8,128)(2,1)S(1)}, u32[]{:S(2)}, u32[]{:S(2)}) %collective-permute-start.12) | collective-permute-done | bytes 262176 | tf_op jit(solution)/shard_map/ppermute | solution.py:191
  75.6 1.6 %shard_map.57 = (f32[4,256,256]{2,1,0:T(8,128)S(1)}, bf16[4,256,256]{2,1,0:T(8,128)(2,1)S(1)}) custom-call(s32[24]{0:T(128)S(1)} %add_bitcast_fusion.table, s32[1,1]{1,0:T(1,128)S(6)} %copy.10.count, bf16[1,1,24,256,256]{4,3,2,1,0:T(8,128)(2,1)S(1)} %get-tuple-element.19.blocks, bf16[2,256,256]{2,1,0:T(8,128)(2,1)S(1)} %bitcast.35, ...), custom_call_target="tpu_custom_call" | custom-call | flops 805306368 | bytes 1048576 | tf_op jit(solution)/shard_map/pallas_call | solution.py:141
  77.2 4.8 %collective-permute-start.13 = (bf16[4,256,256]{2,1,0:T(8,128)(2,1)S(1)}, bf16[4,256,256]{2,1,0:T(8,128)(2,1)S(1)}, u32[]{:S(2)}, u32[]{:S(2)}) collective-permute-start(bf16[4,256,256]{2,1,0:T(8,128)(2,1)S(1)} %get-tuple-element.28), channel_id=1, source_target_pairs={{0,32},{32,0},{64,96},{96,64},{128,160},{160,128},{192,224},{224,1... | collective-permute-start | bytes 1572872 | tf_op jit(solution)/shard_map/ppermute | solution.py:199
  82.1 1.5 %collective-permute-done.13 = bf16[4,256,256]{2,1,0:T(8,128)(2,1)S(1)} collective-permute-done((bf16[4,256,256]{2,1,0:T(8,128)(2,1)S(1)}, bf16[4,256,256]{2,1,0:T(8,128)(2,1)S(1)}, u32[]{:S(2)}, u32[]{:S(2)}) %collective-permute-start.13) | collective-permute-done | bytes 524320 | tf_op jit(solution)/shard_map/ppermute | solution.py:199
  83.6 0.1 convert_add_fusion
  83.7 0.1 fusion.6
  83.8 0.1 collective-permute-start.14
  83.9 2.7 %collective-permute-start.15 = (bf16[256,256]{1,0:T(8,128)(2,1)S(1)}, bf16[256,256]{1,0:T(8,128)(2,1)S(1)}, u32[]{:S(2)}, u32[]{:S(2)}) collective-permute-start(bf16[256,256]{1,0:T(8,128)(2,1)S(1)} %get-tuple-element.33), channel_id=1, source_target_pairs={{0,192},{32,224},{64,0},{96,32},{128,64},{160,96},{192,128},{224,1... | collective-permute-start | bytes 393224 | tf_op jit(solution)/shard_map/ppermute | solution.py:202
  86.5 1.1 %collective-permute-start.16 = (bf16[256,256]{1,0:T(8,128)(2,1)S(1)}, bf16[256,256]{1,0:T(8,128)(2,1)S(1)}, u32[]{:S(2)}, u32[]{:S(2)}) collective-permute-start(bf16[256,256]{1,0:T(8,128)(2,1)S(1)} %get-tuple-element.32), channel_id=1, source_target_pairs={{0,128},{32,160},{64,192},{96,224},{128,0},{160,32},{192,64},{224,... | collective-permute-start | bytes 393224 | tf_op jit(solution)/shard_map/ppermute | solution.py:202
  87.6 2.2 %collective-permute-done.14 = bf16[256,256]{1,0:T(8,128)(2,1)S(1)} collective-permute-done((bf16[256,256]{1,0:T(8,128)(2,1)S(1)}, bf16[256,256]{1,0:T(8,128)(2,1)S(1)}, u32[]{:S(2)}, u32[]{:S(2)}) %collective-permute-start.14) | collective-permute-done | bytes 131104 | tf_op jit(solution)/shard_map/ppermute | solution.py:202
  89.8 0.0 collective-permute-done.15
  89.8 3.9 %collective-permute-done.16 = bf16[256,256]{1,0:T(8,128)(2,1)S(1)} collective-permute-done((bf16[256,256]{1,0:T(8,128)(2,1)S(1)}, bf16[256,256]{1,0:T(8,128)(2,1)S(1)}, u32[]{:S(2)}, u32[]{:S(2)}) %collective-permute-start.16) | collective-permute-done | bytes 131104 | tf_op jit(solution)/shard_map/ppermute | solution.py:202
  93.7 0.8 fusion.5
  (10 shorter events, 0.2 us)
Async XLA Ops:
  0.0 13.2 %copy-start.1 = (s32[1,1,24]{2,1,0:T(1,128)S(1)}, s32[1,1,24]{2,1,0:T(1,128)}, u32[]{:S(2)}) copy-start(s32[1,1,24]{2,1,0:T(1,128)} %param.6) | copy-start | bytes 292
  0.0 13.2 %copy-start = (s32[1,1,24]{2,1,0:T(1,128)S(1)}, s32[1,1,24]{2,1,0:T(1,128)}, u32[]{:S(2)}) copy-start(s32[1,1,24]{2,1,0:T(1,128)} %param.7) | copy-start | bytes 292
  0.0 9.3 %collective-permute-start = (bf16[256,256]{1,0:T(8,128)(2,1)}, bf16[256,256]{1,0:T(8,128)(2,1)S(1)}, u32[]{:S(2)}, u32[]{:S(2)}) collective-permute-start(bf16[256,256]{1,0:T(8,128)(2,1)} %basis.1), channel_id=1, source_target_pairs={{0,64},{32,96},{64,128},{96,160},{128,192},{160,224},{192,0},{224,... | collective-permute-start | bytes 393224 | tf_op jit(solution)/shard_map/ppermute | solution.py:157
  2.1 8.9 %collective-permute-start.1 = (bf16[256,256]{1,0:T(8,128)(2,1)}, bf16[256,256]{1,0:T(8,128)(2,1)S(1)}, u32[]{:S(2)}, u32[]{:S(2)}) collective-permute-start(bf16[256,256]{1,0:T(8,128)(2,1)} %basis.1), channel_id=1, source_target_pairs={{0,192},{32,224},{64,0},{96,32},{128,64},{160,96},{192,128},{224,1... | collective-permute-start | bytes 393224 | tf_op jit(solution)/shard_map/ppermute | solution.py:157
  3.7 7.8 %collective-permute-start.2 = (bf16[256,256]{1,0:T(8,128)(2,1)}, bf16[256,256]{1,0:T(8,128)(2,1)S(1)}, u32[]{:S(2)}, u32[]{:S(2)}) collective-permute-start(bf16[256,256]{1,0:T(8,128)(2,1)} %basis.1), channel_id=1, source_target_pairs={{0,128},{32,160},{64,192},{96,224},{128,0},{160,32},{192,64},{224,... | collective-permute-start | bytes 393224 | tf_op jit(solution)/shard_map/ppermute | solution.py:157
  5.2 8.0 %collective-permute-start.3 = (bf16[256,256]{1,0:T(8,128)(2,1)}, bf16[256,256]{1,0:T(8,128)(2,1)S(1)}, u32[]{:S(2)}, u32[]{:S(2)}) collective-permute-start(bf16[256,256]{1,0:T(8,128)(2,1)} %basis.1), channel_id=1, source_target_pairs={{0,32},{32,0},{64,96},{96,64},{128,160},{160,128},{192,224},{224,1... | collective-permute-start | bytes 393224 | tf_op jit(solution)/shard_map/ppermute | solution.py:160
  9.3 3.9 %collective-permute-start.4 = (bf16[256,256]{1,0:T(8,128)(2,1)S(1)}, bf16[256,256]{1,0:T(8,128)(2,1)S(1)}, u32[]{:S(2)}, u32[]{:S(2)}) collective-permute-start(bf16[256,256]{1,0:T(8,128)(2,1)S(1)} %collective-permute-done.refs_1_), channel_id=1, source_target_pairs={{0,32},{32,0},{64,96},{96,64},{128,160},{160,128},{192,224},{224,1... | collective-permute-start | bytes 393224 | tf_op jit(solution)/shard_map/ppermute | solution.py:160
  11.0 2.2 %collective-permute-start.5 = (bf16[256,256]{1,0:T(8,128)(2,1)S(1)}, bf16[256,256]{1,0:T(8,128)(2,1)S(1)}, u32[]{:S(2)}, u32[]{:S(2)}) collective-permute-start(bf16[256,256]{1,0:T(8,128)(2,1)S(1)} %collective-permute-done.1.refs_2_), channel_id=1, source_target_pairs={{0,32},{32,0},{64,96},{96,64},{128,160},{160,128},{192,224},{224,1... | collective-permute-start | bytes 393224 | tf_op jit(solution)/shard_map/ppermute | solution.py:160
  11.4 2.7 %collective-permute-start.6 = (bf16[256,256]{1,0:T(8,128)(2,1)S(1)}, bf16[256,256]{1,0:T(8,128)(2,1)S(1)}, u32[]{:S(2)}, u32[]{:S(2)}) collective-permute-start(bf16[256,256]{1,0:T(8,128)(2,1)S(1)} %collective-permute-done.2.refs_3_), channel_id=1, source_target_pairs={{0,32},{32,0},{64,96},{96,64},{128,160},{160,128},{192,224},{224,1... | collective-permute-start | bytes 393224 | tf_op jit(solution)/shard_map/ppermute | solution.py:160
  16.0 8.1 %collective-permute-start.7 = (f16[520,256]{1,0:T(8,128)(2,1)S(1)}, f16[520,256]{1,0:T(8,128)(2,1)S(1)}, u32[]{:S(2)}, u32[]{:S(2)}) collective-permute-start(f16[520,256]{1,0:T(8,128)(2,1)S(1)} %convert_element_type.78), channel_id=1, source_target_pairs={{0,1},{1,2},{2,3},{3,0},{4,5},{5,6},{6,7},{7,4},{8,9},{9,10},{10,1... | collective-permute-start | bytes 798728 | tf_op jit(solution)/shard_map/ppermute | solution.py:172
  16.3 7.8 %collective-permute-start.8 = (f16[520,256]{1,0:T(8,128)(2,1)S(1)}, f16[520,256]{1,0:T(8,128)(2,1)S(1)}, u32[]{:S(2)}, u32[]{:S(2)}) collective-permute-start(f16[520,256]{1,0:T(8,128)(2,1)S(1)} %convert_element_type.81), channel_id=1, source_target_pairs={{0,3},{1,0},{2,1},{3,2},{4,7},{5,4},{6,5},{7,6},{8,11},{9,8},{10,9... | collective-permute-start | bytes 798728 | tf_op jit(solution)/shard_map/ppermute | solution.py:172
  18.9 11.7 %collective-permute-start.9 = (f16[520,256]{1,0:T(8,128)(2,1)S(1)}, f16[520,256]{1,0:T(8,128)(2,1)S(1)}, u32[]{:S(2)}, u32[]{:S(2)}) collective-permute-start(f16[520,256]{1,0:T(8,128)(2,1)S(1)} %convert_element_type.84), channel_id=1, source_target_pairs={{0,2},{1,3},{2,0},{3,1},{4,6},{5,7},{6,4},{7,5},{8,10},{9,11},{10,... | collective-permute-start | bytes 798728 | tf_op jit(solution)/shard_map/ppermute | solution.py:172
  63.5 6.4 %collective-permute-start.10 = (bf16[2,256,256]{2,1,0:T(8,128)(2,1)S(1)}, bf16[2,256,256]{2,1,0:T(8,128)(2,1)S(1)}, u32[]{:S(2)}, u32[]{:S(2)}) collective-permute-start(bf16[2,256,256]{2,1,0:T(8,128)(2,1)S(1)} %bitcast.32), channel_id=1, source_target_pairs={{0,1},{1,2},{2,3},{3,0},{4,5},{5,6},{6,7},{7,4},{8,9},{9,10},{10,1... | collective-permute-start | bytes 786440 | tf_op jit(solution)/shard_map/ppermute | solution.py:191
  64.5 6.6 %collective-permute-start.11 = (bf16[2,256,256]{2,1,0:T(8,128)(2,1)S(1)}, bf16[2,256,256]{2,1,0:T(8,128)(2,1)S(1)}, u32[]{:S(2)}, u32[]{:S(2)}) collective-permute-start(bf16[2,256,256]{2,1,0:T(8,128)(2,1)S(1)} %bitcast.33), channel_id=1, source_target_pairs={{0,3},{1,0},{2,1},{3,2},{4,7},{5,4},{6,5},{7,6},{8,11},{9,8},{10,9... | collective-permute-start | bytes 786440 | tf_op jit(solution)/shard_map/ppermute | solution.py:191
  66.2 9.4 %collective-permute-start.12 = (bf16[2,256,256]{2,1,0:T(8,128)(2,1)S(1)}, bf16[2,256,256]{2,1,0:T(8,128)(2,1)S(1)}, u32[]{:S(2)}, u32[]{:S(2)}) collective-permute-start(bf16[2,256,256]{2,1,0:T(8,128)(2,1)S(1)} %bitcast.34), channel_id=1, source_target_pairs={{0,2},{1,3},{2,0},{3,1},{4,6},{5,7},{6,4},{7,5},{8,10},{9,11},{10,... | collective-permute-start | bytes 786440 | tf_op jit(solution)/shard_map/ppermute | solution.py:191
  77.2 6.4 %collective-permute-start.13 = (bf16[4,256,256]{2,1,0:T(8,128)(2,1)S(1)}, bf16[4,256,256]{2,1,0:T(8,128)(2,1)S(1)}, u32[]{:S(2)}, u32[]{:S(2)}) collective-permute-start(bf16[4,256,256]{2,1,0:T(8,128)(2,1)S(1)} %get-tuple-element.28), channel_id=1, source_target_pairs={{0,32},{32,0},{64,96},{96,64},{128,160},{160,128},{192,224},{224,1... | collective-permute-start | bytes 1572872 | tf_op jit(solution)/shard_map/ppermute | solution.py:199
  83.8 6.0 %collective-permute-start.14 = (bf16[256,256]{1,0:T(8,128)(2,1)S(1)}, bf16[256,256]{1,0:T(8,128)(2,1)S(1)}, u32[]{:S(2)}, u32[]{:S(2)}) collective-permute-start(bf16[256,256]{1,0:T(8,128)(2,1)S(1)} %get-tuple-element.31), channel_id=1, source_target_pairs={{0,64},{32,96},{64,128},{96,160},{128,192},{160,224},{192,0},{224,... | collective-permute-start | bytes 393224 | tf_op jit(solution)/shard_map/ppermute | solution.py:202
  83.9 5.9 %collective-permute-start.15 = (bf16[256,256]{1,0:T(8,128)(2,1)S(1)}, bf16[256,256]{1,0:T(8,128)(2,1)S(1)}, u32[]{:S(2)}, u32[]{:S(2)}) collective-permute-start(bf16[256,256]{1,0:T(8,128)(2,1)S(1)} %get-tuple-element.33), channel_id=1, source_target_pairs={{0,192},{32,224},{64,0},{96,32},{128,64},{160,96},{192,128},{224,1... | collective-permute-start | bytes 393224 | tf_op jit(solution)/shard_map/ppermute | solution.py:202
  86.5 7.1 %collective-permute-start.16 = (bf16[256,256]{1,0:T(8,128)(2,1)S(1)}, bf16[256,256]{1,0:T(8,128)(2,1)S(1)}, u32[]{:S(2)}, u32[]{:S(2)}) collective-permute-start(bf16[256,256]{1,0:T(8,128)(2,1)S(1)} %get-tuple-element.32), channel_id=1, source_target_pairs={{0,128},{32,160},{64,192},{96,224},{128,0},{160,32},{192,64},{224,... | collective-permute-start | bytes 393224 | tf_op jit(solution)/shard_map/ppermute | solution.py:202

commit v7 on v5

--- a/solution.py
+++ b/solution.py
@@ -11,7 +11,7 @@
 CORES = 2
 NX = 4
 UNROLL = 8
-SHIFTS_A, SHIFTS_B, SHIFTS_C, SHIFTS_D = (1, 3, 2), (1, 3, 2), (1, 3, 2), (1, 3, 2)
+SHIFTS_A, SHIFTS_B, SHIFTS_C, SHIFTS_D = (1, 3, 2), (1, 3, 2), (2, 1, 3), (2, 1, 3)
 TOP = 13.0
 LEAST = -100.0
 EXTRA = 8

time: 94.5 us -> 92.9 us (0.983)
  starting transfers between devices: 21.5 us -> 25.3 us
  blocking collectives: 32.7 us -> 29.2 us
  waiting for transfers between devices: 29.5 us -> 28.4 us
    all_to_all x1, blocking collectives: 20.2 us -> 16.5 us  [body(): lax.all_to_all(parts, 'col', 0, 0, tiled=True, axis_index_groups=z_groups...]
    ppermute x3, starting transfers between devices: 2.68 us -> 5.28 us  [body(): lax.ppermute(chunk, 'col', shift_x(n_col, d))]
    ppermute x3, waiting for transfers between devices: 9.74 us -> 7.61 us  [body(): lax.ppermute(chunk, 'col', shift_x(n_col, d))]
    ppermute x3, waiting for transfers between devices: 5.32 us -> 6.31 us  [body(): lax.ppermute(pick(d).astype(BF16), 'row', shift_y(n_row, d))]
  transfers between devices with their start and end apart: 17 -> 17, of which waited for: 9 -> 8; matrix products, arithmetic and copies ran while one was open for 0% -> 0% of each run, Pallas kernels for 2% -> 2%
where the time goes in v7:
time: 92.9 us; the launch traced here: 92.2 us
  blocking collectives  29.2 us (31%)
  waiting for transfers between devices  28.4 us (31%)
  starting transfers between devices  25.3 us (27%)
  Pallas kernels  6.93 us (7%)
  other arithmetic  1.41 us (2%)
    all_to_all x1, blocking collectives, body(): lax.all_to_all(parts, 'col', 0, 0, tiled=True, axis_index_groups=z_groups...  16.5 us
    all_to_all x1, blocking collectives, body(): lax.all_to_all(copies, 'col', 0, 0, tiled=True, axis_index_groups=z_group...  12.7 us
    ppermute x3, waiting for transfers between devices, body(): lax.ppermute(s.astype(F16), 'col', shift_x(n_col, d))  12 us
    ppermute x3, waiting for transfers between devices, body(): lax.ppermute(chunk, 'col', shift_x(n_col, d))  7.61 us
    ppermute x3, waiting for transfers between devices, body(): lax.ppermute(pick(d).astype(BF16), 'row', shift_y(n_row, d))  6.31 us
    ppermute x4, starting transfers between devices, body(): other = [lax.ppermute(p, 'row', swap_core(n_row)) for p in mine]  5.37 us
    ppermute x3, starting transfers between devices, body(): lax.ppermute(chunk, 'col', shift_x(n_col, d))  5.28 us
    ppermute x3, starting transfers between devices, body(): lax.ppermute(basis, 'row', shift_y(n_row, d))  5.21 us
  transfers between devices with their start and end apart: 17, of which 8 were waited for; matrix products, arithmetic and copies ran while one was open for 0% of the time, Pallas kernels for 2%

profile of v7, /device:TPU:1, one launch (start us, length us, event | category | flops | bytes accessed | tf_op | source)
XLA Modules:
  0.0 92.2 jit_solution(9292384302571205730)
XLA Ops:
  0.0 0.0 copy-start.1
  0.0 0.0 copy-start
  0.0 2.1 %collective-permute-start = (bf16[256,256]{1,0:T(8,128)(2,1)}, bf16[256,256]{1,0:T(8,128)(2,1)S(1)}, u32[]{:S(2)}, u32[]{:S(2)}) collective-permute-start(bf16[256,256]{1,0:T(8,128)(2,1)} %basis.1), channel_id=1, source_target_pairs={{0,64},{32,96},{64,128},{96,160},{128,192},{160,224},{192,0},{224,... | collective-permute-start | bytes 393224 | tf_op jit(solution)/shard_map/ppermute | solution.py:157
  2.1 1.5 %collective-permute-start.1 = (bf16[256,256]{1,0:T(8,128)(2,1)}, bf16[256,256]{1,0:T(8,128)(2,1)S(1)}, u32[]{:S(2)}, u32[]{:S(2)}) collective-permute-start(bf16[256,256]{1,0:T(8,128)(2,1)} %basis.1), channel_id=1, source_target_pairs={{0,192},{32,224},{64,0},{96,32},{128,64},{160,96},{192,128},{224,1... | collective-permute-start | bytes 393224 | tf_op jit(solution)/shard_map/ppermute | solution.py:157
  3.7 1.6 %collective-permute-start.2 = (bf16[256,256]{1,0:T(8,128)(2,1)}, bf16[256,256]{1,0:T(8,128)(2,1)S(1)}, u32[]{:S(2)}, u32[]{:S(2)}) collective-permute-start(bf16[256,256]{1,0:T(8,128)(2,1)} %basis.1), channel_id=1, source_target_pairs={{0,128},{32,160},{64,192},{96,224},{128,0},{160,32},{192,64},{224,... | collective-permute-start | bytes 393224 | tf_op jit(solution)/shard_map/ppermute | solution.py:157
  5.2 1.5 %collective-permute-start.3 = (bf16[256,256]{1,0:T(8,128)(2,1)}, bf16[256,256]{1,0:T(8,128)(2,1)S(1)}, u32[]{:S(2)}, u32[]{:S(2)}) collective-permute-start(bf16[256,256]{1,0:T(8,128)(2,1)} %basis.1), channel_id=1, source_target_pairs={{0,32},{32,0},{64,96},{96,64},{128,160},{160,128},{192,224},{224,1... | collective-permute-start | bytes 393224 | tf_op jit(solution)/shard_map/ppermute | solution.py:160
  6.7 1.9 %shard_map.55 = (bf16[1,1,24,256,256]{4,3,2,1,0:T(8,128)(2,1)S(1)}, bf16[256,256]{1,0:T(8,128)(2,1)S(1)}) custom-call(bf16[1,1,24,256,256]{4,3,2,1,0:T(8,128)(2,1)} %blocks.1, bf16[256,256]{1,0:T(8,128)(2,1)} %basis.1), custom_call_target="tpu_custom_call" | custom-call | bytes 8388608 | tf_op jit(solution)/shard_map/pallas_call | solution.py:65
  9.3 0.0 collective-permute-done.refs_1_
  9.3 1.7 %collective-permute-start.4 = (bf16[256,256]{1,0:T(8,128)(2,1)S(1)}, bf16[256,256]{1,0:T(8,128)(2,1)S(1)}, u32[]{:S(2)}, u32[]{:S(2)}) collective-permute-start(bf16[256,256]{1,0:T(8,128)(2,1)S(1)} %collective-permute-done.refs_1_), channel_id=1, source_target_pairs={{0,32},{32,0},{64,96},{96,64},{128,160},{160,128},{192,224},{224,1... | collective-permute-start | bytes 393224 | tf_op jit(solution)/shard_map/ppermute | solution.py:160
  11.0 0.0 collective-permute-done.1.refs_2_
  11.0 0.4 collective-permute-start.5
  11.4 0.0 collective-permute-done.2.refs_3_
  11.4 1.7 %collective-permute-start.6 = (bf16[256,256]{1,0:T(8,128)(2,1)S(1)}, bf16[256,256]{1,0:T(8,128)(2,1)S(1)}, u32[]{:S(2)}, u32[]{:S(2)}) collective-permute-start(bf16[256,256]{1,0:T(8,128)(2,1)S(1)} %collective-permute-done.2.refs_3_), channel_id=1, source_target_pairs={{0,32},{32,0},{64,96},{96,64},{128,160},{160,128},{192,224},{224,1... | collective-permute-start | bytes 393224 | tf_op jit(solution)/shard_map/ppermute | solution.py:160
  13.2 0.0 copy-done.1
  13.2 0.0 copy-done
  13.2 0.0 collective-permute-done.3.refs_4_
  13.2 0.0 collective-permute-done.4.refs_5_
  13.2 0.0 collective-permute-done.5.refs_6_
  13.2 0.9 %collective-permute-done.6.refs_7_ = bf16[256,256]{1,0:T(8,128)(2,1)S(1)} collective-permute-done((bf16[256,256]{1,0:T(8,128)(2,1)S(1)}, bf16[256,256]{1,0:T(8,128)(2,1)S(1)}, u32[]{:S(2)}, u32[]{:S(2)}) %collective-permute-start.6) | collective-permute-done | bytes 131104 | tf_op jit(solution)/shard_map/ppermute | solution.py:160
  14.2 2.6 %shard_map.56 = (f32[8,256]{1,0:T(8,128)S(1)}, f32[2,256,256]{2,1,0:T(8,128)S(1)}, f32[520,256]{1,0:T(8,128)S(1)}, f32[520,256]{1,0:T(8,128)S(1)}, f32[520,256]{1,0:T(8,128)S(1)}) custom-call(s32[24]{0:T(128)S(1)} %add_bitcast_fusion.table, s32[1,1]{1,0:T(1,128)S(6)} %copy.10.count, bf16[1,1,24,256,256]{4,3,2,1,0:T(8,128)(2,1)S(1)} %get-tuple-element.19.blocks, ...), custom_call_target="tpu_custom_call" | custom-call | flops 805306368 | bytes 1048576 | tf_op jit(solution)/shard_map/pallas_call | solution.py:141
  16.8 0.3 collective-permute-start.7
  17.2 2.5 %collective-permute-start.8 = (f16[520,256]{1,0:T(8,128)(2,1)S(1)}, f16[520,256]{1,0:T(8,128)(2,1)S(1)}, u32[]{:S(2)}, u32[]{:S(2)}) collective-permute-start(f16[520,256]{1,0:T(8,128)(2,1)S(1)} %convert_element_type.81), channel_id=1, source_target_pairs={{0,3},{1,0},{2,1},{3,2},{4,7},{5,4},{6,5},{7,6},{8,11},{9,8},{10,9... | collective-permute-start | bytes 798728 | tf_op jit(solution)/shard_map/ppermute | solution.py:172
  19.7 0.1 collective-permute-start.9
  19.8 12.0 %collective-permute-done.7 = f16[520,256]{1,0:T(8,128)(2,1)S(1)} collective-permute-done((f16[520,256]{1,0:T(8,128)(2,1)S(1)}, f16[520,256]{1,0:T(8,128)(2,1)S(1)}, u32[]{:S(2)}, u32[]{:S(2)}) %collective-permute-start.7) | collective-permute-done | bytes 266272 | tf_op jit(solution)/shard_map/ppermute | solution.py:172
  31.8 0.0 collective-permute-done.8
  31.8 0.0 collective-permute-done.9
  31.8 0.2 fusion.3
  32.1 0.1 pad_maximum_fusion
  32.2 16.5 %all_to_all.10 = f16[8,72,256]{2,1,0:T(8,128)(2,1)S(1)} all-to-all(f16[8,72,256]{2,1,0:T(8,128)(2,1)S(1)} %pad_maximum_fusion), channel_id=1, replica_groups={{0,4,8,12,16,20,24,28},{1,5,9,13,17,21,25,29},{2,6,10,14,18,22,26,30},{..., dimensions={0} | all-to-all | bytes 589824 | tf_op jit(solution)/shard_map/all_to_all | solution.py:184
  48.8 0.1 multiply_reduce_fusion
  48.8 12.7 %all_to_all.11 = bf16[8,64,256]{2,1,0:T(8,128)(2,1)S(1)} all-to-all(bf16[8,64,256]{2,1,0:T(8,128)(2,1)S(1)} %broadcast_in_dim.5), channel_id=1, replica_groups={{0,4,8,12,16,20,24,28},{1,5,9,13,17,21,25,29},{2,6,10,14,18,22,26,30},{..., dimensions={0} | all-to-all | bytes 524288 | tf_op jit(solution)/shard_map/all_to_all | solution.py:189
  61.5 2.6 %collective-permute-start.10 = (bf16[2,256,256]{2,1,0:T(8,128)(2,1)S(1)}, bf16[2,256,256]{2,1,0:T(8,128)(2,1)S(1)}, u32[]{:S(2)}, u32[]{:S(2)}) collective-permute-start(bf16[2,256,256]{2,1,0:T(8,128)(2,1)S(1)} %bitcast.32), channel_id=1, source_target_pairs={{0,2},{1,3},{2,0},{3,1},{4,6},{5,7},{6,4},{7,5},{8,10},{9,11},{10,... | collective-permute-start | bytes 786440 | tf_op jit(solution)/shard_map/ppermute | solution.py:191
  64.1 1.3 %collective-permute-start.11 = (bf16[2,256,256]{2,1,0:T(8,128)(2,1)S(1)}, bf16[2,256,256]{2,1,0:T(8,128)(2,1)S(1)}, u32[]{:S(2)}, u32[]{:S(2)}) collective-permute-start(bf16[2,256,256]{2,1,0:T(8,128)(2,1)S(1)} %bitcast.33), channel_id=1, source_target_pairs={{0,1},{1,2},{2,3},{3,0},{4,5},{5,6},{6,7},{7,4},{8,9},{9,10},{10,1... | collective-permute-start | bytes 786440 | tf_op jit(solution)/shard_map/ppermute | solution.py:191
  65.5 1.4 %collective-permute-start.12 = (bf16[2,256,256]{2,1,0:T(8,128)(2,1)S(1)}, bf16[2,256,256]{2,1,0:T(8,128)(2,1)S(1)}, u32[]{:S(2)}, u32[]{:S(2)}) collective-permute-start(bf16[2,256,256]{2,1,0:T(8,128)(2,1)S(1)} %bitcast.34), channel_id=1, source_target_pairs={{0,3},{1,0},{2,1},{3,2},{4,7},{5,4},{6,5},{7,6},{8,11},{9,8},{10,9... | collective-permute-start | bytes 786440 | tf_op jit(solution)/shard_map/ppermute | solution.py:191
  66.8 1.5 %collective-permute-done.10.refs_1_ = bf16[2,256,256]{2,1,0:T(8,128)(2,1)S(1)} collective-permute-done((bf16[2,256,256]{2,1,0:T(8,128)(2,1)S(1)}, bf16[2,256,256]{2,1,0:T(8,128)(2,1)S(1)}, u32[]{:S(2)}, u32[]{:S(2)}) %collective-permute-start.10) | collective-permute-done | bytes 262176 | tf_op jit(solution)/shard_map/ppermute | solution.py:191
  68.3 4.4 %collective-permute-done.11.refs_2_ = bf16[2,256,256]{2,1,0:T(8,128)(2,1)S(1)} collective-permute-done((bf16[2,256,256]{2,1,0:T(8,128)(2,1)S(1)}, bf16[2,256,256]{2,1,0:T(8,128)(2,1)S(1)}, u32[]{:S(2)}, u32[]{:S(2)}) %collective-permute-start.11) | collective-permute-done | bytes 262176 | tf_op jit(solution)/shard_map/ppermute | solution.py:191
  72.7 1.8 %collective-permute-done.12.refs_3_ = bf16[2,256,256]{2,1,0:T(8,128)(2,1)S(1)} collective-permute-done((bf16[2,256,256]{2,1,0:T(8,128)(2,1)S(1)}, bf16[2,256,256]{2,1,0:T(8,128)(2,1)S(1)}, u32[]{:S(2)}, u32[]{:S(2)}) %collective-permute-start.12) | collective-permute-done | bytes 262176 | tf_op jit(solution)/shard_map/ppermute | solution.py:191
  74.4 2.4 %shard_map.57 = (f32[4,256,256]{2,1,0:T(8,128)S(1)}, bf16[4,256,256]{2,1,0:T(8,128)(2,1)S(1)}) custom-call(s32[24]{0:T(128)S(1)} %add_bitcast_fusion.table, s32[1,1]{1,0:T(1,128)S(6)} %copy.10.count, bf16[1,1,24,256,256]{4,3,2,1,0:T(8,128)(2,1)S(1)} %get-tuple-element.19.blocks, bf16[2,256,256]{2,1,0:T(8,128)(2,1)S(1)} %bitcast.35, ...), custom_call_target="tpu_custom_call" | custom-call | flops 805306368 | bytes 1048576 | tf_op jit(solution)/shard_map/pallas_call | solution.py:141
  76.9 3.0 %collective-permute-start.13 = (bf16[4,256,256]{2,1,0:T(8,128)(2,1)S(1)}, bf16[4,256,256]{2,1,0:T(8,128)(2,1)S(1)}, u32[]{:S(2)}, u32[]{:S(2)}) collective-permute-start(bf16[4,256,256]{2,1,0:T(8,128)(2,1)S(1)} %get-tuple-element.28), channel_id=1, source_target_pairs={{0,32},{32,0},{64,96},{96,64},{128,160},{160,128},{192,224},{224,1... | collective-permute-start | bytes 1572872 | tf_op jit(solution)/shard_map/ppermute | solution.py:199
  79.9 1.5 %collective-permute-done.13 = bf16[4,256,256]{2,1,0:T(8,128)(2,1)S(1)} collective-permute-done((bf16[4,256,256]{2,1,0:T(8,128)(2,1)S(1)}, bf16[4,256,256]{2,1,0:T(8,128)(2,1)S(1)}, u32[]{:S(2)}, u32[]{:S(2)}) %collective-permute-start.13) | collective-permute-done | bytes 524320 | tf_op jit(solution)/shard_map/ppermute | solution.py:199
  81.4 0.1 convert_add_fusion
  81.5 0.1 fusion.6
  81.6 0.7 collective-permute-start.14
  82.3 2.8 %collective-permute-start.15 = (bf16[256,256]{1,0:T(8,128)(2,1)S(1)}, bf16[256,256]{1,0:T(8,128)(2,1)S(1)}, u32[]{:S(2)}, u32[]{:S(2)}) collective-permute-start(bf16[256,256]{1,0:T(8,128)(2,1)S(1)} %get-tuple-element.33), channel_id=1, source_target_pairs={{0,64},{32,96},{64,128},{96,160},{128,192},{160,224},{192,0},{224,... | collective-permute-start | bytes 393224 | tf_op jit(solution)/shard_map/ppermute | solution.py:202
  85.1 0.0 collective-permute-start.16
  85.1 2.8 %collective-permute-done.14 = bf16[256,256]{1,0:T(8,128)(2,1)S(1)} collective-permute-done((bf16[256,256]{1,0:T(8,128)(2,1)S(1)}, bf16[256,256]{1,0:T(8,128)(2,1)S(1)}, u32[]{:S(2)}, u32[]{:S(2)}) %collective-permute-start.14) | collective-permute-done | bytes 131104 | tf_op jit(solution)/shard_map/ppermute | solution.py:202
  87.9 3.5 %collective-permute-done.15 = bf16[256,256]{1,0:T(8,128)(2,1)S(1)} collective-permute-done((bf16[256,256]{1,0:T(8,128)(2,1)S(1)}, bf16[256,256]{1,0:T(8,128)(2,1)S(1)}, u32[]{:S(2)}, u32[]{:S(2)}) %collective-permute-start.15) | collective-permute-done | bytes 131104 | tf_op jit(solution)/shard_map/ppermute | solution.py:202
  91.4 0.0 collective-permute-done.16
  91.4 0.8 fusion.5
  (10 shorter events, 0.2 us)
Async XLA Ops:
  0.0 13.2 %copy-start.1 = (s32[1,1,24]{2,1,0:T(1,128)S(1)}, s32[1,1,24]{2,1,0:T(1,128)}, u32[]{:S(2)}) copy-start(s32[1,1,24]{2,1,0:T(1,128)} %param.6) | copy-start | bytes 292
  0.0 13.2 %copy-start = (s32[1,1,24]{2,1,0:T(1,128)S(1)}, s32[1,1,24]{2,1,0:T(1,128)}, u32[]{:S(2)}) copy-start(s32[1,1,24]{2,1,0:T(1,128)} %param.7) | copy-start | bytes 292
  0.0 9.3 %collective-permute-start = (bf16[256,256]{1,0:T(8,128)(2,1)}, bf16[256,256]{1,0:T(8,128)(2,1)S(1)}, u32[]{:S(2)}, u32[]{:S(2)}) collective-permute-start(bf16[256,256]{1,0:T(8,128)(2,1)} %basis.1), channel_id=1, source_target_pairs={{0,64},{32,96},{64,128},{96,160},{128,192},{160,224},{192,0},{224,... | collective-permute-start | bytes 393224 | tf_op jit(solution)/shard_map/ppermute | solution.py:157
  2.1 8.9 %collective-permute-start.1 = (bf16[256,256]{1,0:T(8,128)(2,1)}, bf16[256,256]{1,0:T(8,128)(2,1)S(1)}, u32[]{:S(2)}, u32[]{:S(2)}) collective-permute-start(bf16[256,256]{1,0:T(8,128)(2,1)} %basis.1), channel_id=1, source_target_pairs={{0,192},{32,224},{64,0},{96,32},{128,64},{160,96},{192,128},{224,1... | collective-permute-start | bytes 393224 | tf_op jit(solution)/shard_map/ppermute | solution.py:157
  3.7 7.8 %collective-permute-start.2 = (bf16[256,256]{1,0:T(8,128)(2,1)}, bf16[256,256]{1,0:T(8,128)(2,1)S(1)}, u32[]{:S(2)}, u32[]{:S(2)}) collective-permute-start(bf16[256,256]{1,0:T(8,128)(2,1)} %basis.1), channel_id=1, source_target_pairs={{0,128},{32,160},{64,192},{96,224},{128,0},{160,32},{192,64},{224,... | collective-permute-start | bytes 393224 | tf_op jit(solution)/shard_map/ppermute | solution.py:157
  5.2 8.0 %collective-permute-start.3 = (bf16[256,256]{1,0:T(8,128)(2,1)}, bf16[256,256]{1,0:T(8,128)(2,1)S(1)}, u32[]{:S(2)}, u32[]{:S(2)}) collective-permute-start(bf16[256,256]{1,0:T(8,128)(2,1)} %basis.1), channel_id=1, source_target_pairs={{0,32},{32,0},{64,96},{96,64},{128,160},{160,128},{192,224},{224,1... | collective-permute-start | bytes 393224 | tf_op jit(solution)/shard_map/ppermute | solution.py:160
  9.3 3.9 %collective-permute-start.4 = (bf16[256,256]{1,0:T(8,128)(2,1)S(1)}, bf16[256,256]{1,0:T(8,128)(2,1)S(1)}, u32[]{:S(2)}, u32[]{:S(2)}) collective-permute-start(bf16[256,256]{1,0:T(8,128)(2,1)S(1)} %collective-permute-done.refs_1_), channel_id=1, source_target_pairs={{0,32},{32,0},{64,96},{96,64},{128,160},{160,128},{192,224},{224,1... | collective-permute-start | bytes 393224 | tf_op jit(solution)/shard_map/ppermute | solution.py:160
  11.0 2.2 %collective-permute-start.5 = (bf16[256,256]{1,0:T(8,128)(2,1)S(1)}, bf16[256,256]{1,0:T(8,128)(2,1)S(1)}, u32[]{:S(2)}, u32[]{:S(2)}) collective-permute-start(bf16[256,256]{1,0:T(8,128)(2,1)S(1)} %collective-permute-done.1.refs_2_), channel_id=1, source_target_pairs={{0,32},{32,0},{64,96},{96,64},{128,160},{160,128},{192,224},{224,1... | collective-permute-start | bytes 393224 | tf_op jit(solution)/shard_map/ppermute | solution.py:160
  11.4 2.7 %collective-permute-start.6 = (bf16[256,256]{1,0:T(8,128)(2,1)S(1)}, bf16[256,256]{1,0:T(8,128)(2,1)S(1)}, u32[]{:S(2)}, u32[]{:S(2)}) collective-permute-start(bf16[256,256]{1,0:T(8,128)(2,1)S(1)} %collective-permute-done.2.refs_3_), channel_id=1, source_target_pairs={{0,32},{32,0},{64,96},{96,64},{128,160},{160,128},{192,224},{224,1... | collective-permute-start | bytes 393224 | tf_op jit(solution)/shard_map/ppermute | solution.py:160
  16.8 15.0 %collective-permute-start.7 = (f16[520,256]{1,0:T(8,128)(2,1)S(1)}, f16[520,256]{1,0:T(8,128)(2,1)S(1)}, u32[]{:S(2)}, u32[]{:S(2)}) collective-permute-start(f16[520,256]{1,0:T(8,128)(2,1)S(1)} %convert_element_type.78), channel_id=1, source_target_pairs={{0,1},{1,2},{2,3},{3,0},{4,5},{5,6},{6,7},{7,4},{8,9},{9,10},{10,1... | collective-permute-start | bytes 798728 | tf_op jit(solution)/shard_map/ppermute | solution.py:172
  17.2 14.6 %collective-permute-start.8 = (f16[520,256]{1,0:T(8,128)(2,1)S(1)}, f16[520,256]{1,0:T(8,128)(2,1)S(1)}, u32[]{:S(2)}, u32[]{:S(2)}) collective-permute-start(f16[520,256]{1,0:T(8,128)(2,1)S(1)} %convert_element_type.81), channel_id=1, source_target_pairs={{0,3},{1,0},{2,1},{3,2},{4,7},{5,4},{6,5},{7,6},{8,11},{9,8},{10,9... | collective-permute-start | bytes 798728 | tf_op jit(solution)/shard_map/ppermute | solution.py:172
  19.7 12.1 %collective-permute-start.9 = (f16[520,256]{1,0:T(8,128)(2,1)S(1)}, f16[520,256]{1,0:T(8,128)(2,1)S(1)}, u32[]{:S(2)}, u32[]{:S(2)}) collective-permute-start(f16[520,256]{1,0:T(8,128)(2,1)S(1)} %convert_element_type.84), channel_id=1, source_target_pairs={{0,2},{1,3},{2,0},{3,1},{4,6},{5,7},{6,4},{7,5},{8,10},{9,11},{10,... | collective-permute-start | bytes 798728 | tf_op jit(solution)/shard_map/ppermute | solution.py:172
  61.5 6.8 %collective-permute-start.10 = (bf16[2,256,256]{2,1,0:T(8,128)(2,1)S(1)}, bf16[2,256,256]{2,1,0:T(8,128)(2,1)S(1)}, u32[]{:S(2)}, u32[]{:S(2)}) collective-permute-start(bf16[2,256,256]{2,1,0:T(8,128)(2,1)S(1)} %bitcast.32), channel_id=1, source_target_pairs={{0,2},{1,3},{2,0},{3,1},{4,6},{5,7},{6,4},{7,5},{8,10},{9,11},{10,... | collective-permute-start | bytes 786440 | tf_op jit(solution)/shard_map/ppermute | solution.py:191
  64.1 8.5 %collective-permute-start.11 = (bf16[2,256,256]{2,1,0:T(8,128)(2,1)S(1)}, bf16[2,256,256]{2,1,0:T(8,128)(2,1)S(1)}, u32[]{:S(2)}, u32[]{:S(2)}) collective-permute-start(bf16[2,256,256]{2,1,0:T(8,128)(2,1)S(1)} %bitcast.33), channel_id=1, source_target_pairs={{0,1},{1,2},{2,3},{3,0},{4,5},{5,6},{6,7},{7,4},{8,9},{9,10},{10,1... | collective-permute-start | bytes 786440 | tf_op jit(solution)/shard_map/ppermute | solution.py:191
  65.5 9.0 %collective-permute-start.12 = (bf16[2,256,256]{2,1,0:T(8,128)(2,1)S(1)}, bf16[2,256,256]{2,1,0:T(8,128)(2,1)S(1)}, u32[]{:S(2)}, u32[]{:S(2)}) collective-permute-start(bf16[2,256,256]{2,1,0:T(8,128)(2,1)S(1)} %bitcast.34), channel_id=1, source_target_pairs={{0,3},{1,0},{2,1},{3,2},{4,7},{5,4},{6,5},{7,6},{8,11},{9,8},{10,9... | collective-permute-start | bytes 786440 | tf_op jit(solution)/shard_map/ppermute | solution.py:191
  76.9 4.5 %collective-permute-start.13 = (bf16[4,256,256]{2,1,0:T(8,128)(2,1)S(1)}, bf16[4,256,256]{2,1,0:T(8,128)(2,1)S(1)}, u32[]{:S(2)}, u32[]{:S(2)}) collective-permute-start(bf16[4,256,256]{2,1,0:T(8,128)(2,1)S(1)} %get-tuple-element.28), channel_id=1, source_target_pairs={{0,32},{32,0},{64,96},{96,64},{128,160},{160,128},{192,224},{224,1... | collective-permute-start | bytes 1572872 | tf_op jit(solution)/shard_map/ppermute | solution.py:199
  81.6 6.3 %collective-permute-start.14 = (bf16[256,256]{1,0:T(8,128)(2,1)S(1)}, bf16[256,256]{1,0:T(8,128)(2,1)S(1)}, u32[]{:S(2)}, u32[]{:S(2)}) collective-permute-start(bf16[256,256]{1,0:T(8,128)(2,1)S(1)} %get-tuple-element.31), channel_id=1, source_target_pairs={{0,128},{32,160},{64,192},{96,224},{128,0},{160,32},{192,64},{224,... | collective-permute-start | bytes 393224 | tf_op jit(solution)/shard_map/ppermute | solution.py:202
  82.3 9.2 %collective-permute-start.15 = (bf16[256,256]{1,0:T(8,128)(2,1)S(1)}, bf16[256,256]{1,0:T(8,128)(2,1)S(1)}, u32[]{:S(2)}, u32[]{:S(2)}) collective-permute-start(bf16[256,256]{1,0:T(8,128)(2,1)S(1)} %get-tuple-element.33), channel_id=1, source_target_pairs={{0,64},{32,96},{64,128},{96,160},{128,192},{160,224},{192,0},{224,... | collective-permute-start | bytes 393224 | tf_op jit(solution)/shard_map/ppermute | solution.py:202
  85.1 6.3 %collective-permute-start.16 = (bf16[256,256]{1,0:T(8,128)(2,1)S(1)}, bf16[256,256]{1,0:T(8,128)(2,1)S(1)}, u32[]{:S(2)}, u32[]{:S(2)}) collective-permute-start(bf16[256,256]{1,0:T(8,128)(2,1)S(1)} %get-tuple-element.32), channel_id=1, source_target_pairs={{0,192},{32,224},{64,0},{96,32},{128,64},{160,96},{192,128},{224,1... | collective-permute-start | bytes 393224 | tf_op jit(solution)/shard_map/ppermute | solution.py:202
